TPU v7x, 512 devices: a whole 4x4x16 slice. The times are simulated.
512 devices in a mesh: gx: 32 (over x, y, core), gy: 16 (over z).
Axes of the slice: x: 4, y: 4, z: 16, core: 2. Of those that a mesh axis runs over, the one named last changes fastest.
Arguments:
- rhs: float32 [1024, 512, 128], P('gx', 'gy'), may hold values from -8 to 8, as said below
- heights: int32 [1024, 512], P('gx', 'gy'), may hold values from 0 to 63
- index_map: int32 [512], replicated, may hold values from 0 to 511, each once
- coarse_inverse: bfloat16 [512, 512], replicated, may hold values from 0 to 40, as said below
Outputs:
- solution: float32 [1024, 512, 128], P('gx', 'gy')
- residual: float32 [1024, 512, 128], P('gx', 'gy')
Inputs may be any that keep to these rules, and one draw needn't show every extreme that they name: `rhs`: the rough part is at most 8 in size and the remaining part is small and positive. `coarse_inverse`: symmetric and positive definite.
All inputs are finite; a program needn't handle non-finite values.
Results may differ from a plain program's by a relative error of at most 0.0003.
Values sent between devices are 32-bit elements; how exact they have to be, the bound alone decides.
No kernel may reach another device: no remote copies, remote signals or barrier semaphores. Data moves between devices by JAX's collectives and lax.ppermute only.
A program may use at most 64 MiB of HBM per device.

v0:
```python
import jax
import jax.numpy as jnp
from jax import lax
from jax.sharding import PartitionSpec as P

ITERS = 2


def with_halo(cells, sides, width):
    for axis, dim in sides:
        count = lax.axis_size(axis)
        ends = count - 1
        head = lax.slice_in_dim(cells, 0, width, axis=dim)
        tail = lax.slice_in_dim(cells, cells.shape[dim] - width, cells.shape[dim], axis=dim)
        cells = jnp.concatenate(
            [
                lax.ppermute(tail, axis, [(i, (i + 1) % count) for i in range(ends)]),
                cells,
                lax.ppermute(head, axis, [((i + 1) % count, i) for i in range(ends)]),
            ],
            axis=dim,
        )
    return cells


def extend(field):
    return with_halo(field, (("gx", 0), ("gy", 1)), 1)


def sine_table(count):
    order = jnp.arange(count, dtype=jnp.float32) + 1.0
    modes = jnp.sqrt(2.0 / (count + 1.0)) * jnp.sin(
        jnp.pi * order[:, None] * order[None, :] / (count + 1.0)
    )
    values = 2.0 - 2.0 * jnp.cos(jnp.pi * order / (count + 1.0))
    return (modes, values)


def beside_all(array):
    return [
        array[2:, 1:-1, 1:-1],
        array[:-2, 1:-1, 1:-1],
        array[1:-1, 2:, 1:-1],
        array[1:-1, :-2, 1:-1],
        array[1:-1, 1:-1, 2:],
        array[1:-1, 1:-1, :-2],
    ]


def modal(block, sine_x, sine_y, sine_z):
    high = lax.Precision.HIGHEST
    section = jnp.einsum("ia,abk->ibk", sine_x, block, precision=high)
    section = jnp.einsum("jb,ibk->ijk", sine_y, section, precision=high)
    return jnp.einsum("kc,ijc->ijk", sine_z, section, precision=high)


def margin_sum(block):
    core = block[1:-1, 1:-1]
    rows_x = core.shape[0]
    rows_y = core.shape[1]
    depth = core.shape[2]
    face_x = jnp.concatenate(
        [block[0:1, 1:-1], jnp.zeros((rows_x - 2, rows_y, depth), jnp.float32), block[-1:, 1:-1]], 0
    )
    face_y = jnp.concatenate(
        [block[1:-1, 0:1], jnp.zeros((rows_x, rows_y - 2, depth), jnp.float32), block[1:-1, -1:]], 1
    )
    corner = jnp.zeros_like(core)
    corner = corner.at[0, 0].set(block[0, 0]).at[0, -1].set(block[0, -1])
    corner = corner.at[-1, 0].set(block[-1, 0]).at[-1, -1].set(block[-1, -1])
    arrived = with_halo(jnp.stack([face_x, face_y, corner]), (("gx", 1), ("gy", 2)), 1)
    result = core.at[0].add(arrived[0, 0, 1:-1]).at[-1].add(arrived[0, -1, 1:-1])
    result = result.at[:, 0].add(arrived[1, 1:-1, 0]).at[:, -1].add(arrived[1, 1:-1, -1])
    result = result.at[0, 0].add(arrived[2, 0, 0]).at[0, -1].add(arrived[2, 0, -1])
    result = result.at[-1, 0].add(arrived[2, -1, 0]).at[-1, -1].add(arrived[2, -1, -1])
    return result


def body(rhs, heights, index_map, coarse_inverse):
    rows_x, rows_y, depth = rhs.shape
    subdomains = coarse_inverse.shape[0]
    high = lax.Precision.HIGHEST
    levels = jnp.arange(depth, dtype=jnp.int32)
    solid = (levels[None, None, :] < heights[:, :, None]).astype(jnp.float32)
    fluid = 1.0 - solid
    solid_side = extend(solid)
    bottom = jnp.ones((rows_x + 2, rows_y + 2, 1), jnp.float32)
    top = jnp.zeros((rows_x + 2, rows_y + 2, 1), jnp.float32)
    fluid_wide = 1.0 - jnp.concatenate([bottom, solid_side, top], 2)
    count = jnp.zeros_like(fluid)
    for weight in beside_all(fluid_wide):
        count = count + weight
    sine_x, value_x = sine_table(rows_x + 2)
    sine_y, value_y = sine_table(rows_y + 2)
    sine_z, value_z = sine_table(depth)
    inv_eig = 1.0 / (value_x[:, None, None] + value_y[None, :, None] + value_z[None, None, :])
    my_slot = lax.dynamic_index_in_dim(index_map, lax.axis_index(("gx", "gy")), 0, keepdims=False)
    inverse_row = lax.dynamic_index_in_dim(coarse_inverse, my_slot, 0, keepdims=False).astype(
        jnp.float32
    )
    slot_range = jnp.arange(subdomains, dtype=jnp.int32)

    def precondition(resid):
        masked = resid * fluid
        wide = extend(masked)
        spectral = modal(wide, sine_x, sine_y, sine_z) * inv_eig
        local = margin_sum(modal(spectral, sine_x, sine_y, sine_z))
        coarse_res = jnp.sum(masked) / (rows_x * rows_y * depth)
        every = lax.all_gather(coarse_res.reshape(1), ("gx", "gy"), axis=0, tiled=True)
        one_hot = (index_map[None, :] == slot_range[:, None]).astype(jnp.float32)
        coarse_vec = jnp.dot(one_hot, every, precision=high)
        coarse_value = jnp.dot(inverse_row, coarse_vec, precision=high)
        return fluid * (local + coarse_value)

    def energy_sum(resid, precond):
        return lax.psum(jnp.sum(resid * precond), ("gx", "gy"))

    source = fluid * rhs
    solution = jnp.zeros_like(source)
    residual = source
    precond = precondition(residual)
    direction = precond
    energy_now = energy_sum(residual, precond)
    for iteration in range(ITERS):
        operate_wide = extend(direction)
        padded_field = jnp.pad(operate_wide, ((0, 0), (0, 0), (1, 1)))
        beside = jnp.zeros_like(direction)
        for operate_weight, value in zip(beside_all(fluid_wide), beside_all(padded_field)):
            beside = beside + operate_weight * value
        image = fluid * (count * direction - beside) + solid * direction
        step_size = energy_now / lax.psum(jnp.sum(direction * image), ("gx", "gy"))
        solution = solution + step_size * direction
        residual = residual - step_size * image
        if iteration + 1 < ITERS:
            precond = precondition(residual)
            energy_next = energy_sum(residual, precond)
            direction = precond + energy_next / energy_now * direction
            energy_now = energy_next
    return (solution, residual)


def solution(mesh):
    in_specs = (P("gx", "gy", None), P("gx", "gy"), P(), P())
    out_specs = (P("gx", "gy", None), P("gx", "gy", None))
    return jax.shard_map(body, mesh=mesh, in_specs=in_specs, out_specs=out_specs, check_vma=False)
```

profile of v0, /device:TPU:1, one launch (start us, length us, event | category | flops | bytes accessed | tf_op | source)
XLA Modules:
  0.0 701.1 jit_solution(3966021483471346099)
XLA Ops:
  1.5 2.0 fusion.167
  3.6 4.6 collective-permute-start
  8.1 5.5 collective-permute-start.1
  13.8 1.9 collective-permute-start.8
  15.8 2.4 collective-permute-start.9
  19.8 109.8 %all-reduce.4 = f32[512]{0:T(512)S(1)} all-reduce(f32[512]{0:T(512)S(1)} %dynamic-update-slice.78), channel_id=1, replica_groups=mesh['gx'=32,'gy'=16] {'gx','gy'}, use_global_device_ids=true, to_apply=%add.4 | all-reduce | flops 512 | bytes 4096
  130.9 2.6 collective-permute-start.2
  133.6 1.3 collective-permute-start.3
  143.7 1.8 slice_bitcast_fusion.15
  147.2 2.9 collective-permute-start.4
  150.1 2.9 collective-permute-start.5
  155.5 2.6 collective-permute-start.6
  159.1 1.3 collective-permute-start.7
  160.4 3.9 collective-permute-done.7
  164.4 1.8 broadcast_select_fusion
  168.5 2.2 collective-permute-start.12
  170.7 3.3 collective-permute-start.13
  174.1 2.9 collective-permute-start.10
  177.0 1.3 collective-permute-start.11
  178.3 1.3 collective-permute-start.14
  179.6 5.1 collective-permute-start.15
  186.4 3.5 multiply_reduce_fusion.2
  189.9 109.8 %all-reduce.6 = (f32[]{:T(128)}, f32[]{:T(128)}) all-reduce(f32[]{:T(128)} %get-tuple-element.297, f32[]{:T(128)} %get-tuple-element.296), channel_id=1, replica_groups=mesh['gx'=32,'gy'=16] {'gx','gy'}, use_global_device_ids=true, to_apply=%region_3.4 | all-reduce | flops 2 | bytes 16 | tf_op jit(solution)/shard_map/psum | solution.py:116
  301.0 2.1 fusion.165
  303.9 2.1 collective-permute-start.16
  306.0 2.2 collective-permute-start.17
  309.1 103.2 %all-reduce.5 = f32[512]{0:T(512)S(1)} all-reduce(f32[512]{0:T(512)S(1)} %dynamic-update-slice.79), channel_id=1, replica_groups=mesh['gx'=32,'gy'=16] {'gx','gy'}, use_global_device_ids=true, to_apply=%add.5 | all-reduce | flops 512 | bytes 4096
  413.0 1.9 collective-permute-start.18
  415.0 1.3 collective-permute-start.19
  417.4 2.1 collective-permute-done.19
  419.5 1.9 fusion.13
  426.9 2.4 slice_bitcast_fusion.9
  429.4 1.9 scatter.35
  433.7 2.9 collective-permute-start.20
  436.6 3.1 collective-permute-start.21
  442.7 2.7 collective-permute-start.22
  446.9 1.3 collective-permute-start.23
  450.1 2.9 collective-permute-done.23
  453.6 1.6 scatter-add.71
  457.2 2.5 broadcast_select_fusion.2
  459.7 2.5 scatter-add.75
  466.2 1.7 broadcast_add_fusion
  468.9 105.5 %psum.30 = f32[]{:T(128)} all-reduce(f32[]{:T(128)} %multiply_reduce_fusion.1), channel_id=1, replica_groups=mesh['gx'=32,'gy'=16] {'gx','gy'}, use_global_device_ids=true, to_apply=%region_8.9 | all-reduce | flops 1 | bytes 8 | tf_op jit(solution)/shard_map/psum | solution.py:116
  576.8 2.6 collective-permute-start.24
  579.4 3.0 collective-permute-start.25
  584.5 4.0 collective-permute-start.27
  590.0 2.4 multiply_reduce_fusion
  592.4 104.2 %psum.31 = f32[]{:T(128)} all-reduce(f32[]{:T(128)} %get-tuple-element.300), channel_id=1, replica_groups=mesh['gx'=32,'gy'=16] {'gx','gy'}, use_global_device_ids=true, to_apply=%region_10.11 | all-reduce | flops 1 | bytes 8 | tf_op jit(solution)/shard_map/psum | solution.py:131
  (169 shorter events, 51.3 us)
Async XLA Ops:
  0.6 136.9 %copy-start = (bf16[512,512]{1,0:T(8,128)(2,1)S(1)}, bf16[512,512]{1,0:T(8,128)(2,1)}, u32[]{:S(2)}) copy-start(bf16[512,512]{1,0:T(8,128)(2,1)} %param.55) | copy-start | bytes 1572868
  0.6 129.0 %copy-start.13 = (s32[3]{0:T(128)S(1)}, s32[3]{0:T(128)}, u32[]{:S(2)}) copy-start(s32[3]{0:T(128)} %constant.617.clone.1) | copy-start | bytes 40
  0.7 129.7 %copy-start.14 = (s32[512]{0:T(512)S(1)}, s32[512]{0:T(512)}, u32[]{:S(2)}) copy-start(s32[512]{0:T(512)} %param.54) | copy-start | bytes 6148
  3.6 127.3 %collective-permute-start = (f32[1,32,128]{2,0,1:T(1,128)S(1)}, f32[1,32,128]{2,0,1:T(1,128)S(1)}, u32[]{:S(2)}, u32[]{:S(2)}) collective-permute-start(f32[1,32,128]{2,0,1:T(1,128)S(1)} %get-tuple-element.348), channel_id=1, source_target_pairs={{0,16},{16,32},{32,48},{48,64},{64,80},{80,96},{96,112},{112,128},... | collective-permute-start | bytes 49160 | tf_op jit(solution)/shard_map/ppermute | solution.py:17
  8.1 122.8 %collective-permute-start.1 = (f32[1,32,128]{2,0,1:T(1,128)S(1)}, f32[1,32,128]{2,0,1:T(1,128)S(1)}, u32[]{:S(2)}, u32[]{:S(2)}) collective-permute-start(f32[1,32,128]{2,0,1:T(1,128)S(1)} %get-tuple-element.349), channel_id=1, source_target_pairs={{16,0},{32,16},{48,32},{64,48},{80,64},{96,80},{112,96},{128,112},... | collective-permute-start | bytes 49160 | tf_op jit(solution)/shard_map/ppermute | solution.py:19
  13.8 160.2 %collective-permute-start.8 = (f32[1,32,128]{2,0,1:T(1,128)S(1)}, f32[1,32,128]{2,0,1:T(1,128)S(1)}, u32[]{:S(2)}, u32[]{:S(2)}) collective-permute-start(f32[1,32,128]{2,0,1:T(1,128)S(1)} %get-tuple-element.344), channel_id=1, source_target_pairs={{0,16},{16,32},{32,48},{48,64},{64,80},{80,96},{96,112},{112,128},... | collective-permute-start | bytes 49160 | tf_op jit(solution)/shard_map/ppermute | solution.py:17
  15.8 158.3 %collective-permute-start.9 = (f32[1,32,128]{2,0,1:T(1,128)S(1)}, f32[1,32,128]{2,0,1:T(1,128)S(1)}, u32[]{:S(2)}, u32[]{:S(2)}) collective-permute-start(f32[1,32,128]{2,0,1:T(1,128)S(1)} %get-tuple-element.345), channel_id=1, source_target_pairs={{16,0},{32,16},{48,32},{64,48},{80,64},{96,80},{112,96},{128,112},... | collective-permute-start | bytes 49160 | tf_op jit(solution)/shard_map/ppermute | solution.py:19
  130.9 6.6 collective-permute-start.2
  133.6 4.5 collective-permute-start.3
  136.9 10.0 %copy-start.10 = (f32[32]{0:T(128)}, f32[32]{0:T(128)S(1)}, u32[]{:S(2)}) copy-start(f32[32]{0:T(128)S(1)} %pad.157.clone) | copy-start | bytes 388
  137.6 15.4 %copy-start.8 = (bf16[512]{0:T(512)(128)(2,1)}, bf16[512]{0:T(512)(128)(2,1)S(1)}, u32[]{:S(2)}) copy-start(bf16[512]{0:T(512)(128)(2,1)S(1)} %dynamic-slice_reduce_fusion) | copy-start | bytes 3076
  143.6 11.0 %copy-start.4 = (f32[34,34,128]{2,1,0:T(8,128)}, f32[34,34,128]{2,1,0:T(8,128)S(1)}, u32[]{:S(2)}) copy-start(f32[34,34,128]{2,1,0:T(8,128)S(1)} %fusion.61) | copy-start | bytes 1775620
  147.2 7.8 %collective-permute-start.4 = (f32[3,1,32,128]{3,2,1,0:T(8,128)S(1)}, f32[3,1,32,128]{3,2,1,0:T(8,128)S(1)}, u32[]{:S(2)}, u32[]{:S(2)}) collective-permute-start(f32[3,1,32,128]{3,2,1,0:T(8,128)S(1)} %get-tuple-element.315), channel_id=1, source_target_pairs={{0,16},{16,32},{32,48},{48,64},{64,80},{80,96},{96,112},{112,128},... | collective-permute-start | bytes 147464 | tf_op jit(solution)/shard_map/ppermute | solution.py:17
  150.1 5.4 collective-permute-start.5
  155.5 4.9 collective-permute-start.6
  159.1 5.2 collective-permute-start.7
  168.5 9.8 %collective-permute-start.12 = (f32[1,32,128]{2,0,1:T(1,128)S(1)}, f32[1,32,128]{2,0,1:T(1,128)S(1)}, u32[]{:S(2)}, u32[]{:S(2)}) collective-permute-start(f32[1,32,128]{2,0,1:T(1,128)S(1)} %get-tuple-element.347), channel_id=1, source_target_pairs={{16,0},{32,16},{48,32},{64,48},{80,64},{96,80},{112,96},{128,112},... | collective-permute-start | bytes 49160 | tf_op jit(solution)/shard_map/ppermute | solution.py:19
  170.7 7.6 %collective-permute-start.13 = (f32[1,32,128]{2,0,1:T(1,128)S(1)}, f32[1,32,128]{2,0,1:T(1,128)S(1)}, u32[]{:S(2)}, u32[]{:S(2)}) collective-permute-start(f32[1,32,128]{2,0,1:T(1,128)S(1)} %get-tuple-element.346), channel_id=1, source_target_pairs={{0,16},{16,32},{32,48},{48,64},{64,80},{80,96},{96,112},{112,128},... | collective-permute-start | bytes 49160 | tf_op jit(solution)/shard_map/ppermute | solution.py:17
  174.1 10.6 %collective-permute-start.10 = (f32[34,1,128]{2,0,1:T(8,128)S(1)}, f32[34,1,128]{2,0,1:T(8,128)S(1)}, u32[]{:S(2)}, u32[]{:S(2)}) collective-permute-start(f32[34,1,128]{2,0,1:T(8,128)S(1)} %get-tuple-element.334), channel_id=1, source_target_pairs={{0,1},{1,2},{2,3},{3,4},{4,5},{5,6},{6,7},{7,8},{8,9},{9,10},{10,1... | collective-permute-start | bytes 52232 | tf_op jit(solution)/shard_map/ppermute | solution.py:17
  177.0 7.7 %collective-permute-start.11 = (f32[34,1,128]{2,0,1:T(8,128)S(1)}, f32[34,1,128]{2,0,1:T(8,128)S(1)}, u32[]{:S(2)}, u32[]{:S(2)}) collective-permute-start(f32[34,1,128]{2,0,1:T(8,128)S(1)} %get-tuple-element.335), channel_id=1, source_target_pairs={{1,0},{2,1},{3,2},{4,3},{5,4},{6,5},{7,6},{8,7},{9,8},{10,9},{11,1... | collective-permute-start | bytes 52232 | tf_op jit(solution)/shard_map/ppermute | solution.py:19
  178.3 7.0 collective-permute-start.14
  179.6 5.8 collective-permute-start.15
  185.3 1.0 copy-start.1
  303.1 0.8 copy-start.7
  303.1 164.8 %copy-start.2 = (f32[32,32,128]{2,0,1:T(8,128)}, f32[32,32,128]{2,0,1:T(8,128)S(1)}, u32[]{:S(2)}) copy-start(f32[32,32,128]{2,0,1:T(8,128)S(1)} %get-tuple-element.304) | copy-start | bytes 1572868
  303.9 108.3 %collective-permute-start.16 = (f32[1,32,128]{2,0,1:T(1,128)S(1)}, f32[1,32,128]{2,0,1:T(1,128)S(1)}, u32[]{:S(2)}, u32[]{:S(2)}) collective-permute-start(f32[1,32,128]{2,0,1:T(1,128)S(1)} %get-tuple-element.342), channel_id=1, source_target_pairs={{0,16},{16,32},{32,48},{48,64},{64,80},{80,96},{96,112},{112,128},... | collective-permute-start | bytes 49160 | tf_op jit(solution)/shard_map/ppermute | solution.py:17
  306.0 106.3 %collective-permute-start.17 = (f32[1,32,128]{2,0,1:T(1,128)S(1)}, f32[1,32,128]{2,0,1:T(1,128)S(1)}, u32[]{:S(2)}, u32[]{:S(2)}) collective-permute-start(f32[1,32,128]{2,0,1:T(1,128)S(1)} %get-tuple-element.343), channel_id=1, source_target_pairs={{16,0},{32,16},{48,32},{64,48},{80,64},{96,80},{112,96},{128,112},... | collective-permute-start | bytes 49160 | tf_op jit(solution)/shard_map/ppermute | solution.py:19
  413.0 4.4 collective-permute-start.18
  415.0 4.5 collective-permute-start.19
  426.1 0.9 copy-start.5
  433.5 6.2 copy-start.9
  433.5 6.2 copy-start.12
  433.7 8.2 %collective-permute-start.20 = (f32[3,1,32,128]{3,2,1,0:T(8,128)S(1)}, f32[3,1,32,128]{3,2,1,0:T(8,128)S(1)}, u32[]{:S(2)}, u32[]{:S(2)}) collective-permute-start(f32[3,1,32,128]{3,2,1,0:T(8,128)S(1)} %get-tuple-element.313), channel_id=1, source_target_pairs={{0,16},{16,32},{32,48},{48,64},{64,80},{80,96},{96,112},{112,128},... | collective-permute-start | bytes 147464 | tf_op jit(solution)/shard_map/ppermute | solution.py:17
  436.6 5.4 collective-permute-start.21
  440.4 1.1 copy-start.6
  442.7 5.5 collective-permute-start.22
  446.9 6.1 collective-permute-start.23
  453.0 0.6 copy-start.11
  576.8 5.6 collective-permute-start.24
  579.4 3.9 collective-permute-start.25
  583.2 5.3 collective-permute-start.26
  584.5 4.9 collective-permute-start.27
  592.4 106.4 %copy-start.3 = (f32[32,32,128]{2,0,1:T(8,128)S(1)}, f32[32,32,128]{2,0,1:T(8,128)}, u32[]{:S(2)}) copy-start(f32[32,32,128]{2,0,1:T(8,128)} %copy-done.2) | copy-start | bytes 1572868
where the time goes:
time: 704 us; the launch traced here: 701 us
  blocking collectives  532 us (76%)
  starting transfers between devices  72.5 us (10%)
  other arithmetic  35.1 us (5%)
  local copies, waits for them, and re-layouts  26.5 us (4%)
  matrix products  13.6 us (2%)
  waiting for transfers between devices  12 us (2%)
  between operations  9.05 us (1%)
    psum x2, blocking collectives, energy_sum(): return lax.psum(jnp.sum(resid * precond), ('gx', 'gy'))  215 us
    unnamed x2, blocking collectives  213 us
    psum x1, blocking collectives, body(): step_size = energy_now / lax.psum(jnp.sum(direction * image), ('gx', 'gy'))  104 us
    ppermute x14, starting transfers between devices, with_halo(): lax.ppermute(tail, axis, [(i, (i + 1) % count) for i in range(ends)])  42.6 us
    ppermute x14, starting transfers between devices, with_halo(): lax.ppermute(head, axis, [((i + 1) % count, i) for i in range(ends)])  29.9 us
  transfers between devices with their start and end apart: 28, of which 9 were waited for; matrix products, arithmetic and copies ran while one was open for 4% of the time, Pallas kernels for 0%

commit v1 on v0

--- a/solution.py
+++ b/solution.py
@@ -21,6 +21,24 @@
             axis=dim,
         )
     return cells
+
+
+def exchange(gathered, summed):
+    parts = []
+    k1 = gathered.shape[0]
+    stage = jnp.concatenate([gathered, summed])
+    for axis in ("gy", "gx"):
+        count = lax.axis_size(axis)
+        got = lax.all_to_all(jnp.broadcast_to(stage[None], (count,) + stage.shape), axis, 0, 0, tiled=False)
+        width = got.shape[1] - summed.shape[0]
+        summed = jnp.sum(got[:, width:], axis=0)
+        gathered = got[:, :width].reshape(-1)
+        stage = jnp.concatenate([gathered, summed])
+    return gathered, summed
+
+
+def total(value):
+    return exchange(jnp.zeros((0,), jnp.float32), value.reshape(1))[1][0]
 
 
 def extend(field):
@@ -98,7 +116,7 @@
     inverse_row = lax.dynamic_index_in_dim(coarse_inverse, my_slot, 0, keepdims=False).astype(
         jnp.float32
     )
-    slot_range = jnp.arange(subdomains, dtype=jnp.int32)
+    picked_row = inverse_row[index_map]
 
     def precondition(resid):
         masked = resid * fluid
@@ -106,14 +124,12 @@
         spectral = modal(wide, sine_x, sine_y, sine_z) * inv_eig
         local = margin_sum(modal(spectral, sine_x, sine_y, sine_z))
         coarse_res = jnp.sum(masked) / (rows_x * rows_y * depth)
-        every = lax.all_gather(coarse_res.reshape(1), ("gx", "gy"), axis=0, tiled=True)
-        one_hot = (index_map[None, :] == slot_range[:, None]).astype(jnp.float32)
-        coarse_vec = jnp.dot(one_hot, every, precision=high)
-        coarse_value = jnp.dot(inverse_row, coarse_vec, precision=high)
+        every = exchange(coarse_res.reshape(1), jnp.zeros((0,), jnp.float32))[0]
+        coarse_value = jnp.sum(picked_row * every)
         return fluid * (local + coarse_value)
 
     def energy_sum(resid, precond):
-        return lax.psum(jnp.sum(resid * precond), ("gx", "gy"))
+        return total(jnp.sum(resid * precond))
 
     source = fluid * rhs
     solution = jnp.zeros_like(source)
@@ -128,7 +144,7 @@
         for operate_weight, value in zip(beside_all(fluid_wide), beside_all(padded_field)):
             beside = beside + operate_weight * value
         image = fluid * (count * direction - beside) + solid * direction
-        step_size = energy_now / lax.psum(jnp.sum(direction * image), ("gx", "gy"))
+        step_size = energy_now / total(jnp.sum(direction * image))
         solution = solution + step_size * direction
         residual = residual - step_size * image
         if iteration + 1 < ITERS:

time: 704 us -> 372 us (0.53)
  blocking collectives: 532 us -> 108 us
  starting transfers between devices: 72.5 us -> 126 us
  waiting for transfers between devices: 12 us -> 37.5 us
  local copies, waits for them, and re-layouts: 26.5 us -> 39.9 us
    psum x3 -> x0, blocking collectives: 319 us -> none  [the longest x2 215 us: energy_sum(): return lax.psum(jnp.sum(resid * precond), ('gx', 'gy'))]
    unnamed x2 -> x0, blocking collectives: 213 us -> none
    all_to_all x0 -> x6, blocking collectives: none -> 108 us  [exchange(): lax.all_to_all(jnp.broadcast_to(stage[None], (count,) + stage.shape), axi...]
    all_to_all x0 -> x6, starting transfers between devices: none -> 48 us  [exchange(): lax.all_to_all(jnp.broadcast_to(stage[None], (count,) + stage.shape), axi...]
    all_to_all x0 -> x6, waiting for transfers between devices: none -> 23.1 us  [exchange(): lax.all_to_all(jnp.broadcast_to(stage[None], (count,) + stage.shape), axi...]
    broadcast_in_dim x0 -> x12, local copies, waits for them, and re-layouts: none -> 8.87 us  [exchange(): jnp.broadcast_to(stage[None], (count,) + stage.shape)]
    ppermute x14, starting transfers between devices: 42.6 us -> 51 us  [with_halo(): lax.ppermute(tail, axis, [(i, (i + 1) % count) for i in range(ends)])]
  transfers between devices with their start and end apart: 28 -> 34, of which waited for: 9 -> 11; matrix products, arithmetic and copies ran while one was open for 4% -> 12% of each run, Pallas kernels for 0% -> 0%
where the time goes in v1:
time: 372 us; the launch traced here: 369 us
  starting transfers between devices  126 us (34%)
  blocking collectives  108 us (29%)
  local copies, waits for them, and re-layouts  39.9 us (11%)
  other arithmetic  37.8 us (10%)
  waiting for transfers between devices  37.5 us (10%)
  matrix products  10.9 us (3%)
  between operations  9.15 us (2%)
    all_to_all x6, blocking collectives, exchange(): lax.all_to_all(jnp.broadcast_to(stage[None], (count,) + stage.shape), axi...  108 us
    ppermute x14, starting transfers between devices, with_halo(): lax.ppermute(tail, axis, [(i, (i + 1) % count) for i in range(ends)])  51 us
    all_to_all x6, starting transfers between devices, exchange(): lax.all_to_all(jnp.broadcast_to(stage[None], (count,) + stage.shape), axi...  48 us
    ppermute x14, starting transfers between devices, with_halo(): lax.ppermute(head, axis, [((i + 1) % count, i) for i in range(ends)])  26.9 us
    all_to_all x6, waiting for transfers between devices, exchange(): lax.all_to_all(jnp.broadcast_to(stage[None], (count,) + stage.shape), axi...  23.1 us
    ppermute x14, waiting for transfers between devices, with_halo(): lax.ppermute(head, axis, [((i + 1) % count, i) for i in range(ends)])  12.5 us
    broadcast_in_dim x12, local copies, waits for them, and re-layouts, exchange(): jnp.broadcast_to(stage[None], (count,) + stage.shape)  8.87 us
  transfers between devices with their start and end apart: 34, of which 11 were waited for; matrix products, arithmetic and copies ran while one was open for 12% of the time, Pallas kernels for 0%

profile of v1, /device:TPU:1, one launch (start us, length us, event | category | flops | bytes accessed | tf_op | source)
XLA Modules:
  0.0 369.4 jit_solution(12159284014645674606)
XLA Ops:
  1.5 2.0 fusion.161
  3.5 4.6 %collective-permute-start = (f32[1,32,128]{2,0,1:T(1,128)S(1)}, f32[1,32,128]{2,0,1:T(1,128)S(1)}, u32[]{:S(2)}, u32[]{:S(2)}) collective-permute-start(f32[1,32,128]{2,0,1:T(1,128)S(1)} %get-tuple-element.352), channel_id=1, source_target_pairs={{0,16},{16,32},{32,48},{48,64},{64,80},{80,96},{96,112},{112,128},... | collective-permute-start | bytes 49160 | tf_op jit(solution)/shard_map/ppermute | solution.py:17
  8.1 5.5 %collective-permute-start.1 = (f32[1,32,128]{2,0,1:T(1,128)S(1)}, f32[1,32,128]{2,0,1:T(1,128)S(1)}, u32[]{:S(2)}, u32[]{:S(2)}) collective-permute-start(f32[1,32,128]{2,0,1:T(1,128)S(1)} %get-tuple-element.353), channel_id=1, source_target_pairs={{16,0},{32,16},{48,32},{64,48},{80,64},{96,80},{112,96},{128,112},... | collective-permute-start | bytes 49160 | tf_op jit(solution)/shard_map/ppermute | solution.py:19
  14.8 11.4 %all-to-all-start = ((f32[16,1,1]{2,1,0:T(1,128)}), f32[16,1,1]{2,1,0:T(1,128)S(1)}, u32[]{:S(2)}, u32[]{:S(2)}) async-start(f32[16,1,1]{2,1,0:T(1,128)} %broadcast_in_dim.35), calls=%async_computation | async-start | bytes 16384 | tf_op jit(solution)/shard_map/all_to_all | solution.py:32
  27.0 3.9 %collective-permute-start.8 = (f32[1,32,128]{2,0,1:T(1,128)}, f32[1,32,128]{2,0,1:T(1,128)S(1)}, u32[]{:S(2)}, u32[]{:S(2)}) collective-permute-start(f32[1,32,128]{2,0,1:T(1,128)} %get-tuple-element.348), channel_id=1, source_target_pairs={{0,16},{16,32},{32,48},{48,64},{64,80},{80,96},{96,112},{112,128},... | collective-permute-start | bytes 49160 | tf_op jit(solution)/shard_map/ppermute | solution.py:17
  30.9 1.9 collective-permute-start.9
  37.8 3.5 collective-permute-start.2
  42.7 3.5 gather_fusion
  47.8 9.5 %all-to-all-start.1 = ((f32[32,1,16]{2,1,0:T(1,128)}), f32[32,1,16]{2,1,0:T(1,128)S(1)}, u32[]{:S(2)}, u32[]{:S(2)}) async-start(f32[32,1,16]{2,1,0:T(1,128)} %broadcast_in_dim.37), calls=%async_computation.1 | async-start | bytes 32768 | tf_op jit(solution)/shard_map/all_to_all | solution.py:32
  63.0 1.9 slice_bitcast_fusion.15
  68.7 3.5 collective-permute-start.4
  72.3 1.9 collective-permute-start.5
  77.9 4.3 %collective-permute-start.6 = (f32[3,34,1,128]{3,1,2,0:T(8,128)S(1)}, f32[3,34,1,128]{3,1,2,0:T(8,128)S(1)}, u32[]{:S(2)}, u32[]{:S(2)}) collective-permute-start(f32[3,34,1,128]{3,1,2,0:T(8,128)S(1)} %get-tuple-element.315), channel_id=1, source_target_pairs={{0,1},{1,2},{2,3},{3,4},{4,5},{5,6},{6,7},{7,8},{8,9},{9,10},{10,1... | collective-permute-start | bytes 156680 | tf_op jit(solution)/shard_map/ppermute | solution.py:17
  83.8 3.6 collective-permute-done.7
  87.5 1.8 broadcast_select_fusion
  91.5 1.9 collective-permute-start.12
  93.4 3.8 %collective-permute-start.13 = (f32[1,32,128]{2,0,1:T(1,128)S(1)}, f32[1,32,128]{2,0,1:T(1,128)S(1)}, u32[]{:S(2)}, u32[]{:S(2)}) collective-permute-start(f32[1,32,128]{2,0,1:T(1,128)S(1)} %get-tuple-element.350), channel_id=1, source_target_pairs={{0,16},{16,32},{32,48},{48,64},{64,80},{80,96},{96,112},{112,128},... | collective-permute-start | bytes 49160 | tf_op jit(solution)/shard_map/ppermute | solution.py:17
  97.3 3.3 collective-permute-start.10
  103.2 6.3 %collective-permute-start.15 = (f32[34,1,128]{2,0,1:T(8,128)S(1)}, f32[34,1,128]{2,0,1:T(8,128)S(1)}, u32[]{:S(2)}, u32[]{:S(2)}) collective-permute-start(f32[34,1,128]{2,0,1:T(8,128)S(1)} %get-tuple-element.340), channel_id=1, source_target_pairs={{0,1},{1,2},{2,3},{3,4},{4,5},{5,6},{6,7},{7,8},{8,9},{9,10},{10,1... | collective-permute-start | bytes 52232 | tf_op jit(solution)/shard_map/ppermute | solution.py:17
  111.2 2.7 multiply_reduce_fusion.2
  114.6 26.3 %all_to_all.72 = f32[16,1,1]{2,1,0:T(1,128)S(1)} all-to-all(f32[16,1,1]{2,1,0:T(1,128)S(1)} %broadcast_in_dim.38), channel_id=1, replica_groups=mesh['gx'=32,'gy'=16] {'gy'}, dimensions={0} | all-to-all | bytes 128 | tf_op jit(solution)/shard_map/all_to_all | solution.py:32
  142.1 3.5 all-to-all-start.4
  146.2 10.5 %all-to-all-done.4 = f32[16,1,1]{2,1,0:T(1,128)S(1)} async-done(((f32[16,1,1]{2,1,0:T(1,128)}), f32[16,1,1]{2,1,0:T(1,128)S(1)}, u32[]{:S(2)}, u32[]{:S(2)}) %all-to-all-start.4) | async-done | bytes 96 | tf_op jit(solution)/shard_map/all_to_all | solution.py:32
  158.0 11.7 %all-to-all-start.3 = ((f32[32,1,1]{2,1,0:T(1,128)}), f32[32,1,1]{2,1,0:T(1,128)S(1)}, u32[]{:S(2)}, u32[]{:S(2)}) async-start(f32[32,1,1]{2,1,0:T(1,128)} %broadcast_in_dim.39), calls=%async_computation.3 | async-start | bytes 32768 | tf_op jit(solution)/shard_map/all_to_all | solution.py:32
  170.3 6.3 %all-to-all-done.3 = f32[32,1,1]{2,1,0:T(1,128)S(1)} async-done(((f32[32,1,1]{2,1,0:T(1,128)}), f32[32,1,1]{2,1,0:T(1,128)S(1)}, u32[]{:S(2)}, u32[]{:S(2)}) %all-to-all-start.3) | async-done | bytes 160 | tf_op jit(solution)/shard_map/all_to_all | solution.py:32
  177.9 4.1 %all-to-all-start.5 = ((f32[32,1,1]{2,1,0:T(1,128)}), f32[32,1,1]{2,1,0:T(1,128)S(1)}, u32[]{:S(2)}, u32[]{:S(2)}) async-start(f32[32,1,1]{2,1,0:T(1,128)} %broadcast_in_dim.43), calls=%async_computation.5 | async-start | bytes 32768 | tf_op jit(solution)/shard_map/all_to_all | solution.py:32
  182.7 6.3 %all-to-all-done.5 = f32[32,1,1]{2,1,0:T(1,128)S(1)} async-done(((f32[32,1,1]{2,1,0:T(1,128)}), f32[32,1,1]{2,1,0:T(1,128)S(1)}, u32[]{:S(2)}, u32[]{:S(2)}) %all-to-all-start.5) | async-done | bytes 160 | tf_op jit(solution)/shard_map/all_to_all | solution.py:32
  192.8 2.7 collective-permute-start.16
  195.6 1.9 collective-permute-start.17
  197.5 3.1 collective-permute-done.17
  200.7 2.1 collective-permute-start.18
  204.8 15.9 %all_to_all.73 = f32[16,1,1]{2,1,0:T(1,128)S(1)} all-to-all(f32[16,1,1]{2,1,0:T(1,128)S(1)} %broadcast_in_dim.44), channel_id=1, replica_groups=mesh['gx'=32,'gy'=16] {'gy'}, dimensions={0} | all-to-all | bytes 128 | tf_op jit(solution)/shard_map/all_to_all | solution.py:32
  221.5 7.8 %all-to-all-start.7 = ((f32[32,1,16]{2,1,0:T(1,128)}), f32[32,1,16]{2,1,0:T(1,128)S(1)}, u32[]{:S(2)}, u32[]{:S(2)}) async-start(f32[32,1,16]{2,1,0:T(1,128)} %broadcast_in_dim.46), calls=%async_computation.7 | async-start | bytes 32768 | tf_op jit(solution)/shard_map/all_to_all | solution.py:32
  235.8 1.8 slice_bitcast_fusion.9
  241.6 3.5 collective-permute-start.20
  245.1 2.1 collective-permute-start.21
  251.6 2.4 collective-permute-start.22
  258.1 2.5 collective-permute-done.23
  264.2 2.5 broadcast_select_fusion.2
  266.7 2.5 scatter-add.75
  276.6 16.1 %all_to_all.74 = f32[16,1,1]{2,1,0:T(1,128)S(1)} all-to-all(f32[16,1,1]{2,1,0:T(1,128)S(1)} %broadcast_in_dim.47), channel_id=1, replica_groups=mesh['gx'=32,'gy'=16] {'gy'}, dimensions={0} | all-to-all | bytes 128 | tf_op jit(solution)/shard_map/all_to_all | solution.py:32
  294.0 16.1 %all_to_all.75 = f32[32,1,1]{2,1,0:T(1,128)S(1)} all-to-all(f32[32,1,1]{2,1,0:T(1,128)S(1)} %broadcast_in_dim.48), channel_id=1, replica_groups=mesh['gx'=32,'gy'=16] {'gx'}, dimensions={0} | all-to-all | bytes 256 | tf_op jit(solution)/shard_map/all_to_all | solution.py:32
  313.0 2.6 collective-permute-start.24
  315.6 3.0 collective-permute-start.25
  320.8 4.0 %collective-permute-start.27 = (f32[34,1,128]{2,0,1:T(8,128)S(1)}, f32[34,1,128]{2,0,1:T(8,128)S(1)}, u32[]{:S(2)}, u32[]{:S(2)}) collective-permute-start(f32[34,1,128]{2,0,1:T(8,128)S(1)} %get-tuple-element.334), channel_id=1, source_target_pairs={{0,1},{1,2},{2,3},{3,4},{4,5},{5,6},{6,7},{7,8},{8,9},{9,10},{10,1... | collective-permute-start | bytes 52232 | tf_op jit(solution)/shard_map/ppermute | solution.py:17
  326.2 2.3 multiply_reduce_fusion
  329.2 17.1 %all_to_all.76 = f32[16,1,1]{2,1,0:T(1,128)S(1)} all-to-all(f32[16,1,1]{2,1,0:T(1,128)S(1)} %broadcast_in_dim.49), channel_id=1, replica_groups=mesh['gx'=32,'gy'=16] {'gy'}, dimensions={0} | all-to-all | bytes 128 | tf_op jit(solution)/shard_map/all_to_all | solution.py:32
  347.7 16.7 %all_to_all.77 = f32[32,1,1]{2,1,0:T(1,128)S(1)} all-to-all(f32[32,1,1]{2,1,0:T(1,128)S(1)} %broadcast_in_dim.50), channel_id=1, replica_groups=mesh['gx'=32,'gy'=16] {'gx'}, dimensions={0} | all-to-all | bytes 256 | tf_op jit(solution)/shard_map/all_to_all | solution.py:32
  (208 shorter events, 81.5 us)
Async XLA Ops:
  0.6 35.0 %copy-start.15 = (s32[3]{0:T(128)S(1)}, s32[3]{0:T(128)}, u32[]{:S(2)}) copy-start(s32[3]{0:T(128)} %constant.619.clone.1) | copy-start | bytes 40
  0.6 32.4 %copy-start.14 = (s32[512]{0:T(512)S(1)}, s32[512]{0:T(512)}, u32[]{:S(2)}) copy-start(s32[512]{0:T(512)} %param.54) | copy-start | bytes 6148
  3.5 34.3 %collective-permute-start = (f32[1,32,128]{2,0,1:T(1,128)S(1)}, f32[1,32,128]{2,0,1:T(1,128)S(1)}, u32[]{:S(2)}, u32[]{:S(2)}) collective-permute-start(f32[1,32,128]{2,0,1:T(1,128)S(1)} %get-tuple-element.352), channel_id=1, source_target_pairs={{0,16},{16,32},{32,48},{48,64},{64,80},{80,96},{96,112},{112,128},... | collective-permute-start | bytes 49160 | tf_op jit(solution)/shard_map/ppermute | solution.py:17
  8.1 29.7 %collective-permute-start.1 = (f32[1,32,128]{2,0,1:T(1,128)S(1)}, f32[1,32,128]{2,0,1:T(1,128)S(1)}, u32[]{:S(2)}, u32[]{:S(2)}) collective-permute-start(f32[1,32,128]{2,0,1:T(1,128)S(1)} %get-tuple-element.353), channel_id=1, source_target_pairs={{16,0},{32,16},{48,32},{64,48},{80,64},{96,80},{112,96},{128,112},... | collective-permute-start | bytes 49160 | tf_op jit(solution)/shard_map/ppermute | solution.py:19
  14.8 32.1 %all-to-all-start = ((f32[16,1,1]{2,1,0:T(1,128)}), f32[16,1,1]{2,1,0:T(1,128)S(1)}, u32[]{:S(2)}, u32[]{:S(2)}) async-start(f32[16,1,1]{2,1,0:T(1,128)} %broadcast_in_dim.35), calls=%async_computation | async-start | bytes 16384 | tf_op jit(solution)/shard_map/all_to_all | solution.py:32
  27.0 70.2 %collective-permute-start.8 = (f32[1,32,128]{2,0,1:T(1,128)}, f32[1,32,128]{2,0,1:T(1,128)S(1)}, u32[]{:S(2)}, u32[]{:S(2)}) collective-permute-start(f32[1,32,128]{2,0,1:T(1,128)} %get-tuple-element.348), channel_id=1, source_target_pairs={{0,16},{16,32},{32,48},{48,64},{64,80},{80,96},{96,112},{112,128},... | collective-permute-start | bytes 49160 | tf_op jit(solution)/shard_map/ppermute | solution.py:17
  30.9 66.3 %collective-permute-start.9 = (f32[1,32,128]{2,0,1:T(1,128)}, f32[1,32,128]{2,0,1:T(1,128)S(1)}, u32[]{:S(2)}, u32[]{:S(2)}) collective-permute-start(f32[1,32,128]{2,0,1:T(1,128)} %get-tuple-element.349), channel_id=1, source_target_pairs={{16,0},{32,16},{48,32},{64,48},{80,64},{96,80},{112,96},{128,112},... | collective-permute-start | bytes 49160 | tf_op jit(solution)/shard_map/ppermute | solution.py:19
  32.9 26.1 %copy-start.16 = (f32[128]{0:T(128)}, f32[128]{0:T(128)S(1)}, u32[]{:S(2)}) copy-start(f32[128]{0:T(128)S(1)} %get-tuple-element.360) | copy-start | bytes 1540
  32.9 28.9 %copy-start.10 = (f32[128]{0:T(128)}, f32[128]{0:T(128)S(1)}, u32[]{:S(2)}) copy-start(f32[128]{0:T(128)S(1)} %get-tuple-element.361) | copy-start | bytes 1540
  35.0 24.1 %copy-start.7 = (f32[34,34]{1,0:T(8,128)}, f32[34,34]{1,0:T(8,128)S(1)}, u32[]{:S(2)}) copy-start(f32[34,34]{1,0:T(8,128)S(1)} %broadcast_add_fusion.1) | copy-start | bytes 13876
  37.8 19.5 %collective-permute-start.2 = (f32[34,1,128]{2,0,1:T(8,128)S(1)}, f32[34,1,128]{2,0,1:T(8,128)S(1)}, u32[]{:S(2)}, u32[]{:S(2)}) collective-permute-start(f32[34,1,128]{2,0,1:T(8,128)S(1)} %get-tuple-element.342), channel_id=1, source_target_pairs={{0,1},{1,2},{2,3},{3,4},{4,5},{5,6},{6,7},{7,8},{8,9},{9,10},{10,1... | collective-permute-start | bytes 52232 | tf_op jit(solution)/shard_map/ppermute | solution.py:17
  41.3 16.0 %collective-permute-start.3 = (f32[34,1,128]{2,0,1:T(8,128)S(1)}, f32[34,1,128]{2,0,1:T(8,128)S(1)}, u32[]{:S(2)}, u32[]{:S(2)}) collective-permute-start(f32[34,1,128]{2,0,1:T(8,128)S(1)} %get-tuple-element.343), channel_id=1, source_target_pairs={{1,0},{2,1},{3,2},{4,3},{5,4},{6,5},{7,6},{8,7},{9,8},{10,9},{11,1... | collective-permute-start | bytes 52232 | tf_op jit(solution)/shard_map/ppermute | solution.py:19
  42.7 19.2 %copy-start.12 = (f32[128]{0:T(128)}, f32[128]{0:T(128)S(1)}, u32[]{:S(2)}) copy-start(f32[128]{0:T(128)S(1)} %broadcast_multiply_fusion) | copy-start | bytes 1540
  47.8 26.4 %all-to-all-start.1 = ((f32[32,1,16]{2,1,0:T(1,128)}), f32[32,1,16]{2,1,0:T(1,128)S(1)}, u32[]{:S(2)}, u32[]{:S(2)}) async-start(f32[32,1,16]{2,1,0:T(1,128)} %broadcast_in_dim.37), calls=%async_computation.1 | async-start | bytes 32768 | tf_op jit(solution)/shard_map/all_to_all | solution.py:32
  68.7 7.3 %collective-permute-start.4 = (f32[3,1,32,128]{3,2,1,0:T(8,128)}, f32[3,1,32,128]{3,2,1,0:T(8,128)S(1)}, u32[]{:S(2)}, u32[]{:S(2)}) collective-permute-start(f32[3,1,32,128]{3,2,1,0:T(8,128)} %get-tuple-element.319), channel_id=1, source_target_pairs={{0,16},{16,32},{32,48},{48,64},{64,80},{80,96},{96,112},{112,128},... | collective-permute-start | bytes 147464 | tf_op jit(solution)/shard_map/ppermute | solution.py:17
  72.3 5.6 %collective-permute-start.5 = (f32[3,1,32,128]{3,2,1,0:T(8,128)}, f32[3,1,32,128]{3,2,1,0:T(8,128)S(1)}, u32[]{:S(2)}, u32[]{:S(2)}) collective-permute-start(f32[3,1,32,128]{3,2,1,0:T(8,128)} %get-tuple-element.318), channel_id=1, source_target_pairs={{16,0},{32,16},{48,32},{64,48},{80,64},{96,80},{112,96},{128,112},... | collective-permute-start | bytes 147464 | tf_op jit(solution)/shard_map/ppermute | solution.py:19
  77.9 31.6 %copy-start.9 = (f32[130]{0:T(256)S(1)}, f32[130]{0:T(256)}, u32[]{:S(2)}) copy-start(f32[130]{0:T(256)} %pad.141.clone) | copy-start | bytes 1564
  77.9 5.8 %collective-permute-start.6 = (f32[3,34,1,128]{3,1,2,0:T(8,128)S(1)}, f32[3,34,1,128]{3,1,2,0:T(8,128)S(1)}, u32[]{:S(2)}, u32[]{:S(2)}) collective-permute-start(f32[3,34,1,128]{3,1,2,0:T(8,128)S(1)} %get-tuple-element.315), channel_id=1, source_target_pairs={{0,1},{1,2},{2,3},{3,4},{4,5},{5,6},{6,7},{7,8},{8,9},{9,10},{10,1... | collective-permute-start | bytes 156680 | tf_op jit(solution)/shard_map/ppermute | solution.py:17
  82.5 5.0 %collective-permute-start.7 = (f32[3,34,1,128]{3,1,2,0:T(8,128)S(1)}, f32[3,34,1,128]{3,1,2,0:T(8,128)S(1)}, u32[]{:S(2)}, u32[]{:S(2)}) collective-permute-start(f32[3,34,1,128]{3,1,2,0:T(8,128)S(1)} %get-tuple-element.314), channel_id=1, source_target_pairs={{1,0},{2,1},{3,2},{4,3},{5,4},{6,5},{7,6},{8,7},{9,8},{10,9},{11,1... | collective-permute-start | bytes 156680 | tf_op jit(solution)/shard_map/ppermute | solution.py:19
  91.5 10.4 %collective-permute-start.12 = (f32[1,32,128]{2,0,1:T(1,128)S(1)}, f32[1,32,128]{2,0,1:T(1,128)S(1)}, u32[]{:S(2)}, u32[]{:S(2)}) collective-permute-start(f32[1,32,128]{2,0,1:T(1,128)S(1)} %get-tuple-element.351), channel_id=1, source_target_pairs={{16,0},{32,16},{48,32},{64,48},{80,64},{96,80},{112,96},{128,112},... | collective-permute-start | bytes 49160 | tf_op jit(solution)/shard_map/ppermute | solution.py:19
  93.4 8.5 %collective-permute-start.13 = (f32[1,32,128]{2,0,1:T(1,128)S(1)}, f32[1,32,128]{2,0,1:T(1,128)S(1)}, u32[]{:S(2)}, u32[]{:S(2)}) collective-permute-start(f32[1,32,128]{2,0,1:T(1,128)S(1)} %get-tuple-element.350), channel_id=1, source_target_pairs={{0,16},{16,32},{32,48},{48,64},{64,80},{80,96},{96,112},{112,128},... | collective-permute-start | bytes 49160 | tf_op jit(solution)/shard_map/ppermute | solution.py:17
  97.3 12.2 %collective-permute-start.10 = (f32[34,1,128]{2,0,1:T(8,128)S(1)}, f32[34,1,128]{2,0,1:T(8,128)S(1)}, u32[]{:S(2)}, u32[]{:S(2)}) collective-permute-start(f32[34,1,128]{2,0,1:T(8,128)S(1)} %get-tuple-element.338), channel_id=1, source_target_pairs={{0,1},{1,2},{2,3},{3,4},{4,5},{5,6},{6,7},{7,8},{8,9},{9,10},{10,1... | collective-permute-start | bytes 52232 | tf_op jit(solution)/shard_map/ppermute | solution.py:17
  100.6 8.9 %collective-permute-start.11 = (f32[34,1,128]{2,0,1:T(8,128)S(1)}, f32[34,1,128]{2,0,1:T(8,128)S(1)}, u32[]{:S(2)}, u32[]{:S(2)}) collective-permute-start(f32[34,1,128]{2,0,1:T(8,128)S(1)} %get-tuple-element.339), channel_id=1, source_target_pairs={{1,0},{2,1},{3,2},{4,3},{5,4},{6,5},{7,6},{8,7},{9,8},{10,9},{11,1... | collective-permute-start | bytes 52232 | tf_op jit(solution)/shard_map/ppermute | solution.py:19
  101.9 8.2 %collective-permute-start.14 = (f32[34,1,128]{2,0,1:T(8,128)S(1)}, f32[34,1,128]{2,0,1:T(8,128)S(1)}, u32[]{:S(2)}, u32[]{:S(2)}) collective-permute-start(f32[34,1,128]{2,0,1:T(8,128)S(1)} %get-tuple-element.341), channel_id=1, source_target_pairs={{1,0},{2,1},{3,2},{4,3},{5,4},{6,5},{7,6},{8,7},{9,8},{10,9},{11,1... | collective-permute-start | bytes 52232 | tf_op jit(solution)/shard_map/ppermute | solution.py:19
  103.2 7.0 %collective-permute-start.15 = (f32[34,1,128]{2,0,1:T(8,128)S(1)}, f32[34,1,128]{2,0,1:T(8,128)S(1)}, u32[]{:S(2)}, u32[]{:S(2)}) collective-permute-start(f32[34,1,128]{2,0,1:T(8,128)S(1)} %get-tuple-element.340), channel_id=1, source_target_pairs={{0,1},{1,2},{2,3},{3,4},{4,5},{5,6},{6,7},{7,8},{8,9},{9,10},{10,1... | collective-permute-start | bytes 52232 | tf_op jit(solution)/shard_map/ppermute | solution.py:17
  110.1 1.0 copy-start
  142.1 14.6 %all-to-all-start.4 = ((f32[16,1,1]{2,1,0:T(1,128)}), f32[16,1,1]{2,1,0:T(1,128)S(1)}, u32[]{:S(2)}, u32[]{:S(2)}) async-start(f32[16,1,1]{2,1,0:T(1,128)} %broadcast_in_dim.42), calls=%async_computation.4 | async-start | bytes 16384 | tf_op jit(solution)/shard_map/all_to_all | solution.py:32
  158.0 18.6 %all-to-all-start.3 = ((f32[32,1,1]{2,1,0:T(1,128)}), f32[32,1,1]{2,1,0:T(1,128)S(1)}, u32[]{:S(2)}, u32[]{:S(2)}) async-start(f32[32,1,1]{2,1,0:T(1,128)} %broadcast_in_dim.39), calls=%async_computation.3 | async-start | bytes 32768 | tf_op jit(solution)/shard_map/all_to_all | solution.py:32
  177.9 11.2 %all-to-all-start.5 = ((f32[32,1,1]{2,1,0:T(1,128)}), f32[32,1,1]{2,1,0:T(1,128)S(1)}, u32[]{:S(2)}, u32[]{:S(2)}) async-start(f32[32,1,1]{2,1,0:T(1,128)} %broadcast_in_dim.43), calls=%async_computation.5 | async-start | bytes 32768 | tf_op jit(solution)/shard_map/all_to_all | solution.py:32
  192.8 4.7 %collective-permute-start.16 = (f32[1,32,128]{2,0,1:T(1,128)S(1)}, f32[1,32,128]{2,0,1:T(1,128)S(1)}, u32[]{:S(2)}, u32[]{:S(2)}) collective-permute-start(f32[1,32,128]{2,0,1:T(1,128)S(1)} %get-tuple-element.346), channel_id=1, source_target_pairs={{0,16},{16,32},{32,48},{48,64},{64,80},{80,96},{96,112},{112,128},... | collective-permute-start | bytes 49160 | tf_op jit(solution)/shard_map/ppermute | solution.py:17
  195.6 5.1 %collective-permute-start.17 = (f32[1,32,128]{2,0,1:T(1,128)S(1)}, f32[1,32,128]{2,0,1:T(1,128)S(1)}, u32[]{:S(2)}, u32[]{:S(2)}) collective-permute-start(f32[1,32,128]{2,0,1:T(1,128)S(1)} %get-tuple-element.347), channel_id=1, source_target_pairs={{16,0},{32,16},{48,32},{64,48},{80,64},{96,80},{112,96},{128,112},... | collective-permute-start | bytes 49160 | tf_op jit(solution)/shard_map/ppermute | solution.py:19
  200.7 28.7 %collective-permute-start.18 = (f32[34,1,128]{2,0,1:T(8,128)S(1)}, f32[34,1,128]{2,0,1:T(8,128)S(1)}, u32[]{:S(2)}, u32[]{:S(2)}) collective-permute-start(f32[34,1,128]{2,0,1:T(8,128)S(1)} %get-tuple-element.336), channel_id=1, source_target_pairs={{0,1},{1,2},{2,3},{3,4},{4,5},{5,6},{6,7},{7,8},{8,9},{9,10},{10,1... | collective-permute-start | bytes 52232 | tf_op jit(solution)/shard_map/ppermute | solution.py:17
  202.8 26.6 %collective-permute-start.19 = (f32[34,1,128]{2,0,1:T(8,128)S(1)}, f32[34,1,128]{2,0,1:T(8,128)S(1)}, u32[]{:S(2)}, u32[]{:S(2)}) collective-permute-start(f32[34,1,128]{2,0,1:T(8,128)S(1)} %get-tuple-element.337), channel_id=1, source_target_pairs={{1,0},{2,1},{3,2},{4,3},{5,4},{6,5},{7,6},{8,7},{9,8},{10,9},{11,1... | collective-permute-start | bytes 52232 | tf_op jit(solution)/shard_map/ppermute | solution.py:19
  221.5 25.8 %all-to-all-start.7 = ((f32[32,1,16]{2,1,0:T(1,128)}), f32[32,1,16]{2,1,0:T(1,128)S(1)}, u32[]{:S(2)}, u32[]{:S(2)}) async-start(f32[32,1,16]{2,1,0:T(1,128)} %broadcast_in_dim.46), calls=%async_computation.7 | async-start | bytes 32768 | tf_op jit(solution)/shard_map/all_to_all | solution.py:32
  229.3 1.8 copy-start.8
  229.3 1.8 copy-start.11
  229.3 1.8 copy-start.13
  229.3 1.8 copy-start.17
  241.6 7.9 %collective-permute-start.20 = (f32[3,1,32,128]{3,2,1,0:T(8,128)}, f32[3,1,32,128]{3,2,1,0:T(8,128)}, u32[]{:S(2)}, u32[]{:S(2)}) collective-permute-start(f32[3,1,32,128]{3,2,1,0:T(8,128)} %get-tuple-element.317), channel_id=1, source_target_pairs={{0,16},{16,32},{32,48},{48,64},{64,80},{80,96},{96,112},{112,128},... | collective-permute-start | bytes 147464 | tf_op jit(solution)/shard_map/ppermute | solution.py:17
  245.1 5.7 %collective-permute-start.21 = (f32[3,1,32,128]{3,2,1,0:T(8,128)}, f32[3,1,32,128]{3,2,1,0:T(8,128)}, u32[]{:S(2)}, u32[]{:S(2)}) collective-permute-start(f32[3,1,32,128]{3,2,1,0:T(8,128)} %get-tuple-element.316), channel_id=1, source_target_pairs={{16,0},{32,16},{48,32},{64,48},{80,64},{96,80},{112,96},{128,112},... | collective-permute-start | bytes 147464 | tf_op jit(solution)/shard_map/ppermute | solution.py:19
  248.0 1.1 copy-start.3
  251.6 23.4 %copy-start.1 = (f32[32,32,128]{2,0,1:T(8,128)S(1)}, f32[32,32,128]{2,0,1:T(8,128)}, u32[]{:S(2)}) copy-start(f32[32,32,128]{2,0,1:T(8,128)} %get-tuple-element.308) | copy-start | bytes 1572868
  251.6 5.3 %collective-permute-start.22 = (f32[3,34,1,128]{3,1,2,0:T(8,128)S(1)}, f32[3,34,1,128]{3,1,2,0:T(8,128)S(1)}, u32[]{:S(2)}, u32[]{:S(2)}) collective-permute-start(f32[3,34,1,128]{3,1,2,0:T(8,128)S(1)} %get-tuple-element.313), channel_id=1, source_target_pairs={{0,1},{1,2},{2,3},{3,4},{4,5},{5,6},{6,7},{7,8},{8,9},{9,10},{10,1... | collective-permute-start | bytes 156680 | tf_op jit(solution)/shard_map/ppermute | solution.py:17
  255.6 5.0 %collective-permute-start.23 = (f32[3,34,1,128]{3,1,2,0:T(8,128)S(1)}, f32[3,34,1,128]{3,1,2,0:T(8,128)S(1)}, u32[]{:S(2)}, u32[]{:S(2)}) collective-permute-start(f32[3,34,1,128]{3,1,2,0:T(8,128)S(1)} %get-tuple-element.312), channel_id=1, source_target_pairs={{1,0},{2,1},{3,2},{4,3},{5,4},{6,5},{7,6},{8,7},{9,8},{10,9},{11,1... | collective-permute-start | bytes 156680 | tf_op jit(solution)/shard_map/ppermute | solution.py:19
  313.0 5.6 %collective-permute-start.24 = (f32[1,32,128]{2,0,1:T(1,128)S(1)}, f32[1,32,128]{2,0,1:T(1,128)S(1)}, u32[]{:S(2)}, u32[]{:S(2)}) collective-permute-start(f32[1,32,128]{2,0,1:T(1,128)S(1)} %get-tuple-element.345), channel_id=1, source_target_pairs={{16,0},{32,16},{48,32},{64,48},{80,64},{96,80},{112,96},{128,112},... | collective-permute-start | bytes 49160 | tf_op jit(solution)/shard_map/ppermute | solution.py:19
  315.6 3.9 %collective-permute-start.25 = (f32[1,32,128]{2,0,1:T(1,128)S(1)}, f32[1,32,128]{2,0,1:T(1,128)S(1)}, u32[]{:S(2)}, u32[]{:S(2)}) collective-permute-start(f32[1,32,128]{2,0,1:T(1,128)S(1)} %get-tuple-element.344), channel_id=1, source_target_pairs={{0,16},{16,32},{32,48},{48,64},{64,80},{80,96},{96,112},{112,128},... | collective-permute-start | bytes 49160 | tf_op jit(solution)/shard_map/ppermute | solution.py:17
  319.5 5.3 %collective-permute-start.26 = (f32[34,1,128]{2,0,1:T(8,128)S(1)}, f32[34,1,128]{2,0,1:T(8,128)S(1)}, u32[]{:S(2)}, u32[]{:S(2)}) collective-permute-start(f32[34,1,128]{2,0,1:T(8,128)S(1)} %get-tuple-element.335), channel_id=1, source_target_pairs={{1,0},{2,1},{3,2},{4,3},{5,4},{6,5},{7,6},{8,7},{9,8},{10,9},{11,1... | collective-permute-start | bytes 52232 | tf_op jit(solution)/shard_map/ppermute | solution.py:19
  320.8 4.9 %collective-permute-start.27 = (f32[34,1,128]{2,0,1:T(8,128)S(1)}, f32[34,1,128]{2,0,1:T(8,128)S(1)}, u32[]{:S(2)}, u32[]{:S(2)}) collective-permute-start(f32[34,1,128]{2,0,1:T(8,128)S(1)} %get-tuple-element.334), channel_id=1, source_target_pairs={{0,1},{1,2},{2,3},{3,4},{4,5},{5,6},{6,7},{7,8},{8,9},{9,10},{10,1... | collective-permute-start | bytes 52232 | tf_op jit(solution)/shard_map/ppermute | solution.py:17
  (4 other events, 3.5 us)

commit v2 on v1

--- a/solution.py
+++ b/solution.py
@@ -94,9 +94,26 @@
     return result
 
 
+def face_halo(cells):
+    count_x = lax.axis_size("gx")
+    count_y = lax.axis_size("gy")
+    up_x = [(i, i + 1) for i in range(count_x - 1)]
+    down_x = [(i + 1, i) for i in range(count_x - 1)]
+    up_y = [(i, i + 1) for i in range(count_y - 1)]
+    down_y = [(i + 1, i) for i in range(count_y - 1)]
+    low_x = lax.ppermute(cells[-1:], "gx", up_x)
+    high_x = lax.ppermute(cells[:1], "gx", down_x)
+    low_y = lax.ppermute(cells[:, -1:], "gy", up_y)
+    high_y = lax.ppermute(cells[:, :1], "gy", down_y)
+    middle = jnp.concatenate([low_y, cells, high_y], axis=1)
+    pad_y = ((0, 0), (1, 1), (0, 0))
+    return jnp.concatenate([jnp.pad(low_x, pad_y), middle, jnp.pad(high_x, pad_y)], axis=0)
+
+
 def body(rhs, heights, index_map, coarse_inverse):
     rows_x, rows_y, depth = rhs.shape
     subdomains = coarse_inverse.shape[0]
+    cells = rows_x * rows_y * depth
     high = lax.Precision.HIGHEST
     levels = jnp.arange(depth, dtype=jnp.int32)
     solid = (levels[None, None, :] < heights[:, :, None]).astype(jnp.float32)
@@ -113,45 +130,66 @@
     sine_z, value_z = sine_table(depth)
     inv_eig = 1.0 / (value_x[:, None, None] + value_y[None, :, None] + value_z[None, None, :])
     my_slot = lax.dynamic_index_in_dim(index_map, lax.axis_index(("gx", "gy")), 0, keepdims=False)
-    inverse_row = lax.dynamic_index_in_dim(coarse_inverse, my_slot, 0, keepdims=False).astype(
-        jnp.float32
-    )
-    picked_row = inverse_row[index_map]
+    inverse = coarse_inverse.astype(jnp.float32)
+    none = jnp.zeros((0,), jnp.float32)
 
-    def precondition(resid):
-        masked = resid * fluid
+    def local_solve(masked):
         wide = extend(masked)
         spectral = modal(wide, sine_x, sine_y, sine_z) * inv_eig
-        local = margin_sum(modal(spectral, sine_x, sine_y, sine_z))
-        coarse_res = jnp.sum(masked) / (rows_x * rows_y * depth)
-        every = exchange(coarse_res.reshape(1), jnp.zeros((0,), jnp.float32))[0]
-        coarse_value = jnp.sum(picked_row * every)
-        return fluid * (local + coarse_value)
+        return margin_sum(modal(spectral, sine_x, sine_y, sine_z))
 
-    def energy_sum(resid, precond):
-        return total(jnp.sum(resid * precond))
+    def coarse(gathered):
+        vec = jnp.zeros((subdomains,), jnp.float32).at[index_map].set(gathered)
+        sol = jnp.dot(inverse, vec, precision=high)
+        return vec, sol, lax.dynamic_index_in_dim(sol, my_slot, 0, keepdims=False)
 
-    source = fluid * rhs
-    solution = jnp.zeros_like(source)
-    residual = source
-    precond = precondition(residual)
-    direction = precond
-    energy_now = energy_sum(residual, precond)
-    for iteration in range(ITERS):
-        operate_wide = extend(direction)
-        padded_field = jnp.pad(operate_wide, ((0, 0), (0, 0), (1, 1)))
+    def operate(direction):
+        padded_field = jnp.pad(face_halo(direction), ((0, 0), (0, 0), (1, 1)))
         beside = jnp.zeros_like(direction)
         for operate_weight, value in zip(beside_all(fluid_wide), beside_all(padded_field)):
             beside = beside + operate_weight * value
-        image = fluid * (count * direction - beside) + solid * direction
-        step_size = energy_now / total(jnp.sum(direction * image))
-        solution = solution + step_size * direction
-        residual = residual - step_size * image
-        if iteration + 1 < ITERS:
-            precond = precondition(residual)
-            energy_next = energy_sum(residual, precond)
-            direction = precond + energy_next / energy_now * direction
-            energy_now = energy_next
+        return fluid * (count * direction - beside) + solid * direction
+
+    residual = fluid * rhs
+    masked = residual * fluid
+    local0 = local_solve(masked)
+    every, partial = exchange(
+        (jnp.sum(masked) / cells).reshape(1), jnp.sum(residual * fluid * local0).reshape(1)
+    )
+    vec0, sol0, value0 = coarse(every)
+    energy_now = partial[0] + cells * jnp.sum(vec0 * sol0)
+    precond = fluid * (local0 + value0)
+    direction = precond
+
+    image = operate(direction)
+    masked_w = image * fluid
+    local_w = local_solve(masked_w)
+    every_w, partial = exchange(
+        (jnp.sum(masked_w) / cells).reshape(1),
+        jnp.stack(
+            [
+                jnp.sum(direction * image),
+                jnp.sum(residual * fluid * local_w),
+                jnp.sum(image * fluid * local0),
+                jnp.sum(image * fluid * local_w),
+            ]
+        ),
+    )
+    vec_w, sol_w, value_w = coarse(every_w)
+    step_size = energy_now / partial[0]
+    solution = step_size * direction
+    residual = residual - step_size * image
+    cross_r = partial[1] + cells * jnp.sum(vec0 * sol_w)
+    cross_w = partial[2] + cells * jnp.sum(vec_w * sol0)
+    square_w = partial[3] + cells * jnp.sum(vec_w * sol_w)
+    energy_next = energy_now - step_size * (cross_r + cross_w) + step_size * step_size * square_w
+    precond = precond - step_size * (fluid * (local_w + value_w))
+    direction = precond + energy_next / energy_now * direction
+
+    image = operate(direction)
+    step_size = energy_next / total(jnp.sum(direction * image))
+    solution = solution + step_size * direction
+    residual = residual - step_size * image
     return (solution, residual)
 
 

time: 372 us -> 316 us (0.85)
  blocking collectives: 108 us -> 47.1 us
  starting transfers between devices: 126 us -> 107 us
  local copies, waits for them, and re-layouts: 39.9 us -> 51.8 us
  other arithmetic: 37.8 us -> 42.9 us
    all_to_all x6 -> x3, blocking collectives: 108 us -> 47.1 us  [exchange(): lax.all_to_all(jnp.broadcast_to(stage[None], (count,) + stage.shape), axi...]
    ppermute x14 -> x10, starting transfers between devices: 51 us -> 30.2 us  [with_halo(): lax.ppermute(tail, axis, [(i, (i + 1) % count) for i in range(ends)])]
    ppermute x0 -> x8, starting transfers between devices: none -> 18.1 us  [the longest x2 5.99 us: face_halo(): low_x = lax.ppermute(cells[-1:], 'gx', up_x)]
    all_to_all x6 -> x3, starting transfers between devices: 48 us -> 38.1 us  [exchange(): lax.all_to_all(jnp.broadcast_to(stage[None], (count,) + stage.shape), axi...]
    ppermute x14 -> x10, starting transfers between devices: 26.9 us -> 21 us  [with_halo(): lax.ppermute(head, axis, [((i + 1) % count, i) for i in range(ends)])]
    broadcast_in_dim x12 -> x6, local copies, waits for them, and re-layouts: 8.87 us -> 3.22 us  [exchange(): jnp.broadcast_to(stage[None], (count,) + stage.shape)]
    ppermute x0 -> x8, waiting for transfers between devices: none -> 5.5 us  [the longest x2 5.48 us: face_halo(): high_y = lax.ppermute(cells[:, :1], 'gy', down_y)]
    scatter x0 -> x2, local copies, waits for them, and re-layouts: none -> 5.32 us  [coarse(): vec = jnp.zeros((subdomains,), jnp.float32).at[index_map].set(gathered)]
  transfers between devices with their start and end apart: 34 -> 31, of which waited for: 11 -> 11; matrix products, arithmetic and copies ran while one was open for 12% -> 14% of each run, Pallas kernels for 0% -> 0%
where the time goes in v2:
time: 316 us; the launch traced here: 313 us
  starting transfers between devices  107 us (34%)
  local copies, waits for them, and re-layouts  51.8 us (16%)
  blocking collectives  47.1 us (15%)
  other arithmetic  42.9 us (14%)
  waiting for transfers between devices  40.8 us (13%)
  matrix products  11.9 us (4%)
  between operations  11.4 us (4%)
    all_to_all x3, blocking collectives, exchange(): lax.all_to_all(jnp.broadcast_to(stage[None], (count,) + stage.shape), axi...  47.1 us
    all_to_all x3, starting transfers between devices, exchange(): lax.all_to_all(jnp.broadcast_to(stage[None], (count,) + stage.shape), axi...  38.1 us
    ppermute x10, starting transfers between devices, with_halo(): lax.ppermute(tail, axis, [(i, (i + 1) % count) for i in range(ends)])  30.2 us
    ppermute x10, starting transfers between devices, with_halo(): lax.ppermute(head, axis, [((i + 1) % count, i) for i in range(ends)])  21 us
    all_to_all x3, waiting for transfers between devices, exchange(): lax.all_to_all(jnp.broadcast_to(stage[None], (count,) + stage.shape), axi...  18.1 us
    ppermute x10, waiting for transfers between devices, with_halo(): lax.ppermute(head, axis, [((i + 1) % count, i) for i in range(ends)])  17.2 us
    another operation x6, other arithmetic, margin_sum(): jnp.stack([face_x, face_y, corner])  6.79 us
  transfers between devices with their start and end apart: 31, of which 11 were waited for; matrix products, arithmetic and copies ran while one was open for 14% of the time, Pallas kernels for 0%

profile of v2, /device:TPU:1, one launch (start us, length us, event | category | flops | bytes accessed | tf_op | source)
XLA Modules:
  0.0 313.3 jit_solution(4100759829248072953)
XLA Ops:
  3.0 4.6 %collective-permute-start = (f32[1,32,128]{2,0,1:T(1,128)S(1)}, f32[1,32,128]{2,0,1:T(1,128)S(1)}, u32[]{:S(2)}, u32[]{:S(2)}) collective-permute-start(f32[1,32,128]{2,0,1:T(1,128)S(1)} %get-tuple-element.354), channel_id=1, source_target_pairs={{0,16},{16,32},{32,48},{48,64},{64,80},{80,96},{96,112},{112,128},... | collective-permute-start | bytes 49160 | tf_op jit(solution)/shard_map/ppermute | solution.py:17
  7.5 5.5 %collective-permute-start.1 = (f32[1,32,128]{2,0,1:T(1,128)S(1)}, f32[1,32,128]{2,0,1:T(1,128)S(1)}, u32[]{:S(2)}, u32[]{:S(2)}) collective-permute-start(f32[1,32,128]{2,0,1:T(1,128)S(1)} %get-tuple-element.355), channel_id=1, source_target_pairs={{16,0},{32,16},{48,32},{64,48},{80,64},{96,80},{112,96},{128,112},... | collective-permute-start | bytes 49160 | tf_op jit(solution)/shard_map/ppermute | solution.py:19
  15.8 3.0 collective-permute-start.9
  23.1 3.3 %collective-permute-done.3 = f32[34,1,128]{2,0,1:T(8,128)S(1)} collective-permute-done((f32[34,1,128]{2,0,1:T(8,128)S(1)}, f32[34,1,128]{2,0,1:T(8,128)S(1)}, u32[]{:S(2)}, u32[]{:S(2)}) %collective-permute-start.3) | collective-permute-done | bytes 17440 | tf_op jit(solution)/shard_map/ppermute | solution.py:19
  32.1 1.9 slice_bitcast_fusion.15
  38.0 4.2 %collective-permute-start.4 = (f32[3,1,32,128]{3,2,1,0:T(8,128)}, f32[3,1,32,128]{3,2,1,0:T(8,128)S(1)}, u32[]{:S(2)}, u32[]{:S(2)}) collective-permute-start(f32[3,1,32,128]{3,2,1,0:T(8,128)} %get-tuple-element.321), channel_id=1, source_target_pairs={{0,16},{16,32},{32,48},{48,64},{64,80},{80,96},{96,112},{112,128},... | collective-permute-start | bytes 147464 | tf_op jit(solution)/shard_map/ppermute | solution.py:17
  42.2 1.9 collective-permute-start.5
  48.7 3.5 %collective-permute-start.6 = (f32[3,34,1,128]{3,1,2,0:T(8,128)S(1)}, f32[3,34,1,128]{3,1,2,0:T(8,128)S(1)}, u32[]{:S(2)}, u32[]{:S(2)}) collective-permute-start(f32[3,34,1,128]{3,1,2,0:T(8,128)S(1)} %get-tuple-element.317), channel_id=1, source_target_pairs={{0,1},{1,2},{2,3},{3,4},{4,5},{5,6},{6,7},{7,8},{8,9},{9,10},{10,1... | collective-permute-start | bytes 156680 | tf_op jit(solution)/shard_map/ppermute | solution.py:17
  55.2 4.9 %collective-permute-done.7 = f32[3,34,1,128]{3,1,2,0:T(8,128)S(1)} collective-permute-done((f32[3,34,1,128]{3,1,2,0:T(8,128)S(1)}, f32[3,34,1,128]{3,1,2,0:T(8,128)S(1)}, u32[]{:S(2)}, u32[]{:S(2)}) %collective-permute-start.7) | collective-permute-done | bytes 52256 | tf_op jit(solution)/shard_map/ppermute | solution.py:19
  66.5 13.1 %all-to-all-start = ((f32[16,1,2]{2,1,0:T(1,128)}), f32[16,1,2]{2,1,0:T(1,128)S(1)}, u32[]{:S(2)}, u32[]{:S(2)}) async-start(f32[16,1,2]{2,1,0:T(1,128)} %broadcast_in_dim.18), calls=%async_computation | async-start | bytes 16384 | tf_op jit(solution)/shard_map/all_to_all | solution.py:32
  81.6 9.2 %all-to-all-done = f32[16,1,2]{2,1,0:T(1,128)S(1)} async-done(((f32[16,1,2]{2,1,0:T(1,128)}), f32[16,1,2]{2,1,0:T(1,128)S(1)}, u32[]{:S(2)}, u32[]{:S(2)}) %all-to-all-start) | async-done | bytes 160 | tf_op jit(solution)/shard_map/all_to_all | solution.py:32
  92.8 12.8 %all-to-all-start.1 = ((f32[32,1,17]{2,1,0:T(1,128)}), f32[32,1,17]{2,1,0:T(1,128)S(1)}, u32[]{:S(2)}, u32[]{:S(2)}) async-start(f32[32,1,17]{2,1,0:T(1,128)} %broadcast_in_dim.19), calls=%async_computation.1 | async-start | bytes 32768 | tf_op jit(solution)/shard_map/all_to_all | solution.py:32
  106.3 2.2 collective-permute-start.10
  109.8 2.7 all-to-all-done.1
  112.5 2.7 scatter_custom_fusion
  117.4 2.6 collective-permute-start.14
  119.9 3.0 collective-permute-start.15
  122.9 2.2 collective-permute-start.12
  127.9 2.1 collective-permute-done.13
  130.6 2.6 multiply_reduce_fusion.4
  133.4 3.1 collective-permute-start.16
  136.5 1.9 collective-permute-start.17
  138.4 3.1 collective-permute-done.17
  141.6 2.1 collective-permute-start.18
  145.0 3.2 %collective-permute-done.19 = f32[34,1,128]{2,0,1:T(8,128)S(1)} collective-permute-done((f32[34,1,128]{2,0,1:T(8,128)S(1)}, f32[34,1,128]{2,0,1:T(8,128)S(1)}, u32[]{:S(2)}, u32[]{:S(2)}) %collective-permute-start.19) | collective-permute-done | bytes 17440 | tf_op jit(solution)/shard_map/ppermute | solution.py:19
  154.7 2.5 slice_bitcast_fusion.9
  158.0 2.6 scatter.60
  164.4 3.4 %collective-permute-start.20 = (f32[3,1,32,128]{3,2,1,0:T(8,128)S(1)}, f32[3,1,32,128]{3,2,1,0:T(8,128)S(1)}, u32[]{:S(2)}, u32[]{:S(2)}) collective-permute-start(f32[3,1,32,128]{3,2,1,0:T(8,128)S(1)} %get-tuple-element.319), channel_id=1, source_target_pairs={{0,16},{16,32},{32,48},{48,64},{64,80},{80,96},{96,112},{112,128},... | collective-permute-start | bytes 147464 | tf_op jit(solution)/shard_map/ppermute | solution.py:17
  167.8 2.1 collective-permute-start.21
  174.0 3.8 %collective-permute-start.22 = (f32[3,34,1,128]{3,1,2,0:T(8,128)}, f32[3,34,1,128]{3,1,2,0:T(8,128)}, u32[]{:S(2)}, u32[]{:S(2)}) collective-permute-start(f32[3,34,1,128]{3,1,2,0:T(8,128)} %get-tuple-element.315), channel_id=1, source_target_pairs={{0,1},{1,2},{2,3},{3,4},{4,5},{5,6},{6,7},{7,8},{8,9},{9,10},{10,1... | collective-permute-start | bytes 156680 | tf_op jit(solution)/shard_map/ppermute | solution.py:17
  186.3 2.1 copy.137
  192.7 2.6 broadcast_select_fusion.2
  195.3 2.6 scatter-add.75
  199.9 2.1 copy.138
  204.0 2.2 multiply_reduce_fusion.1
  206.8 2.6 concatenate.161
  209.4 18.5 %all_to_all.48 = f32[16,1,5]{2,1,0:T(1,128)S(1)} all-to-all(f32[16,1,5]{2,1,0:T(1,128)S(1)} %broadcast_in_dim.23), channel_id=1, replica_groups=mesh['gx'=32,'gy'=16] {'gy'}, dimensions={0} | all-to-all | bytes 640 | tf_op jit(solution)/shard_map/all_to_all | solution.py:32
  228.7 12.2 %all-to-all-start.3 = ((f32[32,1,20]{2,1,0:T(1,128)}), f32[32,1,20]{2,1,0:T(1,128)S(1)}, u32[]{:S(2)}, u32[]{:S(2)}) async-start(f32[32,1,20]{2,1,0:T(1,128)} %broadcast_in_dim.24), calls=%async_computation.3 | async-start | bytes 32768 | tf_op jit(solution)/shard_map/all_to_all | solution.py:32
  241.6 6.3 %all-to-all-done.3 = f32[32,1,20]{2,1,0:T(1,128)S(1)} async-done(((f32[32,1,20]{2,1,0:T(1,128)}), f32[32,1,20]{2,1,0:T(1,128)S(1)}, u32[]{:S(2)}, u32[]{:S(2)}) %all-to-all-start.3) | async-done | bytes 2592 | tf_op jit(solution)/shard_map/all_to_all | solution.py:32
  247.9 2.6 scatter_custom_fusion.1
  258.7 2.5 multiply_add_fusion.1
  261.3 2.6 collective-permute-start.26
  263.9 3.0 collective-permute-start.27
  266.9 2.2 collective-permute-start.24
  270.5 3.4 %collective-permute-done.25 = f32[32,1,128]{2,0,1:T(8,128)S(1)} collective-permute-done((f32[32,1,128]{2,0,1:T(8,128)S(1)}, f32[32,1,128]{2,0,1:T(8,128)S(1)}, u32[]{:S(2)}, u32[]{:S(2)}) %collective-permute-start.25) | collective-permute-done | bytes 16416 | tf_op jit(solution)/shard_map/ppermute | solution.py:107
  274.5 3.3 %multiply_reduce_fusion = (f32[]{:T(128)}, f32[32,32,128]{2,0,1:T(8,128)}) fusion(f32[32,32,128]{2,0,1:T(8,128)S(1)} %multiply_add_fusion.1, f32[34,34,130]{2,0,1:T(8,128)S(1)} %select_maximum_fusion, f32[32,1,128]{2,0,1:T(8,128)S(1)} %collective-permute-done.24, f32[32,1,128]{2,0,1:T(8,128)S(1)} %collective-permute-done.25, f32[1,34,128]{2,0,1:T(1,128)S(1)} %pad.90, ...), kind=kLoop, calls=%fused_computation.106 | loop fusion | flops 4456447 | bytes 5314564 | tf_op jit(solution)/shard_map/reduce_sum | solution.py:190
  278.5 16.1 %all_to_all.49 = f32[16,1,1]{2,1,0:T(1,128)S(1)} all-to-all(f32[16,1,1]{2,1,0:T(1,128)S(1)} %broadcast_in_dim.25), channel_id=1, replica_groups=mesh['gx'=32,'gy'=16] {'gy'}, dimensions={0} | all-to-all | bytes 128 | tf_op jit(solution)/shard_map/all_to_all | solution.py:32
  295.9 12.5 %all_to_all.50 = f32[32,1,1]{2,1,0:T(1,128)S(1)} all-to-all(f32[32,1,1]{2,1,0:T(1,128)S(1)} %broadcast_in_dim.26), channel_id=1, replica_groups=mesh['gx'=32,'gy'=16] {'gx'}, dimensions={0} | all-to-all | bytes 256 | tf_op jit(solution)/shard_map/all_to_all | solution.py:32
  (229 shorter events, 87.0 us)
Async XLA Ops:
  0.6 114.7 %copy-start = (bf16[512,512]{1,0:T(8,128)(2,1)S(1)}, bf16[512,512]{1,0:T(8,128)(2,1)}, u32[]{:S(2)}) copy-start(bf16[512,512]{1,0:T(8,128)(2,1)} %param.55) | copy-start | bytes 1572868
  0.6 19.0 %copy-start.27 = (s32[3]{0:T(128)S(1)}, s32[3]{0:T(128)}, u32[]{:S(2)}) copy-start(s32[3]{0:T(128)} %constant.623.clone.1) | copy-start | bytes 40
  3.0 17.4 %collective-permute-start = (f32[1,32,128]{2,0,1:T(1,128)S(1)}, f32[1,32,128]{2,0,1:T(1,128)S(1)}, u32[]{:S(2)}, u32[]{:S(2)}) collective-permute-start(f32[1,32,128]{2,0,1:T(1,128)S(1)} %get-tuple-element.354), channel_id=1, source_target_pairs={{0,16},{16,32},{32,48},{48,64},{64,80},{80,96},{96,112},{112,128},... | collective-permute-start | bytes 49160 | tf_op jit(solution)/shard_map/ppermute | solution.py:17
  7.5 12.8 %collective-permute-start.1 = (f32[1,32,128]{2,0,1:T(1,128)S(1)}, f32[1,32,128]{2,0,1:T(1,128)S(1)}, u32[]{:S(2)}, u32[]{:S(2)}) collective-permute-start(f32[1,32,128]{2,0,1:T(1,128)S(1)} %get-tuple-element.355), channel_id=1, source_target_pairs={{16,0},{32,16},{48,32},{64,48},{80,64},{96,80},{112,96},{128,112},... | collective-permute-start | bytes 49160 | tf_op jit(solution)/shard_map/ppermute | solution.py:19
  13.9 91.7 %collective-permute-start.8 = (f32[1,32,128]{2,0,1:T(1,128)}, f32[1,32,128]{2,0,1:T(1,128)}, u32[]{:S(2)}, u32[]{:S(2)}) collective-permute-start(f32[1,32,128]{2,0,1:T(1,128)} %get-tuple-element.348), channel_id=1, source_target_pairs={{0,16},{16,32},{32,48},{48,64},{64,80},{80,96},{96,112},{112,128},... | collective-permute-start | bytes 49160 | tf_op jit(solution)/shard_map/ppermute | solution.py:17
  15.8 89.8 %collective-permute-start.9 = (f32[1,32,128]{2,0,1:T(1,128)}, f32[1,32,128]{2,0,1:T(1,128)}, u32[]{:S(2)}, u32[]{:S(2)}) collective-permute-start(f32[1,32,128]{2,0,1:T(1,128)} %get-tuple-element.349), channel_id=1, source_target_pairs={{16,0},{32,16},{48,32},{64,48},{80,64},{96,80},{112,96},{128,112},... | collective-permute-start | bytes 49160 | tf_op jit(solution)/shard_map/ppermute | solution.py:19
  18.8 11.2 %copy-start.12 = (f32[34]{0:T(128)}, f32[34]{0:T(128)S(1)}, u32[]{:S(2)}) copy-start(f32[34]{0:T(128)S(1)} %broadcast_multiply_fusion.1) | copy-start | bytes 412
  18.8 9.3 %copy-start.28 = (f32[128]{0:T(128)}, f32[128]{0:T(128)S(1)}, u32[]{:S(2)}) copy-start(f32[128]{0:T(128)S(1)} %get-tuple-element.368) | copy-start | bytes 1540
  18.8 12.1 %copy-start.22 = (f32[128]{0:T(128)}, f32[128]{0:T(128)S(1)}, u32[]{:S(2)}) copy-start(f32[128]{0:T(128)S(1)} %get-tuple-element.369) | copy-start | bytes 1540
  19.0 9.2 %copy-start.10 = (f32[34,34]{1,0:T(8,128)}, f32[34,34]{1,0:T(8,128)S(1)}, u32[]{:S(2)}) copy-start(f32[34,34]{1,0:T(8,128)S(1)} %broadcast_add_fusion) | copy-start | bytes 13876
  20.3 9.7 %copy-start.14 = (f32[34]{0:T(128)}, f32[34]{0:T(128)S(1)}, u32[]{:S(2)}) copy-start(f32[34]{0:T(128)S(1)} %iota_add_fusion.1) | copy-start | bytes 412
  20.4 2.7 collective-permute-start.2
  21.7 4.7 %collective-permute-start.3 = (f32[34,1,128]{2,0,1:T(8,128)S(1)}, f32[34,1,128]{2,0,1:T(8,128)S(1)}, u32[]{:S(2)}, u32[]{:S(2)}) collective-permute-start(f32[34,1,128]{2,0,1:T(8,128)S(1)} %get-tuple-element.341), channel_id=1, source_target_pairs={{1,0},{2,1},{3,2},{4,3},{5,4},{6,5},{7,6},{8,7},{9,8},{10,9},{11,1... | collective-permute-start | bytes 52232 | tf_op jit(solution)/shard_map/ppermute | solution.py:19
  23.1 12.3 %copy-start.18 = (f32[32]{0:T(128)}, f32[32]{0:T(128)S(1)}, u32[]{:S(2)}) copy-start(f32[32]{0:T(128)S(1)} %pad.174.clone) | copy-start | bytes 388
  31.9 14.4 %copy-start.3 = (f32[34,34,128]{2,1,0:T(8,128)}, f32[34,34,128]{2,1,0:T(8,128)S(1)}, u32[]{:S(2)}) copy-start(f32[34,34,128]{2,1,0:T(8,128)S(1)} %fusion.58) | copy-start | bytes 1775620
  38.0 8.8 %collective-permute-start.4 = (f32[3,1,32,128]{3,2,1,0:T(8,128)}, f32[3,1,32,128]{3,2,1,0:T(8,128)S(1)}, u32[]{:S(2)}, u32[]{:S(2)}) collective-permute-start(f32[3,1,32,128]{3,2,1,0:T(8,128)} %get-tuple-element.321), channel_id=1, source_target_pairs={{0,16},{16,32},{32,48},{48,64},{64,80},{80,96},{96,112},{112,128},... | collective-permute-start | bytes 147464 | tf_op jit(solution)/shard_map/ppermute | solution.py:17
  42.2 5.7 %collective-permute-start.5 = (f32[3,1,32,128]{3,2,1,0:T(8,128)}, f32[3,1,32,128]{3,2,1,0:T(8,128)}, u32[]{:S(2)}, u32[]{:S(2)}) collective-permute-start(f32[3,1,32,128]{3,2,1,0:T(8,128)} %get-tuple-element.320), channel_id=1, source_target_pairs={{16,0},{32,16},{48,32},{64,48},{80,64},{96,80},{112,96},{128,112},... | collective-permute-start | bytes 147464 | tf_op jit(solution)/shard_map/ppermute | solution.py:19
  46.4 17.1 %copy-start.1 = (f32[32,32,128]{2,1,0:T(8,128)S(1)}, f32[32,32,128]{2,1,0:T(8,128)}, u32[]{:S(2)}) copy-start(f32[32,32,128]{2,1,0:T(8,128)} %param.52) | copy-start | bytes 1572868
  48.7 6.5 %collective-permute-start.6 = (f32[3,34,1,128]{3,1,2,0:T(8,128)S(1)}, f32[3,34,1,128]{3,1,2,0:T(8,128)S(1)}, u32[]{:S(2)}, u32[]{:S(2)}) collective-permute-start(f32[3,34,1,128]{3,1,2,0:T(8,128)S(1)} %get-tuple-element.317), channel_id=1, source_target_pairs={{0,1},{1,2},{2,3},{3,4},{4,5},{5,6},{6,7},{7,8},{8,9},{9,10},{10,1... | collective-permute-start | bytes 156680 | tf_op jit(solution)/shard_map/ppermute | solution.py:17
  53.9 6.3 %collective-permute-start.7 = (f32[3,34,1,128]{3,1,2,0:T(8,128)S(1)}, f32[3,34,1,128]{3,1,2,0:T(8,128)S(1)}, u32[]{:S(2)}, u32[]{:S(2)}) collective-permute-start(f32[3,34,1,128]{3,1,2,0:T(8,128)S(1)} %get-tuple-element.316), channel_id=1, source_target_pairs={{1,0},{2,1},{3,2},{4,3},{5,4},{6,5},{7,6},{8,7},{9,8},{10,9},{11,1... | collective-permute-start | bytes 156680 | tf_op jit(solution)/shard_map/ppermute | solution.py:19
  66.5 24.3 %all-to-all-start = ((f32[16,1,2]{2,1,0:T(1,128)}), f32[16,1,2]{2,1,0:T(1,128)S(1)}, u32[]{:S(2)}, u32[]{:S(2)}) async-start(f32[16,1,2]{2,1,0:T(1,128)} %broadcast_in_dim.18), calls=%async_computation | async-start | bytes 16384 | tf_op jit(solution)/shard_map/all_to_all | solution.py:32
  92.8 19.7 %all-to-all-start.1 = ((f32[32,1,17]{2,1,0:T(1,128)}), f32[32,1,17]{2,1,0:T(1,128)S(1)}, u32[]{:S(2)}, u32[]{:S(2)}) async-start(f32[32,1,17]{2,1,0:T(1,128)} %broadcast_in_dim.19), calls=%async_computation.1 | async-start | bytes 32768 | tf_op jit(solution)/shard_map/all_to_all | solution.py:32
  106.3 18.9 %collective-permute-start.10 = (f32[34,1,128]{2,0,1:T(8,128)S(1)}, f32[34,1,128]{2,0,1:T(8,128)S(1)}, u32[]{:S(2)}, u32[]{:S(2)}) collective-permute-start(f32[34,1,128]{2,0,1:T(8,128)S(1)} %get-tuple-element.338), channel_id=1, source_target_pairs={{0,1},{1,2},{2,3},{3,4},{4,5},{5,6},{6,7},{7,8},{8,9},{9,10},{10,1... | collective-permute-start | bytes 52232 | tf_op jit(solution)/shard_map/ppermute | solution.py:17
  108.5 18.0 %collective-permute-start.11 = (f32[34,1,128]{2,0,1:T(8,128)S(1)}, f32[34,1,128]{2,0,1:T(8,128)}, u32[]{:S(2)}, u32[]{:S(2)}) collective-permute-start(f32[34,1,128]{2,0,1:T(8,128)S(1)} %get-tuple-element.339), channel_id=1, source_target_pairs={{1,0},{2,1},{3,2},{4,3},{5,4},{6,5},{7,6},{8,7},{9,8},{10,9},{11,1... | collective-permute-start | bytes 52232 | tf_op jit(solution)/shard_map/ppermute | solution.py:19
  115.3 11.2 %copy-start.16 = (f32[512]{0:T(512)}, f32[512]{0:T(512)S(1)}, u32[]{:S(2)}) copy-start(f32[512]{0:T(512)S(1)} %scatter_custom_fusion) | copy-start | bytes 6148
  115.8 10.7 %copy-start.19 = (f32[1,512]{1,0:T(1,128)}, f32[1,512]{1,0:T(1,128)S(1)}, u32[]{:S(2)}) copy-start(f32[1,512]{1,0:T(1,128)S(1)} %fusion.182) | copy-start | bytes 6148
  117.4 10.5 %collective-permute-start.14 = (f32[1,32,128]{2,0,1:T(1,128)S(1)}, f32[1,32,128]{2,0,1:T(1,128)S(1)}, u32[]{:S(2)}, u32[]{:S(2)}) collective-permute-start(f32[1,32,128]{2,0,1:T(1,128)S(1)} %get-tuple-element.353), channel_id=1, source_target_pairs={{16,0},{32,16},{48,32},{64,48},{80,64},{96,80},{112,96},{128,112},... | collective-permute-start | bytes 49160 | tf_op jit(solution)/shard_map/ppermute | solution.py:105
  119.9 7.9 %collective-permute-start.15 = (f32[1,32,128]{2,0,1:T(1,128)S(1)}, f32[1,32,128]{2,0,1:T(1,128)S(1)}, u32[]{:S(2)}, u32[]{:S(2)}) collective-permute-start(f32[1,32,128]{2,0,1:T(1,128)S(1)} %get-tuple-element.352), channel_id=1, source_target_pairs={{0,16},{16,32},{32,48},{48,64},{64,80},{80,96},{96,112},{112,128},... | collective-permute-start | bytes 49160 | tf_op jit(solution)/shard_map/ppermute | solution.py:104
  122.9 5.0 %collective-permute-start.12 = (f32[32,1,128]{2,0,1:T(8,128)S(1)}, f32[32,1,128]{2,0,1:T(8,128)S(1)}, u32[]{:S(2)}, u32[]{:S(2)}) collective-permute-start(f32[32,1,128]{2,0,1:T(8,128)S(1)} %get-tuple-element.350), channel_id=1, source_target_pairs={{0,1},{1,2},{2,3},{3,4},{4,5},{5,6},{6,7},{7,8},{8,9},{9,10},{10,1... | collective-permute-start | bytes 49160 | tf_op jit(solution)/shard_map/ppermute | solution.py:106
  125.2 4.8 %collective-permute-start.13 = (f32[32,1,128]{2,0,1:T(8,128)S(1)}, f32[32,1,128]{2,0,1:T(8,128)S(1)}, u32[]{:S(2)}, u32[]{:S(2)}) collective-permute-start(f32[32,1,128]{2,0,1:T(8,128)S(1)} %get-tuple-element.351), channel_id=1, source_target_pairs={{1,0},{2,1},{3,2},{4,3},{5,4},{6,5},{7,6},{8,7},{9,8},{10,9},{11,1... | collective-permute-start | bytes 49160 | tf_op jit(solution)/shard_map/ppermute | solution.py:107
  133.1 15.1 %copy-start.13 = (f32[34]{0:T(128)S(1)}, f32[34]{0:T(128)}, u32[]{:S(2)}) copy-start(f32[34]{0:T(128)} %copy-done.12) | copy-start | bytes 412
  133.1 15.1 %copy-start.15 = (f32[34]{0:T(128)S(1)}, f32[34]{0:T(128)}, u32[]{:S(2)}) copy-start(f32[34]{0:T(128)} %copy-done.14) | copy-start | bytes 412
  133.4 5.1 %collective-permute-start.16 = (f32[1,32,128]{2,0,1:T(1,128)S(1)}, f32[1,32,128]{2,0,1:T(1,128)S(1)}, u32[]{:S(2)}, u32[]{:S(2)}) collective-permute-start(f32[1,32,128]{2,0,1:T(1,128)S(1)} %get-tuple-element.346), channel_id=1, source_target_pairs={{0,16},{16,32},{32,48},{48,64},{64,80},{80,96},{96,112},{112,128},... | collective-permute-start | bytes 49160 | tf_op jit(solution)/shard_map/ppermute | solution.py:17
  136.5 5.1 %collective-permute-start.17 = (f32[1,32,128]{2,0,1:T(1,128)S(1)}, f32[1,32,128]{2,0,1:T(1,128)S(1)}, u32[]{:S(2)}, u32[]{:S(2)}) collective-permute-start(f32[1,32,128]{2,0,1:T(1,128)S(1)} %get-tuple-element.347), channel_id=1, source_target_pairs={{16,0},{32,16},{48,32},{64,48},{80,64},{96,80},{112,96},{128,112},... | collective-permute-start | bytes 49160 | tf_op jit(solution)/shard_map/ppermute | solution.py:19
  141.6 3.5 %collective-permute-start.18 = (f32[34,1,128]{2,0,1:T(8,128)S(1)}, f32[34,1,128]{2,0,1:T(8,128)S(1)}, u32[]{:S(2)}, u32[]{:S(2)}) collective-permute-start(f32[34,1,128]{2,0,1:T(8,128)S(1)} %get-tuple-element.336), channel_id=1, source_target_pairs={{0,1},{1,2},{2,3},{3,4},{4,5},{5,6},{6,7},{7,8},{8,9},{9,10},{10,1... | collective-permute-start | bytes 52232 | tf_op jit(solution)/shard_map/ppermute | solution.py:17
  143.7 4.5 %collective-permute-start.19 = (f32[34,1,128]{2,0,1:T(8,128)S(1)}, f32[34,1,128]{2,0,1:T(8,128)S(1)}, u32[]{:S(2)}, u32[]{:S(2)}) collective-permute-start(f32[34,1,128]{2,0,1:T(8,128)S(1)} %get-tuple-element.337), channel_id=1, source_target_pairs={{1,0},{2,1},{3,2},{4,3},{5,4},{6,5},{7,6},{8,7},{9,8},{10,9},{11,1... | collective-permute-start | bytes 52232 | tf_op jit(solution)/shard_map/ppermute | solution.py:19
  164.4 7.5 %collective-permute-start.20 = (f32[3,1,32,128]{3,2,1,0:T(8,128)S(1)}, f32[3,1,32,128]{3,2,1,0:T(8,128)S(1)}, u32[]{:S(2)}, u32[]{:S(2)}) collective-permute-start(f32[3,1,32,128]{3,2,1,0:T(8,128)S(1)} %get-tuple-element.319), channel_id=1, source_target_pairs={{0,16},{16,32},{32,48},{48,64},{64,80},{80,96},{96,112},{112,128},... | collective-permute-start | bytes 147464 | tf_op jit(solution)/shard_map/ppermute | solution.py:17
  167.8 5.5 %collective-permute-start.21 = (f32[3,1,32,128]{3,2,1,0:T(8,128)S(1)}, f32[3,1,32,128]{3,2,1,0:T(8,128)S(1)}, u32[]{:S(2)}, u32[]{:S(2)}) collective-permute-start(f32[3,1,32,128]{3,2,1,0:T(8,128)S(1)} %get-tuple-element.318), channel_id=1, source_target_pairs={{16,0},{32,16},{48,32},{64,48},{80,64},{96,80},{112,96},{128,112},... | collective-permute-start | bytes 147464 | tf_op jit(solution)/shard_map/ppermute | solution.py:19
  174.0 10.2 %collective-permute-start.22 = (f32[3,34,1,128]{3,1,2,0:T(8,128)}, f32[3,34,1,128]{3,1,2,0:T(8,128)}, u32[]{:S(2)}, u32[]{:S(2)}) collective-permute-start(f32[3,34,1,128]{3,1,2,0:T(8,128)} %get-tuple-element.315), channel_id=1, source_target_pairs={{0,1},{1,2},{2,3},{3,4},{4,5},{5,6},{6,7},{7,8},{8,9},{9,10},{10,1... | collective-permute-start | bytes 156680 | tf_op jit(solution)/shard_map/ppermute | solution.py:17
  182.7 5.7 %collective-permute-start.23 = (f32[3,34,1,128]{3,1,2,0:T(8,128)}, f32[3,34,1,128]{3,1,2,0:T(8,128)S(1)}, u32[]{:S(2)}, u32[]{:S(2)}) collective-permute-start(f32[3,34,1,128]{3,1,2,0:T(8,128)} %get-tuple-element.314), channel_id=1, source_target_pairs={{1,0},{2,1},{3,2},{4,3},{5,4},{6,5},{7,6},{8,7},{9,8},{10,9},{11,1... | collective-permute-start | bytes 156680 | tf_op jit(solution)/shard_map/ppermute | solution.py:19
  204.0 47.7 %copy-start.17 = (f32[512]{0:T(512)S(1)}, f32[512]{0:T(512)}, u32[]{:S(2)}) copy-start(f32[512]{0:T(512)} %copy-done.16) | copy-start | bytes 6148
  204.0 47.7 %copy-start.20 = (f32[1,512]{1,0:T(1,128)S(1)}, f32[1,512]{1,0:T(1,128)}, u32[]{:S(2)}) copy-start(f32[1,512]{1,0:T(1,128)} %copy-done.19) | copy-start | bytes 6148
  228.7 19.1 %all-to-all-start.3 = ((f32[32,1,20]{2,1,0:T(1,128)}), f32[32,1,20]{2,1,0:T(1,128)S(1)}, u32[]{:S(2)}, u32[]{:S(2)}) async-start(f32[32,1,20]{2,1,0:T(1,128)} %broadcast_in_dim.24), calls=%async_computation.3 | async-start | bytes 32768 | tf_op jit(solution)/shard_map/all_to_all | solution.py:32
  261.3 9.1 %collective-permute-start.26 = (f32[1,32,128]{2,0,1:T(1,128)S(1)}, f32[1,32,128]{2,0,1:T(1,128)S(1)}, u32[]{:S(2)}, u32[]{:S(2)}) collective-permute-start(f32[1,32,128]{2,0,1:T(1,128)S(1)} %get-tuple-element.345), channel_id=1, source_target_pairs={{16,0},{32,16},{48,32},{64,48},{80,64},{96,80},{112,96},{128,112},... | collective-permute-start | bytes 49160 | tf_op jit(solution)/shard_map/ppermute | solution.py:105
  263.9 6.6 %collective-permute-start.27 = (f32[1,32,128]{2,0,1:T(1,128)S(1)}, f32[1,32,128]{2,0,1:T(1,128)S(1)}, u32[]{:S(2)}, u32[]{:S(2)}) collective-permute-start(f32[1,32,128]{2,0,1:T(1,128)S(1)} %get-tuple-element.344), channel_id=1, source_target_pairs={{0,16},{16,32},{32,48},{48,64},{64,80},{80,96},{96,112},{112,128},... | collective-permute-start | bytes 49160 | tf_op jit(solution)/shard_map/ppermute | solution.py:104
  266.9 3.6 %collective-permute-start.24 = (f32[32,1,128]{2,0,1:T(8,128)S(1)}, f32[32,1,128]{2,0,1:T(8,128)S(1)}, u32[]{:S(2)}, u32[]{:S(2)}) collective-permute-start(f32[32,1,128]{2,0,1:T(8,128)S(1)} %get-tuple-element.342), channel_id=1, source_target_pairs={{0,1},{1,2},{2,3},{3,4},{4,5},{5,6},{6,7},{7,8},{8,9},{9,10},{10,1... | collective-permute-start | bytes 49160 | tf_op jit(solution)/shard_map/ppermute | solution.py:106
  269.1 4.8 %collective-permute-start.25 = (f32[32,1,128]{2,0,1:T(8,128)S(1)}, f32[32,1,128]{2,0,1:T(8,128)S(1)}, u32[]{:S(2)}, u32[]{:S(2)}) collective-permute-start(f32[32,1,128]{2,0,1:T(8,128)S(1)} %get-tuple-element.343), channel_id=1, source_target_pairs={{1,0},{2,1},{3,2},{4,3},{5,4},{6,5},{7,6},{8,7},{9,8},{10,9},{11,1... | collective-permute-start | bytes 49160 | tf_op jit(solution)/shard_map/ppermute | solution.py:107
  277.7 32.8 %copy-start.2 = (f32[32,32,128]{2,1,0:T(8,128)S(1)}, f32[32,32,128]{2,1,0:T(8,128)}, u32[]{:S(2)}) copy-start(f32[32,32,128]{2,1,0:T(8,128)} %param.52) | copy-start | bytes 1572868
  (13 other events, 53.2 us)

commit v3 on v2

--- a/solution.py
+++ b/solution.py
@@ -73,25 +73,25 @@
 
 
 def margin_sum(block):
-    core = block[1:-1, 1:-1]
-    rows_x = core.shape[0]
-    rows_y = core.shape[1]
-    depth = core.shape[2]
-    face_x = jnp.concatenate(
-        [block[0:1, 1:-1], jnp.zeros((rows_x - 2, rows_y, depth), jnp.float32), block[-1:, 1:-1]], 0
-    )
-    face_y = jnp.concatenate(
-        [block[1:-1, 0:1], jnp.zeros((rows_x, rows_y - 2, depth), jnp.float32), block[1:-1, -1:]], 1
-    )
-    corner = jnp.zeros_like(core)
-    corner = corner.at[0, 0].set(block[0, 0]).at[0, -1].set(block[0, -1])
-    corner = corner.at[-1, 0].set(block[-1, 0]).at[-1, -1].set(block[-1, -1])
-    arrived = with_halo(jnp.stack([face_x, face_y, corner]), (("gx", 1), ("gy", 2)), 1)
-    result = core.at[0].add(arrived[0, 0, 1:-1]).at[-1].add(arrived[0, -1, 1:-1])
-    result = result.at[:, 0].add(arrived[1, 1:-1, 0]).at[:, -1].add(arrived[1, 1:-1, -1])
-    result = result.at[0, 0].add(arrived[2, 0, 0]).at[0, -1].add(arrived[2, 0, -1])
-    result = result.at[-1, 0].add(arrived[2, -1, 0]).at[-1, -1].add(arrived[2, -1, -1])
-    return result
+    count_x = lax.axis_size("gx")
+    count_y = lax.axis_size("gy")
+    up_x = [(i, i + 1) for i in range(count_x - 1)]
+    down_x = [(i + 1, i) for i in range(count_x - 1)]
+    up_y = [(i, i + 1) for i in range(count_y - 1)]
+    down_y = [(i + 1, i) for i in range(count_y - 1)]
+    rows_x = block.shape[0] - 2
+    rows_y = block.shape[1] - 2
+    from_low = lax.ppermute(block[-1:], "gx", up_x)
+    from_high = lax.ppermute(block[:1], "gx", down_x)
+    body_rows = block[1:-1]
+    body_rows = body_rows + jnp.pad(from_low, ((0, rows_x - 1), (0, 0), (0, 0)))
+    body_rows = body_rows + jnp.pad(from_high, ((rows_x - 1, 0), (0, 0), (0, 0)))
+    from_left = lax.ppermute(body_rows[:, -1:], "gy", up_y)
+    from_right = lax.ppermute(body_rows[:, :1], "gy", down_y)
+    core = body_rows[:, 1:-1]
+    core = core + jnp.pad(from_left, ((0, 0), (0, rows_y - 1), (0, 0)))
+    core = core + jnp.pad(from_right, ((0, 0), (rows_y - 1, 0), (0, 0)))
+    return core
 
 
 def face_halo(cells):
@@ -118,7 +118,10 @@
     levels = jnp.arange(depth, dtype=jnp.int32)
     solid = (levels[None, None, :] < heights[:, :, None]).astype(jnp.float32)
     fluid = 1.0 - solid
-    solid_side = extend(solid)
+    residual = fluid * rhs
+    masked = residual * fluid
+    both_wide = extend(jnp.concatenate([masked, solid], axis=2))
+    solid_side = both_wide[:, :, depth:]
     bottom = jnp.ones((rows_x + 2, rows_y + 2, 1), jnp.float32)
     top = jnp.zeros((rows_x + 2, rows_y + 2, 1), jnp.float32)
     fluid_wide = 1.0 - jnp.concatenate([bottom, solid_side, top], 2)
@@ -133,8 +136,9 @@
     inverse = coarse_inverse.astype(jnp.float32)
     none = jnp.zeros((0,), jnp.float32)
 
-    def local_solve(masked):
-        wide = extend(masked)
+    def local_solve(masked, wide=None):
+        if wide is None:
+            wide = extend(masked)
         spectral = modal(wide, sine_x, sine_y, sine_z) * inv_eig
         return margin_sum(modal(spectral, sine_x, sine_y, sine_z))
 
@@ -150,9 +154,7 @@
             beside = beside + operate_weight * value
         return fluid * (count * direction - beside) + solid * direction
 
-    residual = fluid * rhs
-    masked = residual * fluid
-    local0 = local_solve(masked)
+    local0 = local_solve(masked, both_wide[:, :, :depth])
     every, partial = exchange(
         (jnp.sum(masked) / cells).reshape(1), jnp.sum(residual * fluid * local0).reshape(1)
     )

time: 316 us -> 261 us (0.83)
  local copies, waits for them, and re-layouts: 51.8 us -> 17.6 us
  blocking collectives: 47.1 us -> 74.1 us
  starting transfers between devices: 107 us -> 82.2 us
  other arithmetic: 42.9 us -> 24 us
    all_to_all x3 -> x4, blocking collectives: 47.1 us -> 74.1 us  [exchange(): lax.all_to_all(jnp.broadcast_to(stage[None], (count,) + stage.shape), axi...]
    ppermute x0 -> x8, starting transfers between devices: none -> 18.8 us  [the longest x2 6.52 us: margin_sum(): from_low = lax.ppermute(block[-1:], 'gx', up_x)]
    scatter-add x15 -> x0, local copies, waits for them, and re-layouts: 17.1 us -> none  [the longest x4 5.19 us: margin_sum(): result.at[0, 0].add(arrived[2, 0, 0]).at[0, -1].add(arrived[2, 0, -1])]
    ppermute x10 -> x4, starting transfers between devices: 30.2 us -> 14.2 us  [with_halo(): lax.ppermute(tail, axis, [(i, (i + 1) % count) for i in range(ends)])]
    all_to_all x3 -> x2, starting transfers between devices: 38.1 us -> 22.6 us  [exchange(): lax.all_to_all(jnp.broadcast_to(stage[None], (count,) + stage.shape), axi...]
    ppermute x0 -> x8, waiting for transfers between devices: none -> 13.9 us  [the longest x2 7.63 us: margin_sum(): from_right = lax.ppermute(body_rows[:, :1], 'gy', down_y)]
    another operation x10 -> x0, other arithmetic: 12 us -> none  [the longest x6 6.79 us: margin_sum(): jnp.stack([face_x, face_y, corner])]
    ppermute x10 -> x4, starting transfers between devices: 21 us -> 9.96 us  [with_halo(): lax.ppermute(head, axis, [((i + 1) % count, i) for i in range(ends)])]
  transfers between devices with their start and end apart: 31 -> 26, of which waited for: 11 -> 12; matrix products, arithmetic and copies ran while one was open for 14% -> 2% of each run, Pallas kernels for 0% -> 0%
where the time goes in v3:
time: 261 us; the launch traced here: 260 us
  starting transfers between devices  82.2 us (31%)
  blocking collectives  74.1 us (28%)
  waiting for transfers between devices  38.6 us (15%)
  other arithmetic  24 us (9%)
  local copies, waits for them, and re-layouts  17.6 us (7%)
  matrix products  11.9 us (5%)
  between operations  11.2 us (4%)
    all_to_all x4, blocking collectives, exchange(): lax.all_to_all(jnp.broadcast_to(stage[None], (count,) + stage.shape), axi...  74.1 us
    all_to_all x2, starting transfers between devices, exchange(): lax.all_to_all(jnp.broadcast_to(stage[None], (count,) + stage.shape), axi...  22.6 us
    ppermute x4, starting transfers between devices, with_halo(): lax.ppermute(tail, axis, [(i, (i + 1) % count) for i in range(ends)])  14.2 us
    ppermute x4, waiting for transfers between devices, with_halo(): lax.ppermute(head, axis, [((i + 1) % count, i) for i in range(ends)])  10.5 us
    ppermute x4, starting transfers between devices, with_halo(): lax.ppermute(head, axis, [((i + 1) % count, i) for i in range(ends)])  9.96 us
    all_to_all x2, waiting for transfers between devices, exchange(): lax.all_to_all(jnp.broadcast_to(stage[None], (count,) + stage.shape), axi...  8.64 us
    ppermute x2, waiting for transfers between devices, margin_sum(): from_right = lax.ppermute(body_rows[:, :1], 'gy', down_y)  7.63 us
    ppermute x2, starting transfers between devices, margin_sum(): from_low = lax.ppermute(block[-1:], 'gx', up_x)  6.52 us
  transfers between devices with their start and end apart: 26, of which 12 were waited for; matrix products, arithmetic and copies ran while one was open for 2% of the time, Pallas kernels for 0%

profile of v3, /device:TPU:1, one launch (start us, length us, event | category | flops | bytes accessed | tf_op | source)
XLA Modules:
  0.0 259.6 jit_solution(10715436559078918922)
XLA Ops:
  1.7 1.4 fusion.54
  3.2 4.6 %collective-permute-start = (f32[1,32,256]{2,0,1:T(1,128)S(1)}, f32[1,32,256]{2,0,1:T(1,128)S(1)}, u32[]{:S(2)}, u32[]{:S(2)}) collective-permute-start(f32[1,32,256]{2,0,1:T(1,128)S(1)} %get-tuple-element.24), channel_id=1, source_target_pairs={{0,16},{16,32},{32,48},{48,64},{64,80},{80,96},{96,112},{112,128},... | collective-permute-start | bytes 98312 | tf_op jit(solution)/shard_map/ppermute | solution.py:17
  7.8 5.5 %collective-permute-start.1 = (f32[1,32,256]{2,0,1:T(1,128)S(1)}, f32[1,32,256]{2,0,1:T(1,128)S(1)}, u32[]{:S(2)}, u32[]{:S(2)}) collective-permute-start(f32[1,32,256]{2,0,1:T(1,128)S(1)} %get-tuple-element.25), channel_id=1, source_target_pairs={{16,0},{32,16},{48,32},{64,48},{80,64},{96,80},{112,96},{128,112},... | collective-permute-start | bytes 98312 | tf_op jit(solution)/shard_map/ppermute | solution.py:19
  14.1 2.5 collective-permute-start.2
  17.9 3.6 %collective-permute-done.3 = f32[34,1,256]{2,0,1:T(8,128)S(1)} collective-permute-done((f32[34,1,256]{2,0,1:T(8,128)S(1)}, f32[34,1,256]{2,0,1:T(8,128)S(1)}, u32[]{:S(2)}, u32[]{:S(2)}) %collective-permute-start.3) | collective-permute-done | bytes 34848 | tf_op jit(solution)/shard_map/ppermute | solution.py:19
  27.3 3.2 %collective-permute-start.4 = (f32[1,34,128]{2,0,1:T(1,128)S(1)}, f32[1,34,128]{2,0,1:T(1,128)S(1)}, u32[]{:S(2)}, u32[]{:S(2)}) collective-permute-start(f32[1,34,128]{2,0,1:T(1,128)S(1)} %get-tuple-element.28), channel_id=1, source_target_pairs={{0,16},{16,32},{32,48},{48,64},{64,80},{80,96},{96,112},{112,128},... | collective-permute-start | bytes 52232 | tf_op jit(solution)/shard_map/ppermute | solution.py:84
  30.4 1.9 collective-permute-start.5
  32.4 3.1 %collective-permute-done.5 = f32[1,34,128]{2,0,1:T(1,128)S(1)} collective-permute-done((f32[1,34,128]{2,0,1:T(1,128)S(1)}, f32[1,34,128]{2,0,1:T(1,128)S(1)}, u32[]{:S(2)}, u32[]{:S(2)}) %collective-permute-start.5) | collective-permute-done | bytes 17440 | tf_op jit(solution)/shard_map/ppermute | solution.py:85
  35.6 3.5 %collective-permute-start.6 = (f32[32,1,128]{2,0,1:T(8,128)S(1)}, f32[32,1,128]{2,0,1:T(8,128)S(1)}, u32[]{:S(2)}, u32[]{:S(2)}) collective-permute-start(f32[32,1,128]{2,0,1:T(8,128)S(1)} %get-tuple-element.34), channel_id=1, source_target_pairs={{0,1},{1,2},{2,3},{3,4},{4,5},{5,6},{6,7},{7,8},{8,9},{9,10},{10,1... | collective-permute-start | bytes 49160 | tf_op jit(solution)/shard_map/ppermute | solution.py:89
  40.5 4.5 %collective-permute-done.7 = f32[32,1,128]{2,0,1:T(8,128)S(1)} collective-permute-done((f32[32,1,128]{2,0,1:T(8,128)S(1)}, f32[32,1,128]{2,0,1:T(8,128)S(1)}, u32[]{:S(2)}, u32[]{:S(2)}) %collective-permute-start.7) | collective-permute-done | bytes 16416 | tf_op jit(solution)/shard_map/ppermute | solution.py:90
  47.2 24.2 %all_to_all.48 = f32[16,1,2]{2,1,0:T(1,128)S(1)} all-to-all(f32[16,1,2]{2,1,0:T(1,128)S(1)} %broadcast_in_dim.18), channel_id=1, replica_groups=mesh['gx'=32,'gy'=16] {'gy'}, dimensions={0} | all-to-all | bytes 256 | tf_op jit(solution)/shard_map/all_to_all | solution.py:32
  73.4 10.5 %all-to-all-start.1 = ((f32[32,1,17]{2,1,0:T(1,128)}), f32[32,1,17]{2,1,0:T(1,128)S(1)}, u32[]{:S(2)}, u32[]{:S(2)}) async-start(f32[32,1,17]{2,1,0:T(1,128)} %broadcast_in_dim.19), calls=%async_computation.1 | async-start | bytes 32768 | tf_op jit(solution)/shard_map/all_to_all | solution.py:32
  87.6 3.2 %all-to-all-done.1 = f32[32,1,17]{2,1,0:T(1,128)S(1)} async-done(((f32[32,1,17]{2,1,0:T(1,128)}), f32[32,1,17]{2,1,0:T(1,128)S(1)}, u32[]{:S(2)}, u32[]{:S(2)}) %all-to-all-start.1) | async-done | bytes 2208 | tf_op jit(solution)/shard_map/all_to_all | solution.py:32
  90.9 2.4 scatter_custom_fusion
  95.4 2.7 %collective-permute-start.11 = (f32[1,32,128]{2,0,1:T(1,128)S(1)}, f32[1,32,128]{2,0,1:T(1,128)S(1)}, u32[]{:S(2)}, u32[]{:S(2)}) collective-permute-start(f32[1,32,128]{2,0,1:T(1,128)S(1)} %get-tuple-element.44), channel_id=1, source_target_pairs={{0,16},{16,32},{32,48},{48,64},{64,80},{80,96},{96,112},{112,128},... | collective-permute-start | bytes 49160 | tf_op jit(solution)/shard_map/ppermute | solution.py:104
  98.1 1.9 collective-permute-start.10
  100.0 2.2 collective-permute-start.8
  102.3 1.5 collective-permute-start.9
  104.3 2.5 collective-permute-done.9
  107.4 2.7 %multiply_reduce_fusion.4 = (f32[]{:T(128)}, f32[32,32,128]{2,0,1:T(8,128)S(1)}) fusion(f32[32,32,128]{2,0,1:T(8,128)S(1)} %add_multiply_fusion, f32[34,34,130]{2,0,1:T(8,128)S(1)} %select_maximum_fusion.4, f32[32,1,128]{2,0,1:T(8,128)S(1)} %collective-permute-done.8, f32[32,1,128]{2,0,1:T(8,128)S(1)} %collective-permute-done.9, f32[1,34,128]{2,0,1:T(1,128)S(1)} %pad.53, ...), kind=kLoop, calls=%fused_computation.106 | loop fusion | flops 4456447 | bytes 5314564 | tf_op jit(solution)/shard_map/reduce_sum | solution.py:173
  110.4 5.0 %collective-permute-start.12 = (f32[1,32,128]{2,0,1:T(1,128)S(1)}, f32[1,32,128]{2,0,1:T(1,128)S(1)}, u32[]{:S(2)}, u32[]{:S(2)}) collective-permute-start(f32[1,32,128]{2,0,1:T(1,128)S(1)} %get-tuple-element.40), channel_id=1, source_target_pairs={{0,16},{16,32},{32,48},{48,64},{64,80},{80,96},{96,112},{112,128},... | collective-permute-start | bytes 49160 | tf_op jit(solution)/shard_map/ppermute | solution.py:17
  115.4 1.9 collective-permute-start.13
  117.3 3.1 %collective-permute-done.13 = f32[1,32,128]{2,0,1:T(1,128)S(1)} collective-permute-done((f32[1,32,128]{2,0,1:T(1,128)S(1)}, f32[1,32,128]{2,0,1:T(1,128)S(1)}, u32[]{:S(2)}, u32[]{:S(2)}) %collective-permute-start.13) | collective-permute-done | bytes 16416 | tf_op jit(solution)/shard_map/ppermute | solution.py:19
  120.4 2.1 collective-permute-start.14
  122.6 1.3 collective-permute-start.15
  123.9 3.2 %collective-permute-done.15 = f32[34,1,128]{2,0,1:T(8,128)S(1)} collective-permute-done((f32[34,1,128]{2,0,1:T(8,128)S(1)}, f32[34,1,128]{2,0,1:T(8,128)S(1)}, u32[]{:S(2)}, u32[]{:S(2)}) %collective-permute-start.15) | collective-permute-done | bytes 17440 | tf_op jit(solution)/shard_map/ppermute | solution.py:19
  132.7 3.4 %collective-permute-start.16 = (f32[1,34,128]{2,0,1:T(1,128)S(1)}, f32[1,34,128]{2,0,1:T(1,128)S(1)}, u32[]{:S(2)}, u32[]{:S(2)}) collective-permute-start(f32[1,34,128]{2,0,1:T(1,128)S(1)} %get-tuple-element.26), channel_id=1, source_target_pairs={{0,16},{16,32},{32,48},{48,64},{64,80},{80,96},{96,112},{112,128},... | collective-permute-start | bytes 52232 | tf_op jit(solution)/shard_map/ppermute | solution.py:84
  136.1 1.9 collective-permute-start.17
  138.0 3.1 %collective-permute-done.17 = f32[1,34,128]{2,0,1:T(1,128)S(1)} collective-permute-done((f32[1,34,128]{2,0,1:T(1,128)S(1)}, f32[1,34,128]{2,0,1:T(1,128)S(1)}, u32[]{:S(2)}, u32[]{:S(2)}) %collective-permute-start.17) | collective-permute-done | bytes 17440 | tf_op jit(solution)/shard_map/ppermute | solution.py:85
  141.3 2.3 collective-permute-start.18
  144.9 3.2 %collective-permute-done.19 = f32[32,1,128]{2,0,1:T(8,128)S(1)} collective-permute-done((f32[32,1,128]{2,0,1:T(8,128)S(1)}, f32[32,1,128]{2,0,1:T(8,128)S(1)}, u32[]{:S(2)}, u32[]{:S(2)}) %collective-permute-start.19) | collective-permute-done | bytes 16416 | tf_op jit(solution)/shard_map/ppermute | solution.py:90
  149.8 2.7 %concatenate.80 = f32[5]{0:T(128)S(1)} concatenate(f32[1]{0:T(128)} %bitcast.14, f32[1]{0:T(128)} %bitcast.15, f32[1]{0:T(128)} %bitcast.18, f32[1]{0:T(128)} %bitcast.19, f32[1]{0:T(128)} %bitcast.20), dimensions={0} | concatenate | bytes 40 | tf_op jit(solution)/shard_map/concatenate | solution.py:29
  152.5 17.9 %all_to_all.49 = f32[16,1,5]{2,1,0:T(1,128)S(1)} all-to-all(f32[16,1,5]{2,1,0:T(1,128)S(1)} %broadcast_in_dim.23), channel_id=1, replica_groups=mesh['gx'=32,'gy'=16] {'gy'}, dimensions={0} | all-to-all | bytes 640 | tf_op jit(solution)/shard_map/all_to_all | solution.py:32
  171.3 12.0 %all-to-all-start.3 = ((f32[32,1,20]{2,1,0:T(1,128)}), f32[32,1,20]{2,1,0:T(1,128)S(1)}, u32[]{:S(2)}, u32[]{:S(2)}) async-start(f32[32,1,20]{2,1,0:T(1,128)} %broadcast_in_dim.24), calls=%async_computation.3 | async-start | bytes 32768 | tf_op jit(solution)/shard_map/all_to_all | solution.py:32
  183.4 1.5 slice_reduce_fusion.1
  184.9 5.4 %all-to-all-done.3 = f32[32,1,20]{2,1,0:T(1,128)S(1)} async-done(((f32[32,1,20]{2,1,0:T(1,128)}), f32[32,1,20]{2,1,0:T(1,128)S(1)}, u32[]{:S(2)}, u32[]{:S(2)}) %all-to-all-start.3) | async-done | bytes 2592 | tf_op jit(solution)/shard_map/all_to_all | solution.py:32
  190.4 2.6 scatter_custom_fusion.1
  194.1 1.3 multiply_reduce_fusion.6
  201.9 2.4 multiply_add_fusion.1
  204.4 2.7 %collective-permute-start.23 = (f32[1,32,128]{2,0,1:T(1,128)S(1)}, f32[1,32,128]{2,0,1:T(1,128)S(1)}, u32[]{:S(2)}, u32[]{:S(2)}) collective-permute-start(f32[1,32,128]{2,0,1:T(1,128)S(1)} %get-tuple-element.38), channel_id=1, source_target_pairs={{0,16},{16,32},{32,48},{48,64},{64,80},{80,96},{96,112},{112,128},... | collective-permute-start | bytes 49160 | tf_op jit(solution)/shard_map/ppermute | solution.py:104
  207.2 1.9 collective-permute-start.22
  209.1 2.2 collective-permute-start.20
  211.3 1.5 collective-permute-start.21
  212.9 3.0 %collective-permute-done.21 = f32[32,1,128]{2,0,1:T(8,128)S(1)} collective-permute-done((f32[32,1,128]{2,0,1:T(8,128)S(1)}, f32[32,1,128]{2,0,1:T(8,128)S(1)}, u32[]{:S(2)}, u32[]{:S(2)}) %collective-permute-start.21) | collective-permute-done | bytes 16416 | tf_op jit(solution)/shard_map/ppermute | solution.py:107
  216.5 3.3 %multiply_reduce_fusion = (f32[]{:T(128)}, f32[32,32,128]{2,0,1:T(8,128)}) fusion(f32[32,32,128]{2,0,1:T(8,128)S(1)} %multiply_add_fusion.1, f32[34,34,130]{2,0,1:T(8,128)S(1)} %select_maximum_fusion, f32[32,1,128]{2,0,1:T(8,128)S(1)} %collective-permute-done.20, f32[32,1,128]{2,0,1:T(8,128)S(1)} %collective-permute-done.21, f32[1,34,128]{2,0,1:T(1,128)S(1)} %pad.60, ...), kind=kLoop, calls=%fused_computation.101 | loop fusion | flops 4456447 | bytes 5314564 | tf_op jit(solution)/shard_map/reduce_sum | solution.py:192
  220.4 16.1 %all_to_all.50 = f32[16,1,1]{2,1,0:T(1,128)S(1)} all-to-all(f32[16,1,1]{2,1,0:T(1,128)S(1)} %broadcast_in_dim.25), channel_id=1, replica_groups=mesh['gx'=32,'gy'=16] {'gy'}, dimensions={0} | all-to-all | bytes 128 | tf_op jit(solution)/shard_map/all_to_all | solution.py:32
  237.8 15.9 %all_to_all.51 = f32[32,1,1]{2,1,0:T(1,128)S(1)} all-to-all(f32[32,1,1]{2,1,0:T(1,128)S(1)} %broadcast_in_dim.26), channel_id=1, replica_groups=mesh['gx'=32,'gy'=16] {'gx'}, dimensions={0} | all-to-all | bytes 256 | tf_op jit(solution)/shard_map/all_to_all | solution.py:32
  255.0 1.6 multiply_subtract_fusion
  (153 shorter events, 36.1 us)
Async XLA Ops:
  0.6 92.8 %copy-start = (bf16[512,512]{1,0:T(8,128)(2,1)S(1)}, bf16[512,512]{1,0:T(8,128)(2,1)}, u32[]{:S(2)}) copy-start(bf16[512,512]{1,0:T(8,128)(2,1)} %param.7) | copy-start | bytes 1572868
  3.2 10.3 %collective-permute-start = (f32[1,32,256]{2,0,1:T(1,128)S(1)}, f32[1,32,256]{2,0,1:T(1,128)S(1)}, u32[]{:S(2)}, u32[]{:S(2)}) collective-permute-start(f32[1,32,256]{2,0,1:T(1,128)S(1)} %get-tuple-element.24), channel_id=1, source_target_pairs={{0,16},{16,32},{32,48},{48,64},{64,80},{80,96},{96,112},{112,128},... | collective-permute-start | bytes 98312 | tf_op jit(solution)/shard_map/ppermute | solution.py:17
  7.8 6.3 %collective-permute-start.1 = (f32[1,32,256]{2,0,1:T(1,128)S(1)}, f32[1,32,256]{2,0,1:T(1,128)S(1)}, u32[]{:S(2)}, u32[]{:S(2)}) collective-permute-start(f32[1,32,256]{2,0,1:T(1,128)S(1)} %get-tuple-element.25), channel_id=1, source_target_pairs={{16,0},{32,16},{48,32},{64,48},{80,64},{96,80},{112,96},{128,112},... | collective-permute-start | bytes 98312 | tf_op jit(solution)/shard_map/ppermute | solution.py:19
  13.2 12.1 %copy-start.10 = (f32[34]{0:T(128)}, f32[34]{0:T(128)S(1)}, u32[]{:S(2)}) copy-start(f32[34]{0:T(128)S(1)} %broadcast_multiply_fusion.1) | copy-start | bytes 412
  13.3 10.1 %copy-start.26 = (f32[128]{0:T(128)}, f32[128]{0:T(128)S(1)}, u32[]{:S(2)}) copy-start(f32[128]{0:T(128)S(1)} %get-tuple-element.52) | copy-start | bytes 1540
  13.4 12.8 %copy-start.20 = (f32[128]{0:T(128)}, f32[128]{0:T(128)S(1)}, u32[]{:S(2)}) copy-start(f32[128]{0:T(128)S(1)} %get-tuple-element.53) | copy-start | bytes 1540
  13.4 10.0 %copy-start.14 = (f32[34,34]{1,0:T(8,128)}, f32[34,34]{1,0:T(8,128)S(1)}, u32[]{:S(2)}) copy-start(f32[34,34]{1,0:T(8,128)S(1)} %broadcast_add_fusion) | copy-start | bytes 13876
  13.5 11.9 %copy-start.12 = (f32[34]{0:T(128)}, f32[34]{0:T(128)S(1)}, u32[]{:S(2)}) copy-start(f32[34]{0:T(128)S(1)} %iota_add_fusion.1) | copy-start | bytes 412
  14.1 3.8 %collective-permute-start.2 = (f32[34,1,256]{2,0,1:T(8,128)S(1)}, f32[34,1,256]{2,0,1:T(8,128)S(1)}, u32[]{:S(2)}, u32[]{:S(2)}) collective-permute-start(f32[34,1,256]{2,0,1:T(8,128)S(1)} %get-tuple-element.22), channel_id=1, source_target_pairs={{0,1},{1,2},{2,3},{3,4},{4,5},{5,6},{6,7},{7,8},{8,9},{9,10},{10,1... | collective-permute-start | bytes 104456 | tf_op jit(solution)/shard_map/ppermute | solution.py:17
  16.6 4.9 %collective-permute-start.3 = (f32[34,1,256]{2,0,1:T(8,128)S(1)}, f32[34,1,256]{2,0,1:T(8,128)S(1)}, u32[]{:S(2)}, u32[]{:S(2)}) collective-permute-start(f32[34,1,256]{2,0,1:T(8,128)S(1)} %get-tuple-element.23), channel_id=1, source_target_pairs={{1,0},{2,1},{3,2},{4,3},{5,4},{6,5},{7,6},{8,7},{9,8},{10,9},{11,1... | collective-permute-start | bytes 104456 | tf_op jit(solution)/shard_map/ppermute | solution.py:19
  17.9 8.3 %copy-start.22 = (f32[128]{0:T(128)}, f32[128]{0:T(128)S(1)}, u32[]{:S(2)}) copy-start(f32[128]{0:T(128)S(1)} %broadcast_multiply_fusion) | copy-start | bytes 1540
  21.7 65.9 %copy-start.2 = (f32[34,34,256]{2,0,1:T(8,128)}, f32[34,34,256]{2,0,1:T(8,128)S(1)}, u32[]{:S(2)}) copy-start(f32[34,34,256]{2,0,1:T(8,128)S(1)} %pad_maximum_fusion) | copy-start | bytes 3551236
  26.2 18.7 %copy-start.1 = (f32[32,32,128]{2,1,0:T(8,128)S(1)}, f32[32,32,128]{2,1,0:T(8,128)}, u32[]{:S(2)}) copy-start(f32[32,32,128]{2,1,0:T(8,128)} %param.4) | copy-start | bytes 1572868
  27.2 56.7 %copy-start.24 = (s32[512]{0:T(512)S(1)}, s32[512]{0:T(512)}, u32[]{:S(2)}) copy-start(s32[512]{0:T(512)} %param.6) | copy-start | bytes 6148
  27.3 5.1 %collective-permute-start.4 = (f32[1,34,128]{2,0,1:T(1,128)S(1)}, f32[1,34,128]{2,0,1:T(1,128)S(1)}, u32[]{:S(2)}, u32[]{:S(2)}) collective-permute-start(f32[1,34,128]{2,0,1:T(1,128)S(1)} %get-tuple-element.28), channel_id=1, source_target_pairs={{0,16},{16,32},{32,48},{48,64},{64,80},{80,96},{96,112},{112,128},... | collective-permute-start | bytes 52232 | tf_op jit(solution)/shard_map/ppermute | solution.py:84
  30.4 5.1 %collective-permute-start.5 = (f32[1,34,128]{2,0,1:T(1,128)S(1)}, f32[1,34,128]{2,0,1:T(1,128)S(1)}, u32[]{:S(2)}, u32[]{:S(2)}) collective-permute-start(f32[1,34,128]{2,0,1:T(1,128)S(1)} %get-tuple-element.29), channel_id=1, source_target_pairs={{16,0},{32,16},{48,32},{64,48},{80,64},{96,80},{112,96},{128,112},... | collective-permute-start | bytes 52232 | tf_op jit(solution)/shard_map/ppermute | solution.py:85
  35.6 4.9 %collective-permute-start.6 = (f32[32,1,128]{2,0,1:T(8,128)S(1)}, f32[32,1,128]{2,0,1:T(8,128)S(1)}, u32[]{:S(2)}, u32[]{:S(2)}) collective-permute-start(f32[32,1,128]{2,0,1:T(8,128)S(1)} %get-tuple-element.34), channel_id=1, source_target_pairs={{0,1},{1,2},{2,3},{3,4},{4,5},{5,6},{6,7},{7,8},{8,9},{9,10},{10,1... | collective-permute-start | bytes 49160 | tf_op jit(solution)/shard_map/ppermute | solution.py:89
  39.2 5.8 %collective-permute-start.7 = (f32[32,1,128]{2,0,1:T(8,128)S(1)}, f32[32,1,128]{2,0,1:T(8,128)S(1)}, u32[]{:S(2)}, u32[]{:S(2)}) collective-permute-start(f32[32,1,128]{2,0,1:T(8,128)S(1)} %get-tuple-element.35), channel_id=1, source_target_pairs={{1,0},{2,1},{3,2},{4,3},{5,4},{6,5},{7,6},{8,7},{9,8},{10,9},{11,1... | collective-permute-start | bytes 49160 | tf_op jit(solution)/shard_map/ppermute | solution.py:90
  45.0 49.6 %copy-start.4 = (f32[32,1,128]{2,0,1:T(8,128)}, f32[32,1,128]{2,0,1:T(8,128)S(1)}, u32[]{:S(2)}) copy-start(f32[32,1,128]{2,0,1:T(8,128)S(1)} %collective-permute-done.7) | copy-start | bytes 49156
  73.4 17.4 %all-to-all-start.1 = ((f32[32,1,17]{2,1,0:T(1,128)}), f32[32,1,17]{2,1,0:T(1,128)S(1)}, u32[]{:S(2)}, u32[]{:S(2)}) async-start(f32[32,1,17]{2,1,0:T(1,128)} %broadcast_in_dim.19), calls=%async_computation.1 | async-start | bytes 32768 | tf_op jit(solution)/shard_map/all_to_all | solution.py:32
  84.0 11.3 %copy-start.25 = (s32[512]{0:T(512)}, s32[512]{0:T(512)S(1)}, u32[]{:S(2)}) copy-start(s32[512]{0:T(512)S(1)} %compare_select_fusion) | copy-start | bytes 6148
  87.6 16.2 %copy-start.18 = (f32[130]{0:T(256)S(1)}, f32[130]{0:T(256)}, u32[]{:S(2)}) copy-start(f32[130]{0:T(256)} %pad.106.clone) | copy-start | bytes 1564
  87.6 16.2 %copy-start.19 = (f32[130]{0:T(256)S(1)}, f32[130]{0:T(256)}, u32[]{:S(2)}) copy-start(f32[130]{0:T(256)} %pad.108.clone) | copy-start | bytes 1564
  90.9 11.4 %copy-start.7 = (f32[32,1,17]{2,1,0:T(1,128)}, f32[32,1,17]{2,1,0:T(1,128)S(1)}, u32[]{:S(2)}) copy-start(f32[32,1,17]{2,1,0:T(1,128)S(1)} %all-to-all-done.1) | copy-start | bytes 6532
  93.4 8.9 %copy-start.16 = (f32[512]{0:T(512)}, f32[512]{0:T(512)S(1)}, u32[]{:S(2)}) copy-start(f32[512]{0:T(512)S(1)} %scatter_custom_fusion) | copy-start | bytes 6148
  93.4 10.4 %slice-start = ((f32[34,34,256]{2,0,1:T(8,128)}), f32[34,34,128]{2,0,1:T(8,128)S(1)}, s32[]{:S(2)}) async-start(f32[34,34,256]{2,0,1:T(8,128)} %copy-done.2), calls=%async_computation.6 | async-start | bytes 1392640 | tf_op jit(solution)/shard_map/slice | solution.py:124
  93.9 8.4 %copy-start.17 = (f32[1,512]{1,0:T(1,128)}, f32[1,512]{1,0:T(1,128)S(1)}, u32[]{:S(2)}) copy-start(f32[1,512]{1,0:T(1,128)S(1)} %fusion.157) | copy-start | bytes 6148
  95.4 8.9 %collective-permute-start.11 = (f32[1,32,128]{2,0,1:T(1,128)S(1)}, f32[1,32,128]{2,0,1:T(1,128)S(1)}, u32[]{:S(2)}, u32[]{:S(2)}) collective-permute-start(f32[1,32,128]{2,0,1:T(1,128)S(1)} %get-tuple-element.44), channel_id=1, source_target_pairs={{0,16},{16,32},{32,48},{48,64},{64,80},{80,96},{96,112},{112,128},... | collective-permute-start | bytes 49160 | tf_op jit(solution)/shard_map/ppermute | solution.py:104
  98.1 6.2 %collective-permute-start.10 = (f32[1,32,128]{2,0,1:T(1,128)S(1)}, f32[1,32,128]{2,0,1:T(1,128)S(1)}, u32[]{:S(2)}, u32[]{:S(2)}) collective-permute-start(f32[1,32,128]{2,0,1:T(1,128)S(1)} %get-tuple-element.45), channel_id=1, source_target_pairs={{16,0},{32,16},{48,32},{64,48},{80,64},{96,80},{112,96},{128,112},... | collective-permute-start | bytes 49160 | tf_op jit(solution)/shard_map/ppermute | solution.py:105
  100.0 4.3 %collective-permute-start.8 = (f32[32,1,128]{2,0,1:T(8,128)S(1)}, f32[32,1,128]{2,0,1:T(8,128)S(1)}, u32[]{:S(2)}, u32[]{:S(2)}) collective-permute-start(f32[32,1,128]{2,0,1:T(8,128)S(1)} %get-tuple-element.42), channel_id=1, source_target_pairs={{0,1},{1,2},{2,3},{3,4},{4,5},{5,6},{6,7},{7,8},{8,9},{9,10},{10,1... | collective-permute-start | bytes 49160 | tf_op jit(solution)/shard_map/ppermute | solution.py:106
  102.3 4.6 %collective-permute-start.9 = (f32[32,1,128]{2,0,1:T(8,128)S(1)}, f32[32,1,128]{2,0,1:T(8,128)S(1)}, u32[]{:S(2)}, u32[]{:S(2)}) collective-permute-start(f32[32,1,128]{2,0,1:T(8,128)S(1)} %get-tuple-element.43), channel_id=1, source_target_pairs={{1,0},{2,1},{3,2},{4,3},{5,4},{6,5},{7,6},{8,7},{9,8},{10,9},{11,1... | collective-permute-start | bytes 49160 | tf_op jit(solution)/shard_map/ppermute | solution.py:107
  110.1 17.0 %copy-start.11 = (f32[34]{0:T(128)S(1)}, f32[34]{0:T(128)}, u32[]{:S(2)}) copy-start(f32[34]{0:T(128)} %copy-done.10) | copy-start | bytes 412
  110.1 17.0 %copy-start.13 = (f32[34]{0:T(128)S(1)}, f32[34]{0:T(128)}, u32[]{:S(2)}) copy-start(f32[34]{0:T(128)} %copy-done.12) | copy-start | bytes 412
  110.4 6.9 %collective-permute-start.12 = (f32[1,32,128]{2,0,1:T(1,128)S(1)}, f32[1,32,128]{2,0,1:T(1,128)S(1)}, u32[]{:S(2)}, u32[]{:S(2)}) collective-permute-start(f32[1,32,128]{2,0,1:T(1,128)S(1)} %get-tuple-element.40), channel_id=1, source_target_pairs={{0,16},{16,32},{32,48},{48,64},{64,80},{80,96},{96,112},{112,128},... | collective-permute-start | bytes 49160 | tf_op jit(solution)/shard_map/ppermute | solution.py:17
  115.4 5.1 %collective-permute-start.13 = (f32[1,32,128]{2,0,1:T(1,128)S(1)}, f32[1,32,128]{2,0,1:T(1,128)S(1)}, u32[]{:S(2)}, u32[]{:S(2)}) collective-permute-start(f32[1,32,128]{2,0,1:T(1,128)S(1)} %get-tuple-element.41), channel_id=1, source_target_pairs={{16,0},{32,16},{48,32},{64,48},{80,64},{96,80},{112,96},{128,112},... | collective-permute-start | bytes 49160 | tf_op jit(solution)/shard_map/ppermute | solution.py:19
  120.4 3.5 %collective-permute-start.14 = (f32[34,1,128]{2,0,1:T(8,128)S(1)}, f32[34,1,128]{2,0,1:T(8,128)S(1)}, u32[]{:S(2)}, u32[]{:S(2)}) collective-permute-start(f32[34,1,128]{2,0,1:T(8,128)S(1)} %get-tuple-element.32), channel_id=1, source_target_pairs={{0,1},{1,2},{2,3},{3,4},{4,5},{5,6},{6,7},{7,8},{8,9},{9,10},{10,1... | collective-permute-start | bytes 52232 | tf_op jit(solution)/shard_map/ppermute | solution.py:17
  122.6 4.5 %collective-permute-start.15 = (f32[34,1,128]{2,0,1:T(8,128)S(1)}, f32[34,1,128]{2,0,1:T(8,128)S(1)}, u32[]{:S(2)}, u32[]{:S(2)}) collective-permute-start(f32[34,1,128]{2,0,1:T(8,128)S(1)} %get-tuple-element.33), channel_id=1, source_target_pairs={{1,0},{2,1},{3,2},{4,3},{5,4},{6,5},{7,6},{8,7},{9,8},{10,9},{11,1... | collective-permute-start | bytes 52232 | tf_op jit(solution)/shard_map/ppermute | solution.py:19
  131.7 16.4 %copy-start.5 = (f32[32,1,128]{2,0,1:T(8,128)S(1)}, f32[32,1,128]{2,0,1:T(8,128)}, u32[]{:S(2)}) copy-start(f32[32,1,128]{2,0,1:T(8,128)} %copy-done.4) | copy-start | bytes 49156
  132.7 5.3 %collective-permute-start.16 = (f32[1,34,128]{2,0,1:T(1,128)S(1)}, f32[1,34,128]{2,0,1:T(1,128)S(1)}, u32[]{:S(2)}, u32[]{:S(2)}) collective-permute-start(f32[1,34,128]{2,0,1:T(1,128)S(1)} %get-tuple-element.26), channel_id=1, source_target_pairs={{0,16},{16,32},{32,48},{48,64},{64,80},{80,96},{96,112},{112,128},... | collective-permute-start | bytes 52232 | tf_op jit(solution)/shard_map/ppermute | solution.py:84
  136.1 5.1 %collective-permute-start.17 = (f32[1,34,128]{2,0,1:T(1,128)S(1)}, f32[1,34,128]{2,0,1:T(1,128)S(1)}, u32[]{:S(2)}, u32[]{:S(2)}) collective-permute-start(f32[1,34,128]{2,0,1:T(1,128)S(1)} %get-tuple-element.27), channel_id=1, source_target_pairs={{16,0},{32,16},{48,32},{64,48},{80,64},{96,80},{112,96},{128,112},... | collective-permute-start | bytes 52232 | tf_op jit(solution)/shard_map/ppermute | solution.py:85
  141.3 7.9 %copy-start.3 = (f32[32,34,128]{2,0,1:T(8,128)}, f32[32,34,128]{2,0,1:T(8,128)S(1)}, u32[]{:S(2)}) copy-start(f32[32,34,128]{2,0,1:T(8,128)S(1)} %fusion.25) | copy-start | bytes 1671172
  141.3 3.6 %collective-permute-start.18 = (f32[32,1,128]{2,0,1:T(8,128)S(1)}, f32[32,1,128]{2,0,1:T(8,128)S(1)}, u32[]{:S(2)}, u32[]{:S(2)}) collective-permute-start(f32[32,1,128]{2,0,1:T(8,128)S(1)} %get-tuple-element.30), channel_id=1, source_target_pairs={{0,1},{1,2},{2,3},{3,4},{4,5},{5,6},{6,7},{7,8},{8,9},{9,10},{10,1... | collective-permute-start | bytes 49160 | tf_op jit(solution)/shard_map/ppermute | solution.py:89
  143.6 4.5 %collective-permute-start.19 = (f32[32,1,128]{2,0,1:T(8,128)S(1)}, f32[32,1,128]{2,0,1:T(8,128)S(1)}, u32[]{:S(2)}, u32[]{:S(2)}) collective-permute-start(f32[32,1,128]{2,0,1:T(8,128)S(1)} %get-tuple-element.31), channel_id=1, source_target_pairs={{1,0},{2,1},{3,2},{4,3},{5,4},{6,5},{7,6},{8,7},{9,8},{10,9},{11,1... | collective-permute-start | bytes 49160 | tf_op jit(solution)/shard_map/ppermute | solution.py:90
  171.3 18.9 %all-to-all-start.3 = ((f32[32,1,20]{2,1,0:T(1,128)}), f32[32,1,20]{2,1,0:T(1,128)S(1)}, u32[]{:S(2)}, u32[]{:S(2)}) async-start(f32[32,1,20]{2,1,0:T(1,128)} %broadcast_in_dim.24), calls=%async_computation.3 | async-start | bytes 32768 | tf_op jit(solution)/shard_map/all_to_all | solution.py:32
  204.4 8.4 %collective-permute-start.23 = (f32[1,32,128]{2,0,1:T(1,128)S(1)}, f32[1,32,128]{2,0,1:T(1,128)S(1)}, u32[]{:S(2)}, u32[]{:S(2)}) collective-permute-start(f32[1,32,128]{2,0,1:T(1,128)S(1)} %get-tuple-element.38), channel_id=1, source_target_pairs={{0,16},{16,32},{32,48},{48,64},{64,80},{80,96},{96,112},{112,128},... | collective-permute-start | bytes 49160 | tf_op jit(solution)/shard_map/ppermute | solution.py:104
  207.2 5.7 %collective-permute-start.22 = (f32[1,32,128]{2,0,1:T(1,128)S(1)}, f32[1,32,128]{2,0,1:T(1,128)S(1)}, u32[]{:S(2)}, u32[]{:S(2)}) collective-permute-start(f32[1,32,128]{2,0,1:T(1,128)S(1)} %get-tuple-element.39), channel_id=1, source_target_pairs={{16,0},{32,16},{48,32},{64,48},{80,64},{96,80},{112,96},{128,112},... | collective-permute-start | bytes 49160 | tf_op jit(solution)/shard_map/ppermute | solution.py:105
  209.1 3.8 %collective-permute-start.20 = (f32[32,1,128]{2,0,1:T(8,128)S(1)}, f32[32,1,128]{2,0,1:T(8,128)S(1)}, u32[]{:S(2)}, u32[]{:S(2)}) collective-permute-start(f32[32,1,128]{2,0,1:T(8,128)S(1)} %get-tuple-element.36), channel_id=1, source_target_pairs={{0,1},{1,2},{2,3},{3,4},{4,5},{5,6},{6,7},{7,8},{8,9},{9,10},{10,1... | collective-permute-start | bytes 49160 | tf_op jit(solution)/shard_map/ppermute | solution.py:106
  211.3 4.6 %collective-permute-start.21 = (f32[32,1,128]{2,0,1:T(8,128)S(1)}, f32[32,1,128]{2,0,1:T(8,128)S(1)}, u32[]{:S(2)}, u32[]{:S(2)}) collective-permute-start(f32[32,1,128]{2,0,1:T(8,128)S(1)} %get-tuple-element.37), channel_id=1, source_target_pairs={{1,0},{2,1},{3,2},{4,3},{5,4},{6,5},{7,6},{8,7},{9,8},{10,9},{11,1... | collective-permute-start | bytes 49160 | tf_op jit(solution)/shard_map/ppermute | solution.py:107
  (7 other events, 33.4 us)

commit v4 on v3

--- a/solution.py
+++ b/solution.py
@@ -134,7 +134,8 @@
     inv_eig = 1.0 / (value_x[:, None, None] + value_y[None, :, None] + value_z[None, None, :])
     my_slot = lax.dynamic_index_in_dim(index_map, lax.axis_index(("gx", "gy")), 0, keepdims=False)
     inverse = coarse_inverse.astype(jnp.float32)
-    none = jnp.zeros((0,), jnp.float32)
+    count_x = lax.axis_size("gx")
+    count_y = lax.axis_size("gy")
 
     def local_solve(masked, wide=None):
         if wide is None:
@@ -147,18 +148,34 @@
         sol = jnp.dot(inverse, vec, precision=high)
         return vec, sol, lax.dynamic_index_in_dim(sol, my_slot, 0, keepdims=False)
 
-    def operate(direction):
-        padded_field = jnp.pad(face_halo(direction), ((0, 0), (0, 0), (1, 1)))
+    def operate(direction, wide=None):
+        if wide is None:
+            wide = face_halo(direction)
+        padded_field = jnp.pad(wide, ((0, 0), (0, 0), (1, 1)))
         beside = jnp.zeros_like(direction)
         for operate_weight, value in zip(beside_all(fluid_wide), beside_all(padded_field)):
             beside = beside + operate_weight * value
         return fluid * (count * direction - beside) + solid * direction
 
+    inner = fluid_wide[:, :, 1:-1]
+    k_row = jnp.stack(
+        [
+            jnp.sum(fluid * operate(fluid, jnp.pad(fluid, ((1, 1), (1, 1), (0, 0))))),
+            -jnp.sum(fluid[0] * inner[0, 1:-1]),
+            -jnp.sum(fluid[-1] * inner[-1, 1:-1]),
+            -jnp.sum(fluid[:, 0] * inner[1:-1, 0]),
+            -jnp.sum(fluid[:, -1] * inner[1:-1, -1]),
+        ]
+    )
+
     local0 = local_solve(masked, both_wide[:, :, :depth])
     every, partial = exchange(
-        (jnp.sum(masked) / cells).reshape(1), jnp.sum(residual * fluid * local0).reshape(1)
-    )
-    vec0, sol0, value0 = coarse(every)
+        jnp.concatenate([(jnp.sum(masked) / cells).reshape(1), k_row]),
+        jnp.sum(residual * fluid * local0).reshape(1),
+    )
+    every = every.reshape(subdomains, 6)
+    k_grid = every[:, 1:].reshape(count_x, count_y, 5)
+    vec0, sol0, value0 = coarse(every[:, 0])
     energy_now = partial[0] + cells * jnp.sum(vec0 * sol0)
     precond = fluid * (local0 + value0)
     direction = precond
@@ -166,30 +183,62 @@
     image = operate(direction)
     masked_w = image * fluid
     local_w = local_solve(masked_w)
+    fluid_local_w = fluid * local_w
+    image_local_w = operate(fluid_local_w)
     every_w, partial = exchange(
-        (jnp.sum(masked_w) / cells).reshape(1),
+        jnp.stack([jnp.sum(masked_w) / cells, jnp.sum(fluid * image_local_w)]),
         jnp.stack(
             [
                 jnp.sum(direction * image),
                 jnp.sum(residual * fluid * local_w),
                 jnp.sum(image * fluid * local0),
                 jnp.sum(image * fluid * local_w),
+                jnp.sum(fluid_local_w * image_local_w),
             ]
         ),
     )
-    vec_w, sol_w, value_w = coarse(every_w)
-    step_size = energy_now / partial[0]
+    every_w = every_w.reshape(subdomains, 2)
+    vec_w, sol_w, value_w = coarse(every_w[:, 0])
+    delta_now = partial[0]
+    step_size = energy_now / delta_now
     solution = step_size * direction
     residual = residual - step_size * image
     cross_r = partial[1] + cells * jnp.sum(vec0 * sol_w)
     cross_w = partial[2] + cells * jnp.sum(vec_w * sol0)
     square_w = partial[3] + cells * jnp.sum(vec_w * sol_w)
     energy_next = energy_now - step_size * (cross_r + cross_w) + step_size * step_size * square_w
+    ratio = energy_next / energy_now
     precond = precond - step_size * (fluid * (local_w + value_w))
-    direction = precond + energy_next / energy_now * direction
-
-    image = operate(direction)
-    step_size = energy_next / total(jnp.sum(direction * image))
+    direction = precond + ratio * direction
+
+    coarse_w = sol_w[index_map]
+    grid_w = coarse_w.reshape(count_x, count_y)
+    near_w = jnp.stack(
+        [
+            grid_w,
+            jnp.pad(grid_w[:-1], ((1, 0), (0, 0))),
+            jnp.pad(grid_w[1:], ((0, 1), (0, 0))),
+            jnp.pad(grid_w[:, :-1], ((0, 0), (1, 0))),
+            jnp.pad(grid_w[:, 1:], ((0, 0), (0, 1))),
+        ],
+        axis=-1,
+    )
+    coarse_energy = jnp.sum(grid_w[:, :, None] * k_grid * near_w)
+    square_m = partial[4] + 2.0 * jnp.sum(coarse_w * every_w[:, 1]) + coarse_energy
+    grow = 1.0 + ratio
+    delta_next = grow * grow * delta_now - 2.0 * step_size * grow * square_w + step_size * step_size * square_m
+
+    mine = near_w[lax.axis_index("gx"), lax.axis_index("gy")]
+    coarse_wide = jnp.zeros((rows_x + 2, rows_y + 2, depth), jnp.float32)
+    coarse_wide = coarse_wide.at[1:-1, 1:-1].set(fluid * mine[0])
+    coarse_wide = coarse_wide.at[0, 1:-1].set(inner[0, 1:-1] * mine[1])
+    coarse_wide = coarse_wide.at[-1, 1:-1].set(inner[-1, 1:-1] * mine[2])
+    coarse_wide = coarse_wide.at[1:-1, 0].set(inner[1:-1, 0] * mine[3])
+    coarse_wide = coarse_wide.at[1:-1, -1].set(inner[1:-1, -1] * mine[4])
+    image_m = image_local_w + operate(fluid * mine[0], coarse_wide)
+    image = grow * image - step_size * image_m
+
+    step_size = energy_next / delta_next
     solution = solution + step_size * direction
     residual = residual - step_size * image
     return (solution, residual)

time: 261 us -> 255 us (0.977)
  blocking collectives: 74.1 us -> 26 us
  local copies, waits for them, and re-layouts: 17.6 us -> 31.2 us
  starting transfers between devices: 82.2 us -> 94.2 us
  other arithmetic: 24 us -> 32.6 us
  between operations: 11.2 us -> 15.6 us
  waiting for transfers between devices: 38.6 us -> 42 us
    all_to_all x4 -> x1, blocking collectives: 74.1 us -> 26 us  [exchange(): lax.all_to_all(jnp.broadcast_to(stage[None], (count,) + stage.shape), axi...]
    all_to_all x2 -> x3, waiting for transfers between devices: 8.64 us -> 20.1 us  [exchange(): lax.all_to_all(jnp.broadcast_to(stage[None], (count,) + stage.shape), axi...]
    all_to_all x2 -> x3, starting transfers between devices: 22.6 us -> 32.3 us  [exchange(): lax.all_to_all(jnp.broadcast_to(stage[None], (count,) + stage.shape), axi...]
    mul x1 -> x3, other arithmetic: 1.41 us -> 6.6 us  [the longest x1 3.95 us: body(): image_m = image_local_w + operate(fluid * mine[0], coarse_wide)]
    reduce_sum x2 -> x7, other arithmetic: 4.23 us -> 9.43 us  [the longest x1 4.07 us: body(): jnp.sum(fluid_local_w * image_local_w)]
    gather x0 -> x1, local copies, waits for them, and re-layouts: none -> 3.49 us  [body(): coarse_w = sol_w[index_map]]
    add x2 -> x0, other arithmetic: 3.23 us -> none  [the longest x1 2.45 us: body(): direction = precond + energy_next / energy_now * direction]
    ppermute x2, waiting for transfers between devices: 7.63 us -> 4.43 us  [margin_sum(): from_right = lax.ppermute(body_rows[:, :1], 'gy', down_y)]
  transfers between devices with their start and end apart: 26 -> 27, of which waited for: 12 -> 13; matrix products, arithmetic and copies ran while one was open for 2% -> 4% of each run, Pallas kernels for 0% -> 0%
where the time goes in v4:
time: 255 us; the launch traced here: 253 us
  starting transfers between devices  94.2 us (37%)
  waiting for transfers between devices  42 us (16%)
  other arithmetic  32.6 us (13%)
  local copies, waits for them, and re-layouts  31.2 us (12%)
  blocking collectives  26 us (10%)
  between operations  15.6 us (6%)
  matrix products  11.9 us (5%)
    all_to_all x3, starting transfers between devices, exchange(): lax.all_to_all(jnp.broadcast_to(stage[None], (count,) + stage.shape), axi...  32.3 us
    all_to_all x1, blocking collectives, exchange(): lax.all_to_all(jnp.broadcast_to(stage[None], (count,) + stage.shape), axi...  26 us
    all_to_all x3, waiting for transfers between devices, exchange(): lax.all_to_all(jnp.broadcast_to(stage[None], (count,) + stage.shape), axi...  20.1 us
    ppermute x4, starting transfers between devices, with_halo(): lax.ppermute(tail, axis, [(i, (i + 1) % count) for i in range(ends)])  14.2 us
    ppermute x4, waiting for transfers between devices, with_halo(): lax.ppermute(head, axis, [((i + 1) % count, i) for i in range(ends)])  10.4 us
    ppermute x4, starting transfers between devices, with_halo(): lax.ppermute(head, axis, [((i + 1) % count, i) for i in range(ends)])  9.96 us
    ppermute x2, starting transfers between devices, margin_sum(): from_low = lax.ppermute(block[-1:], 'gx', up_x)  6.52 us
    ppermute x2, starting transfers between devices, face_halo(): low_x = lax.ppermute(cells[-1:], 'gx', up_x)  6.24 us
  transfers between devices with their start and end apart: 27, of which 13 were waited for; matrix products, arithmetic and copies ran while one was open for 4% of the time, Pallas kernels for 0%

profile of v4, /device:TPU:1, one launch (start us, length us, event | category | flops | bytes accessed | tf_op | source)
XLA Modules:
  0.0 253.4 jit_solution(16952938858427964018)
XLA Ops:
  1.7 1.4 broadcast_subtract_fusion
  3.2 4.6 %collective-permute-start = (f32[1,32,256]{2,0,1:T(1,128)S(1)}, f32[1,32,256]{2,0,1:T(1,128)S(1)}, u32[]{:S(2)}, u32[]{:S(2)}) collective-permute-start(f32[1,32,256]{2,0,1:T(1,128)S(1)} %get-tuple-element.93), channel_id=1, source_target_pairs={{0,16},{16,32},{32,48},{48,64},{64,80},{80,96},{96,112},{112,128},... | collective-permute-start | bytes 98312 | tf_op jit(solution)/shard_map/ppermute | solution.py:17
  7.8 5.5 %collective-permute-start.1 = (f32[1,32,256]{2,0,1:T(1,128)S(1)}, f32[1,32,256]{2,0,1:T(1,128)S(1)}, u32[]{:S(2)}, u32[]{:S(2)}) collective-permute-start(f32[1,32,256]{2,0,1:T(1,128)S(1)} %get-tuple-element.94), channel_id=1, source_target_pairs={{16,0},{32,16},{48,32},{64,48},{80,64},{96,80},{112,96},{128,112},... | collective-permute-start | bytes 98312 | tf_op jit(solution)/shard_map/ppermute | solution.py:19
  14.1 2.5 collective-permute-start.2
  18.1 3.5 %collective-permute-done.3 = f32[34,1,256]{2,0,1:T(8,128)S(1)} collective-permute-done((f32[34,1,256]{2,0,1:T(8,128)S(1)}, f32[34,1,256]{2,0,1:T(8,128)S(1)}, u32[]{:S(2)}, u32[]{:S(2)}) %collective-permute-start.3) | collective-permute-done | bytes 34848 | tf_op jit(solution)/shard_map/ppermute | solution.py:19
  27.5 3.2 %collective-permute-start.4 = (f32[1,34,128]{2,0,1:T(1,128)S(1)}, f32[1,34,128]{2,0,1:T(1,128)S(1)}, u32[]{:S(2)}, u32[]{:S(2)}) collective-permute-start(f32[1,34,128]{2,0,1:T(1,128)S(1)} %get-tuple-element.97), channel_id=1, source_target_pairs={{0,16},{16,32},{32,48},{48,64},{64,80},{80,96},{96,112},{112,128},... | collective-permute-start | bytes 52232 | tf_op jit(solution)/shard_map/ppermute | solution.py:84
  30.7 1.9 collective-permute-start.5
  33.0 1.9 fusion.77
  35.9 3.5 %collective-permute-start.6 = (f32[32,1,128]{2,0,1:T(8,128)S(1)}, f32[32,1,128]{2,0,1:T(8,128)S(1)}, u32[]{:S(2)}, u32[]{:S(2)}) collective-permute-start(f32[32,1,128]{2,0,1:T(8,128)S(1)} %get-tuple-element.104), channel_id=1, source_target_pairs={{0,1},{1,2},{2,3},{3,4},{4,5},{5,6},{6,7},{7,8},{8,9},{9,10},{10,1... | collective-permute-start | bytes 49160 | tf_op jit(solution)/shard_map/ppermute | solution.py:89
  39.4 1.3 collective-permute-start.7
  46.7 1.4 concatenate.85
  48.1 26.0 %all_to_all.36 = f32[16,1,7]{2,1,0:T(1,128)S(1)} all-to-all(f32[16,1,7]{2,1,0:T(1,128)S(1)} %broadcast_in_dim.16), channel_id=1, replica_groups=mesh['gx'=32,'gy'=16] {'gy'}, dimensions={0} | all-to-all | bytes 896 | tf_op jit(solution)/shard_map/all_to_all | solution.py:32
  76.3 10.9 %all-to-all-start.1 = ((f32[32,1,97]{2,1,0:T(1,128)}), f32[32,1,97]{2,1,0:T(1,128)S(1)}, u32[]{:S(2)}, u32[]{:S(2)}) async-start(f32[32,1,97]{2,1,0:T(1,128)} %broadcast_in_dim.17), calls=%async_computation.1 | async-start | bytes 32768 | tf_op jit(solution)/shard_map/all_to_all | solution.py:32
  89.7 4.4 %all-to-all-done.1 = f32[32,1,97]{2,1,0:T(1,128)S(1)} async-done(((f32[32,1,97]{2,1,0:T(1,128)}), f32[32,1,97]{2,1,0:T(1,128)S(1)}, u32[]{:S(2)}, u32[]{:S(2)}) %all-to-all-start.1) | async-done | bytes 12448 | tf_op jit(solution)/shard_map/all_to_all | solution.py:32
  94.4 2.4 scatter_custom_fusion
  98.9 2.7 %collective-permute-start.11 = (f32[1,32,128]{2,0,1:T(1,128)S(1)}, f32[1,32,128]{2,0,1:T(1,128)S(1)}, u32[]{:S(2)}, u32[]{:S(2)}) collective-permute-start(f32[1,32,128]{2,0,1:T(1,128)S(1)} %get-tuple-element.114), channel_id=1, source_target_pairs={{0,16},{16,32},{32,48},{48,64},{64,80},{80,96},{96,112},{112,128},... | collective-permute-start | bytes 49160 | tf_op jit(solution)/shard_map/ppermute | solution.py:104
  101.7 1.9 collective-permute-start.10
  103.6 2.2 collective-permute-start.8
  105.8 1.5 collective-permute-start.9
  107.4 3.0 %collective-permute-done.9 = f32[32,1,128]{2,0,1:T(8,128)S(1)} collective-permute-done((f32[32,1,128]{2,0,1:T(8,128)S(1)}, f32[32,1,128]{2,0,1:T(8,128)S(1)}, u32[]{:S(2)}, u32[]{:S(2)}) %collective-permute-start.9) | collective-permute-done | bytes 16416 | tf_op jit(solution)/shard_map/ppermute | solution.py:107
  111.0 2.5 multiply_reduce_fusion.4
  113.8 5.0 %collective-permute-start.12 = (f32[1,32,128]{2,0,1:T(1,128)S(1)}, f32[1,32,128]{2,0,1:T(1,128)S(1)}, u32[]{:S(2)}, u32[]{:S(2)}) collective-permute-start(f32[1,32,128]{2,0,1:T(1,128)S(1)} %get-tuple-element.110), channel_id=1, source_target_pairs={{0,16},{16,32},{32,48},{48,64},{64,80},{80,96},{96,112},{112,128},... | collective-permute-start | bytes 49160 | tf_op jit(solution)/shard_map/ppermute | solution.py:17
  118.8 1.9 collective-permute-start.13
  120.7 3.1 %collective-permute-done.13 = f32[1,32,128]{2,0,1:T(1,128)S(1)} collective-permute-done((f32[1,32,128]{2,0,1:T(1,128)S(1)}, f32[1,32,128]{2,0,1:T(1,128)S(1)}, u32[]{:S(2)}, u32[]{:S(2)}) %collective-permute-start.13) | collective-permute-done | bytes 16416 | tf_op jit(solution)/shard_map/ppermute | solution.py:19
  123.8 2.1 collective-permute-start.14
  127.3 3.2 %collective-permute-done.15 = f32[34,1,128]{2,0,1:T(8,128)S(1)} collective-permute-done((f32[34,1,128]{2,0,1:T(8,128)S(1)}, f32[34,1,128]{2,0,1:T(8,128)S(1)}, u32[]{:S(2)}, u32[]{:S(2)}) %collective-permute-start.15) | collective-permute-done | bytes 17440 | tf_op jit(solution)/shard_map/ppermute | solution.py:19
  136.1 3.4 %collective-permute-start.16 = (f32[1,34,128]{2,0,1:T(1,128)S(1)}, f32[1,34,128]{2,0,1:T(1,128)S(1)}, u32[]{:S(2)}, u32[]{:S(2)}) collective-permute-start(f32[1,34,128]{2,0,1:T(1,128)S(1)} %get-tuple-element.95), channel_id=1, source_target_pairs={{0,16},{16,32},{32,48},{48,64},{64,80},{80,96},{96,112},{112,128},... | collective-permute-start | bytes 52232 | tf_op jit(solution)/shard_map/ppermute | solution.py:84
  139.5 1.9 collective-permute-start.17
  141.4 3.1 %collective-permute-done.17 = f32[1,34,128]{2,0,1:T(1,128)S(1)} collective-permute-done((f32[1,34,128]{2,0,1:T(1,128)S(1)}, f32[1,34,128]{2,0,1:T(1,128)S(1)}, u32[]{:S(2)}, u32[]{:S(2)}) %collective-permute-start.17) | collective-permute-done | bytes 17440 | tf_op jit(solution)/shard_map/ppermute | solution.py:85
  144.7 2.3 collective-permute-start.18
  148.3 3.2 %collective-permute-done.19 = f32[32,1,128]{2,0,1:T(8,128)S(1)} collective-permute-done((f32[32,1,128]{2,0,1:T(8,128)S(1)}, f32[32,1,128]{2,0,1:T(8,128)S(1)}, u32[]{:S(2)}, u32[]{:S(2)}) %collective-permute-start.19) | collective-permute-done | bytes 16416 | tf_op jit(solution)/shard_map/ppermute | solution.py:90
  153.9 3.5 %collective-permute-start.23 = (f32[1,32,128]{2,0,1:T(1,128)}, f32[1,32,128]{2,0,1:T(1,128)}, u32[]{:S(2)}, u32[]{:S(2)}) collective-permute-start(f32[1,32,128]{2,0,1:T(1,128)} %get-tuple-element.108), channel_id=1, source_target_pairs={{0,16},{16,32},{32,48},{48,64},{64,80},{80,96},{96,112},{112,128},... | collective-permute-start | bytes 49160 | tf_op jit(solution)/shard_map/ppermute | solution.py:104
  157.4 1.9 collective-permute-start.22
  159.3 3.9 %collective-permute-start.20 = (f32[32,1,128]{2,0,1:T(8,128)}, f32[32,1,128]{2,0,1:T(8,128)}, u32[]{:S(2)}, u32[]{:S(2)}) collective-permute-start(f32[32,1,128]{2,0,1:T(8,128)} %get-tuple-element.106), channel_id=1, source_target_pairs={{0,1},{1,2},{2,3},{3,4},{4,5},{5,6},{6,7},{7,8},{8,9},{9,10},{10,1... | collective-permute-start | bytes 49160 | tf_op jit(solution)/shard_map/ppermute | solution.py:106
  168.1 1.6 select_maximum_fusion
  169.8 4.1 %multiply_reduce_fusion = (f32[]{:T(128)}, f32[]{:T(128)}, f32[32,32,128]{2,0,1:T(8,128)}) fusion(f32[32,32,128]{2,0,1:T(8,128)S(1)} %copy-done.3, s32[32,32]{0,1:T(8,128)S(1)} %copy.37, f32[34,34,130]{2,0,1:T(8,128)S(1)} %select_maximum_fusion, f32[32,1,128]{2,0,1:T(8,128)} %collective-permute-done.20, f32[32,1,128]{2,0,1:T(8,128)} %collective-permute-done.21, ...), kind=kLoop, calls=%fused_computation.132 | loop fusion | flops 4718590 | bytes 5314568 | tf_op jit(solution)/shard_map/reduce_sum | solution.py:196
  173.8 3.7 %concatenate.101 = f32[7]{0:T(128)S(1)} concatenate(f32[1]{0:T(128)} %bitcast.18, f32[1]{0:T(128)} %bitcast.21, f32[1]{0:T(128)} %bitcast.22, f32[1]{0:T(128)} %bitcast.23, f32[1]{0:T(128)} %bitcast.24, f32[1]{0:T(128)} %bitcast.25, f32[1]{0:T(128)} %bitcast.26), dimensions={0} | concatenate | bytes 56 | tf_op jit(solution)/shard_map/concatenate | solution.py:29
  178.2 6.7 %all-to-all-start.2 = ((f32[16,1,7]{2,1,0:T(1,128)}), f32[16,1,7]{2,1,0:T(1,128)S(1)}, u32[]{:S(2)}, u32[]{:S(2)}) async-start(f32[16,1,7]{2,1,0:T(1,128)} %broadcast_in_dim.19), calls=%async_computation.2 | async-start | bytes 16384 | tf_op jit(solution)/shard_map/all_to_all | solution.py:32
  185.0 11.3 %all-to-all-done.2 = f32[16,1,7]{2,1,0:T(1,128)S(1)} async-done(((f32[16,1,7]{2,1,0:T(1,128)}), f32[16,1,7]{2,1,0:T(1,128)S(1)}, u32[]{:S(2)}, u32[]{:S(2)}) %all-to-all-start.2) | async-done | bytes 480 | tf_op jit(solution)/shard_map/all_to_all | solution.py:32
  197.3 14.6 %all-to-all-start.3 = ((f32[32,1,37]{2,1,0:T(1,128)}), f32[32,1,37]{2,1,0:T(1,128)S(1)}, u32[]{:S(2)}, u32[]{:S(2)}) async-start(f32[32,1,37]{2,1,0:T(1,128)} %broadcast_in_dim.20), calls=%async_computation.3 | async-start | bytes 32768 | tf_op jit(solution)/shard_map/all_to_all | solution.py:32
  212.0 1.4 slice_reduce_fusion.4
  214.5 4.4 %all-to-all-done.3 = f32[32,1,37]{2,1,0:T(1,128)S(1)} async-done(((f32[32,1,37]{2,1,0:T(1,128)}), f32[32,1,37]{2,1,0:T(1,128)S(1)}, u32[]{:S(2)}, u32[]{:S(2)}) %all-to-all-start.3) | async-done | bytes 4768 | tf_op jit(solution)/shard_map/all_to_all | solution.py:32
  219.5 2.6 %scatter_custom_fusion.1 = f32[512]{0:T(512)S(1)} fusion(s32[512]{0:T(512)} %copy-done.22, f32[512]{0:T(512)S(1)} %get-tuple-element.79, f32[]{:T(128)} %constant.209.clone.1), kind=kCustom, calls=%fused_computation.252 | custom fusion | bytes 2560 | tf_op jit(solution)/shard_map/scatter | solution.py:147
  223.8 3.5 %gather_fusion = f32[512]{0:T(512)S(1)} fusion(f32[512]{0:T(512)S(1)} %bitcast.96, s32[1024]{0:T(1024)S(1)} %pad_clamp_fusion), kind=kCustom, calls=%fused_computation | custom fusion | bytes 6144 | tf_op jit(solution)/shard_map/gather | solution.py:214
  239.1 4.0 %broadcast_multiply_fusion = (f32[32,32,128]{2,0,1:T(8,128)S(1)}, f32[32,32,128]{2,0,1:T(8,128)}) fusion(f32[]{:T(128)} %bitcast.42, s32[32,32]{0,1:T(8,128)S(1)} %copy.37, f32[]{:T(128)S(6)} %div.81, f32[]{:T(128)} %bitcast.37, f32[32,1,128]{2,0,1:T(8,128)S(1)} %copy-done.17, f32[32,1,128]{2,0,1:T(8,128)S(1)} %copy-done.15, f32[32,34,128]{2,0,1:T(8,128)} %copy-done.4, ...), kind=kLoop, calls=%fused_computation.148 | loop fusion | flops 2490368 | bytes 2166808 | tf_op jit(solution)/shard_map/mul | solution.py:238
  244.4 1.4 slice_multiply_fusion.14
  245.8 1.4 scatter.42
  247.7 3.5 %fusion.45 = f32[32,32,128]{2,0,1:T(8,128)S(1)} fusion(f32[32,32,128]{2,0,1:T(8,128)} %get-tuple-element.86, f32[34,34,128]{2,0,1:T(8,128)S(1)} %scatter.45, f32[32,32,128]{2,0,1:T(8,128)S(1)} %get-tuple-element.85, f32[32,32,128]{2,1,0:T(8,128)} %param.14, f32[34,34,130]{2,0,1:T(8,128)S(1)} %maximum_subtract_fusion, f32[]{:T(128)S(6)} %add.400, ...), kind=kLoop, calls=%fused_computation.73 | loop fusion | flops 4456448 | bytes 8052752 | tf_op jit(solution)/shard_map/sub | solution.py:243
  (199 shorter events, 46.9 us)
Async XLA Ops:
  0.6 96.2 %copy-start = (bf16[512,512]{1,0:T(8,128)(2,1)S(1)}, bf16[512,512]{1,0:T(8,128)(2,1)}, u32[]{:S(2)}) copy-start(bf16[512,512]{1,0:T(8,128)(2,1)} %param.17) | copy-start | bytes 1572868
  3.2 10.3 %collective-permute-start = (f32[1,32,256]{2,0,1:T(1,128)S(1)}, f32[1,32,256]{2,0,1:T(1,128)S(1)}, u32[]{:S(2)}, u32[]{:S(2)}) collective-permute-start(f32[1,32,256]{2,0,1:T(1,128)S(1)} %get-tuple-element.93), channel_id=1, source_target_pairs={{0,16},{16,32},{32,48},{48,64},{64,80},{80,96},{96,112},{112,128},... | collective-permute-start | bytes 98312 | tf_op jit(solution)/shard_map/ppermute | solution.py:17
  7.8 6.3 %collective-permute-start.1 = (f32[1,32,256]{2,0,1:T(1,128)S(1)}, f32[1,32,256]{2,0,1:T(1,128)S(1)}, u32[]{:S(2)}, u32[]{:S(2)}) collective-permute-start(f32[1,32,256]{2,0,1:T(1,128)S(1)} %get-tuple-element.94), channel_id=1, source_target_pairs={{16,0},{32,16},{48,32},{64,48},{80,64},{96,80},{112,96},{128,112},... | collective-permute-start | bytes 98312 | tf_op jit(solution)/shard_map/ppermute | solution.py:19
  13.3 10.3 %copy-start.29 = (f32[128]{0:T(128)}, f32[128]{0:T(128)S(1)}, u32[]{:S(2)}) copy-start(f32[128]{0:T(128)S(1)} %get-tuple-element.136) | copy-start | bytes 1540
  13.4 13.1 %copy-start.24 = (f32[128]{0:T(128)}, f32[128]{0:T(128)S(1)}, u32[]{:S(2)}) copy-start(f32[128]{0:T(128)S(1)} %get-tuple-element.137) | copy-start | bytes 1540
  13.4 10.2 %copy-start.18 = (f32[34,34]{1,0:T(8,128)}, f32[34,34]{1,0:T(8,128)S(1)}, u32[]{:S(2)}) copy-start(f32[34,34]{1,0:T(8,128)S(1)} %broadcast_add_fusion) | copy-start | bytes 13876
  14.1 4.0 %collective-permute-start.2 = (f32[34,1,256]{2,0,1:T(8,128)S(1)}, f32[34,1,256]{2,0,1:T(8,128)S(1)}, u32[]{:S(2)}, u32[]{:S(2)}) collective-permute-start(f32[34,1,256]{2,0,1:T(8,128)S(1)} %get-tuple-element.91), channel_id=1, source_target_pairs={{0,1},{1,2},{2,3},{3,4},{4,5},{5,6},{6,7},{7,8},{8,9},{9,10},{10,1... | collective-permute-start | bytes 104456 | tf_op jit(solution)/shard_map/ppermute | solution.py:17
  16.6 4.9 %collective-permute-start.3 = (f32[34,1,256]{2,0,1:T(8,128)S(1)}, f32[34,1,256]{2,0,1:T(8,128)S(1)}, u32[]{:S(2)}, u32[]{:S(2)}) collective-permute-start(f32[34,1,256]{2,0,1:T(8,128)S(1)} %get-tuple-element.92), channel_id=1, source_target_pairs={{1,0},{2,1},{3,2},{4,3},{5,4},{6,5},{7,6},{8,7},{9,8},{10,9},{11,1... | collective-permute-start | bytes 104456 | tf_op jit(solution)/shard_map/ppermute | solution.py:19
  17.9 8.6 %copy-start.26 = (f32[128]{0:T(128)}, f32[128]{0:T(128)S(1)}, u32[]{:S(2)}) copy-start(f32[128]{0:T(128)S(1)} %broadcast_multiply_fusion.1) | copy-start | bytes 1540
  27.5 8.2 %collective-permute-start.4 = (f32[1,34,128]{2,0,1:T(1,128)S(1)}, f32[1,34,128]{2,0,1:T(1,128)S(1)}, u32[]{:S(2)}, u32[]{:S(2)}) collective-permute-start(f32[1,34,128]{2,0,1:T(1,128)S(1)} %get-tuple-element.97), channel_id=1, source_target_pairs={{0,16},{16,32},{32,48},{48,64},{64,80},{80,96},{96,112},{112,128},... | collective-permute-start | bytes 52232 | tf_op jit(solution)/shard_map/ppermute | solution.py:84
  30.7 5.1 %collective-permute-start.5 = (f32[1,34,128]{2,0,1:T(1,128)S(1)}, f32[1,34,128]{2,0,1:T(1,128)S(1)}, u32[]{:S(2)}, u32[]{:S(2)}) collective-permute-start(f32[1,34,128]{2,0,1:T(1,128)S(1)} %get-tuple-element.98), channel_id=1, source_target_pairs={{16,0},{32,16},{48,32},{64,48},{80,64},{96,80},{112,96},{128,112},... | collective-permute-start | bytes 52232 | tf_op jit(solution)/shard_map/ppermute | solution.py:85
  34.9 52.3 %copy-start.28 = (s32[512]{0:T(512)S(1)}, s32[512]{0:T(512)}, u32[]{:S(2)}) copy-start(s32[512]{0:T(512)} %param.16) | copy-start | bytes 6148
  35.9 8.0 %collective-permute-start.6 = (f32[32,1,128]{2,0,1:T(8,128)S(1)}, f32[32,1,128]{2,0,1:T(8,128)S(1)}, u32[]{:S(2)}, u32[]{:S(2)}) collective-permute-start(f32[32,1,128]{2,0,1:T(8,128)S(1)} %get-tuple-element.104), channel_id=1, source_target_pairs={{0,1},{1,2},{2,3},{3,4},{4,5},{5,6},{6,7},{7,8},{8,9},{9,10},{10,1... | collective-permute-start | bytes 49160 | tf_op jit(solution)/shard_map/ppermute | solution.py:89
  39.4 5.8 %collective-permute-start.7 = (f32[32,1,128]{2,0,1:T(8,128)S(1)}, f32[32,1,128]{2,0,1:T(8,128)S(1)}, u32[]{:S(2)}, u32[]{:S(2)}) collective-permute-start(f32[32,1,128]{2,0,1:T(8,128)S(1)} %get-tuple-element.105), channel_id=1, source_target_pairs={{1,0},{2,1},{3,2},{4,3},{5,4},{6,5},{7,6},{8,7},{9,8},{10,9},{11,1... | collective-permute-start | bytes 49160 | tf_op jit(solution)/shard_map/ppermute | solution.py:90
  43.9 55.0 %copy-start.7 = (f32[32,1,128]{2,0,1:T(8,128)}, f32[32,1,128]{2,0,1:T(8,128)S(1)}, u32[]{:S(2)}) copy-start(f32[32,1,128]{2,0,1:T(8,128)S(1)} %collective-permute-done.6) | copy-start | bytes 49156
  45.2 53.7 %copy-start.10 = (f32[32,1,128]{2,0,1:T(8,128)}, f32[32,1,128]{2,0,1:T(8,128)S(1)}, u32[]{:S(2)}) copy-start(f32[32,1,128]{2,0,1:T(8,128)S(1)} %collective-permute-done.7) | copy-start | bytes 49156
  76.3 17.8 %all-to-all-start.1 = ((f32[32,1,97]{2,1,0:T(1,128)}), f32[32,1,97]{2,1,0:T(1,128)S(1)}, u32[]{:S(2)}, u32[]{:S(2)}) async-start(f32[32,1,97]{2,1,0:T(1,128)} %broadcast_in_dim.17), calls=%async_computation.1 | async-start | bytes 32768 | tf_op jit(solution)/shard_map/all_to_all | solution.py:32
  87.2 9.6 %copy-start.22 = (s32[512]{0:T(512)}, s32[512]{0:T(512)S(1)}, u32[]{:S(2)}) copy-start(s32[512]{0:T(512)S(1)} %compare_select_fusion) | copy-start | bytes 6148
  94.1 16.3 %copy-start.13 = (f32[32,1,97]{2,1,0:T(1,128)}, f32[32,1,97]{2,1,0:T(1,128)S(1)}, u32[]{:S(2)}) copy-start(f32[32,1,97]{2,1,0:T(1,128)S(1)} %all-to-all-done.1) | copy-start | bytes 37252
  94.2 16.2 %copy-start.5 = (f32[512,6]{1,0:T(8,128)}, f32[512,6]{1,0:T(8,128)S(1)}, u32[]{:S(2)}) copy-start(f32[512,6]{1,0:T(8,128)S(1)} %reshape_reshape.6) | copy-start | bytes 36868
  97.4 13.6 %copy-start.20 = (f32[1,512]{1,0:T(1,128)}, f32[1,512]{1,0:T(1,128)S(1)}, u32[]{:S(2)}) copy-start(f32[1,512]{1,0:T(1,128)S(1)} %fusion.190) | copy-start | bytes 6148
  98.9 8.4 %collective-permute-start.11 = (f32[1,32,128]{2,0,1:T(1,128)S(1)}, f32[1,32,128]{2,0,1:T(1,128)S(1)}, u32[]{:S(2)}, u32[]{:S(2)}) collective-permute-start(f32[1,32,128]{2,0,1:T(1,128)S(1)} %get-tuple-element.114), channel_id=1, source_target_pairs={{0,16},{16,32},{32,48},{48,64},{64,80},{80,96},{96,112},{112,128},... | collective-permute-start | bytes 49160 | tf_op jit(solution)/shard_map/ppermute | solution.py:104
  101.7 5.7 %collective-permute-start.10 = (f32[1,32,128]{2,0,1:T(1,128)S(1)}, f32[1,32,128]{2,0,1:T(1,128)S(1)}, u32[]{:S(2)}, u32[]{:S(2)}) collective-permute-start(f32[1,32,128]{2,0,1:T(1,128)S(1)} %get-tuple-element.115), channel_id=1, source_target_pairs={{16,0},{32,16},{48,32},{64,48},{80,64},{96,80},{112,96},{128,112},... | collective-permute-start | bytes 49160 | tf_op jit(solution)/shard_map/ppermute | solution.py:105
  103.6 3.8 %collective-permute-start.8 = (f32[32,1,128]{2,0,1:T(8,128)S(1)}, f32[32,1,128]{2,0,1:T(8,128)S(1)}, u32[]{:S(2)}, u32[]{:S(2)}) collective-permute-start(f32[32,1,128]{2,0,1:T(8,128)S(1)} %get-tuple-element.112), channel_id=1, source_target_pairs={{0,1},{1,2},{2,3},{3,4},{4,5},{5,6},{6,7},{7,8},{8,9},{9,10},{10,1... | collective-permute-start | bytes 49160 | tf_op jit(solution)/shard_map/ppermute | solution.py:106
  105.8 4.6 %collective-permute-start.9 = (f32[32,1,128]{2,0,1:T(8,128)S(1)}, f32[32,1,128]{2,0,1:T(8,128)S(1)}, u32[]{:S(2)}, u32[]{:S(2)}) collective-permute-start(f32[32,1,128]{2,0,1:T(8,128)S(1)} %get-tuple-element.113), channel_id=1, source_target_pairs={{1,0},{2,1},{3,2},{4,3},{5,4},{6,5},{7,6},{8,7},{9,8},{10,9},{11,1... | collective-permute-start | bytes 49160 | tf_op jit(solution)/shard_map/ppermute | solution.py:107
  113.8 6.9 %collective-permute-start.12 = (f32[1,32,128]{2,0,1:T(1,128)S(1)}, f32[1,32,128]{2,0,1:T(1,128)S(1)}, u32[]{:S(2)}, u32[]{:S(2)}) collective-permute-start(f32[1,32,128]{2,0,1:T(1,128)S(1)} %get-tuple-element.110), channel_id=1, source_target_pairs={{0,16},{16,32},{32,48},{48,64},{64,80},{80,96},{96,112},{112,128},... | collective-permute-start | bytes 49160 | tf_op jit(solution)/shard_map/ppermute | solution.py:17
  118.8 5.1 %collective-permute-start.13 = (f32[1,32,128]{2,0,1:T(1,128)S(1)}, f32[1,32,128]{2,0,1:T(1,128)S(1)}, u32[]{:S(2)}, u32[]{:S(2)}) collective-permute-start(f32[1,32,128]{2,0,1:T(1,128)S(1)} %get-tuple-element.111), channel_id=1, source_target_pairs={{16,0},{32,16},{48,32},{64,48},{80,64},{96,80},{112,96},{128,112},... | collective-permute-start | bytes 49160 | tf_op jit(solution)/shard_map/ppermute | solution.py:19
  123.8 3.5 %collective-permute-start.14 = (f32[34,1,128]{2,0,1:T(8,128)S(1)}, f32[34,1,128]{2,0,1:T(8,128)S(1)}, u32[]{:S(2)}, u32[]{:S(2)}) collective-permute-start(f32[34,1,128]{2,0,1:T(8,128)S(1)} %get-tuple-element.102), channel_id=1, source_target_pairs={{0,1},{1,2},{2,3},{3,4},{4,5},{5,6},{6,7},{7,8},{8,9},{9,10},{10,1... | collective-permute-start | bytes 52232 | tf_op jit(solution)/shard_map/ppermute | solution.py:17
  126.0 4.5 %collective-permute-start.15 = (f32[34,1,128]{2,0,1:T(8,128)S(1)}, f32[34,1,128]{2,0,1:T(8,128)S(1)}, u32[]{:S(2)}, u32[]{:S(2)}) collective-permute-start(f32[34,1,128]{2,0,1:T(8,128)S(1)} %get-tuple-element.103), channel_id=1, source_target_pairs={{1,0},{2,1},{3,2},{4,3},{5,4},{6,5},{7,6},{8,7},{9,8},{10,9},{11,1... | collective-permute-start | bytes 52232 | tf_op jit(solution)/shard_map/ppermute | solution.py:19
  135.1 16.4 %copy-start.8 = (f32[32,1,128]{2,0,1:T(8,128)S(1)}, f32[32,1,128]{2,0,1:T(8,128)}, u32[]{:S(2)}) copy-start(f32[32,1,128]{2,0,1:T(8,128)} %copy-done.7) | copy-start | bytes 49156
  135.1 16.4 %copy-start.11 = (f32[32,1,128]{2,0,1:T(8,128)S(1)}, f32[32,1,128]{2,0,1:T(8,128)}, u32[]{:S(2)}) copy-start(f32[32,1,128]{2,0,1:T(8,128)} %copy-done.10) | copy-start | bytes 49156
  136.1 5.3 %collective-permute-start.16 = (f32[1,34,128]{2,0,1:T(1,128)S(1)}, f32[1,34,128]{2,0,1:T(1,128)S(1)}, u32[]{:S(2)}, u32[]{:S(2)}) collective-permute-start(f32[1,34,128]{2,0,1:T(1,128)S(1)} %get-tuple-element.95), channel_id=1, source_target_pairs={{0,16},{16,32},{32,48},{48,64},{64,80},{80,96},{96,112},{112,128},... | collective-permute-start | bytes 52232 | tf_op jit(solution)/shard_map/ppermute | solution.py:84
  139.5 5.1 %collective-permute-start.17 = (f32[1,34,128]{2,0,1:T(1,128)S(1)}, f32[1,34,128]{2,0,1:T(1,128)S(1)}, u32[]{:S(2)}, u32[]{:S(2)}) collective-permute-start(f32[1,34,128]{2,0,1:T(1,128)S(1)} %get-tuple-element.96), channel_id=1, source_target_pairs={{16,0},{32,16},{48,32},{64,48},{80,64},{96,80},{112,96},{128,112},... | collective-permute-start | bytes 52232 | tf_op jit(solution)/shard_map/ppermute | solution.py:85
  144.7 3.6 %collective-permute-start.18 = (f32[32,1,128]{2,0,1:T(8,128)S(1)}, f32[32,1,128]{2,0,1:T(8,128)S(1)}, u32[]{:S(2)}, u32[]{:S(2)}) collective-permute-start(f32[32,1,128]{2,0,1:T(8,128)S(1)} %get-tuple-element.100), channel_id=1, source_target_pairs={{0,1},{1,2},{2,3},{3,4},{4,5},{5,6},{6,7},{7,8},{8,9},{9,10},{10,1... | collective-permute-start | bytes 49160 | tf_op jit(solution)/shard_map/ppermute | solution.py:89
  147.0 4.5 %collective-permute-start.19 = (f32[32,1,128]{2,0,1:T(8,128)S(1)}, f32[32,1,128]{2,0,1:T(8,128)S(1)}, u32[]{:S(2)}, u32[]{:S(2)}) collective-permute-start(f32[32,1,128]{2,0,1:T(8,128)S(1)} %get-tuple-element.101), channel_id=1, source_target_pairs={{1,0},{2,1},{3,2},{4,3},{5,4},{6,5},{7,6},{8,7},{9,8},{10,9},{11,1... | collective-permute-start | bytes 49160 | tf_op jit(solution)/shard_map/ppermute | solution.py:90
  153.9 15.9 %copy-start.3 = (f32[32,32,128]{2,0,1:T(8,128)S(1)}, f32[32,32,128]{2,0,1:T(8,128)}, u32[]{:S(2)}) copy-start(f32[32,32,128]{2,0,1:T(8,128)} %copy-done.2) | copy-start | bytes 1572868
  153.9 11.9 %collective-permute-start.23 = (f32[1,32,128]{2,0,1:T(1,128)}, f32[1,32,128]{2,0,1:T(1,128)}, u32[]{:S(2)}, u32[]{:S(2)}) collective-permute-start(f32[1,32,128]{2,0,1:T(1,128)} %get-tuple-element.108), channel_id=1, source_target_pairs={{0,16},{16,32},{32,48},{48,64},{64,80},{80,96},{96,112},{112,128},... | collective-permute-start | bytes 49160 | tf_op jit(solution)/shard_map/ppermute | solution.py:104
  157.4 9.2 %collective-permute-start.22 = (f32[1,32,128]{2,0,1:T(1,128)}, f32[1,32,128]{2,0,1:T(1,128)}, u32[]{:S(2)}, u32[]{:S(2)}) collective-permute-start(f32[1,32,128]{2,0,1:T(1,128)} %get-tuple-element.109), channel_id=1, source_target_pairs={{16,0},{32,16},{48,32},{64,48},{80,64},{96,80},{112,96},{128,112},... | collective-permute-start | bytes 49160 | tf_op jit(solution)/shard_map/ppermute | solution.py:105
  159.3 8.0 %collective-permute-start.20 = (f32[32,1,128]{2,0,1:T(8,128)}, f32[32,1,128]{2,0,1:T(8,128)}, u32[]{:S(2)}, u32[]{:S(2)}) collective-permute-start(f32[32,1,128]{2,0,1:T(8,128)} %get-tuple-element.106), channel_id=1, source_target_pairs={{0,1},{1,2},{2,3},{3,4},{4,5},{5,6},{6,7},{7,8},{8,9},{9,10},{10,1... | collective-permute-start | bytes 49160 | tf_op jit(solution)/shard_map/ppermute | solution.py:106
  163.3 4.8 %collective-permute-start.21 = (f32[32,1,128]{2,0,1:T(8,128)}, f32[32,1,128]{2,0,1:T(8,128)}, u32[]{:S(2)}, u32[]{:S(2)}) collective-permute-start(f32[32,1,128]{2,0,1:T(8,128)} %get-tuple-element.107), channel_id=1, source_target_pairs={{1,0},{2,1},{3,2},{4,3},{5,4},{6,5},{7,6},{8,7},{9,8},{10,9},{11,1... | collective-permute-start | bytes 49160 | tf_op jit(solution)/shard_map/ppermute | solution.py:107
  169.8 15.2 %copy-start.23 = (s32[512]{0:T(512)S(1)}, s32[512]{0:T(512)}, u32[]{:S(2)}) copy-start(s32[512]{0:T(512)} %copy-done.22) | copy-start | bytes 6148
  173.8 49.3 %copy-start.21 = (f32[1,512]{1,0:T(1,128)S(1)}, f32[1,512]{1,0:T(1,128)}, u32[]{:S(2)}) copy-start(f32[1,512]{1,0:T(1,128)} %copy-done.20) | copy-start | bytes 6148
  178.2 18.1 %all-to-all-start.2 = ((f32[16,1,7]{2,1,0:T(1,128)}), f32[16,1,7]{2,1,0:T(1,128)S(1)}, u32[]{:S(2)}, u32[]{:S(2)}) async-start(f32[16,1,7]{2,1,0:T(1,128)} %broadcast_in_dim.19), calls=%async_computation.2 | async-start | bytes 16384 | tf_op jit(solution)/shard_map/all_to_all | solution.py:32
  197.3 21.6 %all-to-all-start.3 = ((f32[32,1,37]{2,1,0:T(1,128)}), f32[32,1,37]{2,1,0:T(1,128)S(1)}, u32[]{:S(2)}, u32[]{:S(2)}) async-start(f32[32,1,37]{2,1,0:T(1,128)} %broadcast_in_dim.20), calls=%async_computation.3 | async-start | bytes 32768 | tf_op jit(solution)/shard_map/all_to_all | solution.py:32
  223.8 15.3 %copy-start.9 = (f32[32,1,128]{2,0,1:T(8,128)S(1)}, f32[32,1,128]{2,0,1:T(8,128)}, u32[]{:S(2)}) copy-start(f32[32,1,128]{2,0,1:T(8,128)} %copy-done.7) | copy-start | bytes 49156
  223.8 15.3 %copy-start.12 = (f32[32,1,128]{2,0,1:T(8,128)S(1)}, f32[32,1,128]{2,0,1:T(8,128)}, u32[]{:S(2)}) copy-start(f32[32,1,128]{2,0,1:T(8,128)} %copy-done.10) | copy-start | bytes 49156
  223.8 15.3 %copy-start.15 = (f32[32,1,128]{2,0,1:T(8,128)S(1)}, f32[32,1,128]{2,0,1:T(8,128)}, u32[]{:S(2)}) copy-start(f32[32,1,128]{2,0,1:T(8,128)} %copy-done.14) | copy-start | bytes 49156
  223.8 15.3 %copy-start.17 = (f32[32,1,128]{2,0,1:T(8,128)S(1)}, f32[32,1,128]{2,0,1:T(8,128)}, u32[]{:S(2)}) copy-start(f32[32,1,128]{2,0,1:T(8,128)} %copy-done.16) | copy-start | bytes 49156
  (11 other events, 51.8 us)

commit v5 on v4

--- a/solution.py
+++ b/solution.py
@@ -132,7 +132,6 @@
     sine_y, value_y = sine_table(rows_y + 2)
     sine_z, value_z = sine_table(depth)
     inv_eig = 1.0 / (value_x[:, None, None] + value_y[None, :, None] + value_z[None, None, :])
-    my_slot = lax.dynamic_index_in_dim(index_map, lax.axis_index(("gx", "gy")), 0, keepdims=False)
     inverse = coarse_inverse.astype(jnp.float32)
     count_x = lax.axis_size("gx")
     count_y = lax.axis_size("gy")
@@ -143,10 +142,12 @@
         spectral = modal(wide, sine_x, sine_y, sine_z) * inv_eig
         return margin_sum(modal(spectral, sine_x, sine_y, sine_z))
 
+    permuted = jnp.transpose(jnp.transpose(inverse[index_map])[index_map])
+    me = lax.axis_index(("gx", "gy"))
+
     def coarse(gathered):
-        vec = jnp.zeros((subdomains,), jnp.float32).at[index_map].set(gathered)
-        sol = jnp.dot(inverse, vec, precision=high)
-        return vec, sol, lax.dynamic_index_in_dim(sol, my_slot, 0, keepdims=False)
+        sol = jnp.dot(permuted, gathered, precision=high)
+        return gathered, sol, lax.dynamic_index_in_dim(sol, me, 0, keepdims=False)
 
     def operate(direction, wide=None):
         if wide is None:
@@ -168,15 +169,9 @@
         ]
     )
 
+    every = exchange((jnp.sum(masked) / cells).reshape(1), jnp.zeros((0,), jnp.float32))[0]
+    vec0, sol0, value0 = coarse(every)
     local0 = local_solve(masked, both_wide[:, :, :depth])
-    every, partial = exchange(
-        jnp.concatenate([(jnp.sum(masked) / cells).reshape(1), k_row]),
-        jnp.sum(residual * fluid * local0).reshape(1),
-    )
-    every = every.reshape(subdomains, 6)
-    k_grid = every[:, 1:].reshape(count_x, count_y, 5)
-    vec0, sol0, value0 = coarse(every[:, 0])
-    energy_now = partial[0] + cells * jnp.sum(vec0 * sol0)
     precond = fluid * (local0 + value0)
     direction = precond
 
@@ -186,9 +181,10 @@
     fluid_local_w = fluid * local_w
     image_local_w = operate(fluid_local_w)
     every_w, partial = exchange(
-        jnp.stack([jnp.sum(masked_w) / cells, jnp.sum(fluid * image_local_w)]),
+        jnp.concatenate([jnp.stack([jnp.sum(masked_w) / cells, jnp.sum(fluid * image_local_w)]), k_row]),
         jnp.stack(
             [
+                jnp.sum(residual * fluid * local0),
                 jnp.sum(direction * image),
                 jnp.sum(residual * fluid * local_w),
                 jnp.sum(image * fluid * local0),
@@ -197,7 +193,10 @@
             ]
         ),
     )
-    every_w = every_w.reshape(subdomains, 2)
+    energy_now = partial[0] + cells * jnp.sum(vec0 * sol0)
+    partial = partial[1:]
+    every_w = every_w.reshape(subdomains, 7)
+    k_grid = every_w[:, 2:].reshape(count_x, count_y, 5)
     vec_w, sol_w, value_w = coarse(every_w[:, 0])
     delta_now = partial[0]
     step_size = energy_now / delta_now
@@ -211,7 +210,7 @@
     precond = precond - step_size * (fluid * (local_w + value_w))
     direction = precond + ratio * direction
 
-    coarse_w = sol_w[index_map]
+    coarse_w = sol_w
     grid_w = coarse_w.reshape(count_x, count_y)
     near_w = jnp.stack(
         [

time: 255 us -> 246 us (0.965)
  waiting for transfers between devices: 42 us -> 26.4 us
  starting transfers between devices: 94.2 us -> 107 us
  blocking collectives: 26 us -> 21.6 us
    all_to_all x3, waiting for transfers between devices: 20.1 us -> 4.92 us  [exchange(): lax.all_to_all(jnp.broadcast_to(stage[None], (count,) + stage.shape), axi...]
    all_to_all x3, starting transfers between devices: 32.3 us -> 41.5 us  [exchange(): lax.all_to_all(jnp.broadcast_to(stage[None], (count,) + stage.shape), axi...]
    scatter x2 -> x0, local copies, waits for them, and re-layouts: 5.01 us -> none  [coarse(): vec = jnp.zeros((subdomains,), jnp.float32).at[index_map].set(gathered)]
    all_to_all x1, blocking collectives: 26 us -> 21.6 us  [exchange(): lax.all_to_all(jnp.broadcast_to(stage[None], (count,) + stage.shape), axi...]
    ppermute x4, starting transfers between devices: 9.96 us -> 6.43 us  [with_halo(): lax.ppermute(head, axis, [((i + 1) % count, i) for i in range(ends)])]
    ppermute x4, starting transfers between devices: 14.2 us -> 17.2 us  [with_halo(): lax.ppermute(tail, axis, [(i, (i + 1) % count) for i in range(ends)])]
    unnamed x70 -> x56, local copies, waits for them, and re-layouts: 3.75 us -> 5.15 us
    concatenate x2 -> x1, local copies, waits for them, and re-layouts: 5.15 us -> 5.15 us  [exchange(): stage = jnp.concatenate([gathered, summed])]
  transfers between devices with their start and end apart: 27 -> 27, of which waited for: 13 -> 8; matrix products, arithmetic and copies ran while one was open for 4% -> 7% of each run, Pallas kernels for 0% -> 0%
where the time goes in v5:
time: 246 us; the launch traced here: 244 us
  starting transfers between devices  107 us (43%)
  local copies, waits for them, and re-layouts  33.1 us (13%)
  other arithmetic  31 us (13%)
  waiting for transfers between devices  26.4 us (11%)
  blocking collectives  21.6 us (9%)
  between operations  13.5 us (5%)
  matrix products  11.5 us (5%)
    all_to_all x3, starting transfers between devices, exchange(): lax.all_to_all(jnp.broadcast_to(stage[None], (count,) + stage.shape), axi...  41.5 us
    all_to_all x1, blocking collectives, exchange(): lax.all_to_all(jnp.broadcast_to(stage[None], (count,) + stage.shape), axi...  21.6 us
    ppermute x4, starting transfers between devices, with_halo(): lax.ppermute(tail, axis, [(i, (i + 1) % count) for i in range(ends)])  17.2 us
    ppermute x4, waiting for transfers between devices, with_halo(): lax.ppermute(head, axis, [((i + 1) % count, i) for i in range(ends)])  10 us
    ppermute x2, starting transfers between devices, face_halo(): low_x = lax.ppermute(cells[-1:], 'gx', up_x)  8.43 us
    ppermute x2, starting transfers between devices, margin_sum(): from_left = lax.ppermute(body_rows[:, -1:], 'gy', up_y)  7.63 us
    ppermute x2, starting transfers between devices, margin_sum(): from_low = lax.ppermute(block[-1:], 'gx', up_x)  6.63 us
    ppermute x4, starting transfers between devices, with_halo(): lax.ppermute(head, axis, [((i + 1) % count, i) for i in range(ends)])  6.43 us
  transfers between devices with their start and end apart: 27, of which 8 were waited for; matrix products, arithmetic and copies ran while one was open for 7% of the time, Pallas kernels for 0%

profile of v5, /device:TPU:1, one launch (start us, length us, event | category | flops | bytes accessed | tf_op | source)
XLA Modules:
  0.0 244.0 jit_solution(9666019973191817972)
XLA Ops:
  1.5 2.0 fusion.176
  4.8 15.7 %all-to-all-start = ((f32[16,1,1]{2,1,0:T(1,128)}), f32[16,1,1]{2,1,0:T(1,128)S(1)}, u32[]{:S(2)}, u32[]{:S(2)}) async-start(f32[16,1,1]{2,1,0:T(1,128)} %broadcast_in_dim.19), calls=%async_computation | async-start | bytes 16384 | tf_op jit(solution)/shard_map/all_to_all | solution.py:32
  20.8 4.0 %collective-permute-start = (f32[1,32,256]{2,0,1:T(1,128)S(1)}, f32[1,32,256]{2,0,1:T(1,128)S(1)}, u32[]{:S(2)}, u32[]{:S(2)}) collective-permute-start(f32[1,32,256]{2,0,1:T(1,128)S(1)} %get-tuple-element.100), channel_id=1, source_target_pairs={{0,16},{16,32},{32,48},{48,64},{64,80},{80,96},{96,112},{112,128},... | collective-permute-start | bytes 98312 | tf_op jit(solution)/shard_map/ppermute | solution.py:17
  24.8 1.9 collective-permute-start.1
  27.0 3.4 %collective-permute-done.1 = f32[1,32,256]{2,0,1:T(1,128)S(1)} collective-permute-done((f32[1,32,256]{2,0,1:T(1,128)S(1)}, f32[1,32,256]{2,0,1:T(1,128)S(1)}, u32[]{:S(2)}, u32[]{:S(2)}) %collective-permute-start.1) | collective-permute-done | bytes 32800 | tf_op jit(solution)/shard_map/ppermute | solution.py:19
  30.4 3.6 %collective-permute-start.2 = (f32[34,1,256]{2,0,1:T(8,128)S(1)}, f32[34,1,256]{2,0,1:T(8,128)S(1)}, u32[]{:S(2)}, u32[]{:S(2)}) collective-permute-start(f32[34,1,256]{2,0,1:T(8,128)S(1)} %get-tuple-element.98), channel_id=1, source_target_pairs={{0,1},{1,2},{2,3},{3,4},{4,5},{5,6},{6,7},{7,8},{8,9},{9,10},{10,1... | collective-permute-start | bytes 104456 | tf_op jit(solution)/shard_map/ppermute | solution.py:17
  36.1 8.4 %all-to-all-start.1 = ((f32[32,1,16]{2,1,0:T(1,128)}), f32[32,1,16]{2,1,0:T(1,128)S(1)}, u32[]{:S(2)}, u32[]{:S(2)}) async-start(f32[32,1,16]{2,1,0:T(1,128)} %broadcast_in_dim.21), calls=%async_computation.1 | async-start | bytes 32768 | tf_op jit(solution)/shard_map/all_to_all | solution.py:32
  51.1 3.5 %collective-permute-start.4 = (f32[1,34,128]{2,0,1:T(1,128)S(1)}, f32[1,34,128]{2,0,1:T(1,128)S(1)}, u32[]{:S(2)}, u32[]{:S(2)}) collective-permute-start(f32[1,34,128]{2,0,1:T(1,128)S(1)} %get-tuple-element.104), channel_id=1, source_target_pairs={{0,16},{16,32},{32,48},{48,64},{64,80},{80,96},{96,112},{112,128},... | collective-permute-start | bytes 52232 | tf_op jit(solution)/shard_map/ppermute | solution.py:84
  54.7 1.9 collective-permute-start.5
  56.7 2.0 gather_fusion
  58.9 2.0 gather_fusion.1
  63.5 4.0 %collective-permute-start.6 = (f32[32,1,128]{2,0,1:T(8,128)S(1)}, f32[32,1,128]{2,0,1:T(8,128)S(1)}, u32[]{:S(2)}, u32[]{:S(2)}) collective-permute-start(f32[32,1,128]{2,0,1:T(8,128)S(1)} %get-tuple-element.111), channel_id=1, source_target_pairs={{0,1},{1,2},{2,3},{3,4},{4,5},{5,6},{6,7},{7,8},{8,9},{9,10},{10,1... | collective-permute-start | bytes 49160 | tf_op jit(solution)/shard_map/ppermute | solution.py:89
  69.7 2.2 collective-permute-done.7
  72.8 5.1 %collective-permute-start.11 = (f32[1,32,128]{2,0,1:T(1,128)S(1)}, f32[1,32,128]{2,0,1:T(1,128)S(1)}, u32[]{:S(2)}, u32[]{:S(2)}) collective-permute-start(f32[1,32,128]{2,0,1:T(1,128)S(1)} %get-tuple-element.121), channel_id=1, source_target_pairs={{0,16},{16,32},{32,48},{48,64},{64,80},{80,96},{96,112},{112,128},... | collective-permute-start | bytes 49160 | tf_op jit(solution)/shard_map/ppermute | solution.py:104
  77.9 1.9 collective-permute-start.10
  79.9 3.2 %collective-permute-start.8 = (f32[32,1,128]{2,0,1:T(8,128)S(1)}, f32[32,1,128]{2,0,1:T(8,128)S(1)}, u32[]{:S(2)}, u32[]{:S(2)}) collective-permute-start(f32[32,1,128]{2,0,1:T(8,128)S(1)} %get-tuple-element.119), channel_id=1, source_target_pairs={{0,1},{1,2},{2,3},{3,4},{4,5},{5,6},{6,7},{7,8},{8,9},{9,10},{10,1... | collective-permute-start | bytes 49160 | tf_op jit(solution)/shard_map/ppermute | solution.py:106
  83.0 1.5 collective-permute-start.9
  85.0 3.7 %collective-permute-done.9 = f32[32,1,128]{2,0,1:T(8,128)S(1)} collective-permute-done((f32[32,1,128]{2,0,1:T(8,128)S(1)}, f32[32,1,128]{2,0,1:T(8,128)S(1)}, u32[]{:S(2)}, u32[]{:S(2)}) %collective-permute-start.9) | collective-permute-done | bytes 16416 | tf_op jit(solution)/shard_map/ppermute | solution.py:107
  89.3 2.6 %multiply_reduce_fusion.4 = (f32[]{:T(128)}, f32[32,32,128]{2,0,1:T(8,128)S(1)}) fusion(f32[32,32,128]{2,0,1:T(8,128)S(1)} %add_multiply_fusion, f32[34,34,130]{2,0,1:T(8,128)S(1)} %select_maximum_fusion.4, f32[32,1,128]{2,0,1:T(8,128)S(1)} %collective-permute-done.8, f32[32,1,128]{2,0,1:T(8,128)S(1)} %collective-permute-done.9, ...), kind=kLoop, calls=%fused_computation.139 | loop fusion | flops 4456447 | bytes 5314564 | tf_op jit(solution)/shard_map/reduce_sum | solution.py:188
  92.2 4.8 %collective-permute-start.12 = (f32[1,32,128]{2,0,1:T(1,128)S(1)}, f32[1,32,128]{2,0,1:T(1,128)S(1)}, u32[]{:S(2)}, u32[]{:S(2)}) collective-permute-start(f32[1,32,128]{2,0,1:T(1,128)S(1)} %get-tuple-element.117), channel_id=1, source_target_pairs={{0,16},{16,32},{32,48},{48,64},{64,80},{80,96},{96,112},{112,128},... | collective-permute-start | bytes 49160 | tf_op jit(solution)/shard_map/ppermute | solution.py:17
  97.0 1.9 collective-permute-start.13
  98.9 3.1 %collective-permute-done.13 = f32[1,32,128]{2,0,1:T(1,128)S(1)} collective-permute-done((f32[1,32,128]{2,0,1:T(1,128)S(1)}, f32[1,32,128]{2,0,1:T(1,128)S(1)}, u32[]{:S(2)}, u32[]{:S(2)}) %collective-permute-start.13) | collective-permute-done | bytes 16416 | tf_op jit(solution)/shard_map/ppermute | solution.py:19
  102.0 4.8 %collective-permute-start.14 = (f32[34,1,128]{2,0,1:T(8,128)S(1)}, f32[34,1,128]{2,0,1:T(8,128)S(1)}, u32[]{:S(2)}, u32[]{:S(2)}) collective-permute-start(f32[34,1,128]{2,0,1:T(8,128)S(1)} %get-tuple-element.109), channel_id=1, source_target_pairs={{0,1},{1,2},{2,3},{3,4},{4,5},{5,6},{6,7},{7,8},{8,9},{9,10},{10,1... | collective-permute-start | bytes 52232 | tf_op jit(solution)/shard_map/ppermute | solution.py:17
  108.2 3.5 %collective-permute-done.15 = f32[34,1,128]{2,0,1:T(8,128)S(1)} collective-permute-done((f32[34,1,128]{2,0,1:T(8,128)S(1)}, f32[34,1,128]{2,0,1:T(8,128)S(1)}, u32[]{:S(2)}, u32[]{:S(2)}) %collective-permute-start.15) | collective-permute-done | bytes 17440 | tf_op jit(solution)/shard_map/ppermute | solution.py:19
  117.3 3.1 %collective-permute-start.16 = (f32[1,34,128]{2,0,1:T(1,128)S(1)}, f32[1,34,128]{2,0,1:T(1,128)S(1)}, u32[]{:S(2)}, u32[]{:S(2)}) collective-permute-start(f32[1,34,128]{2,0,1:T(1,128)S(1)} %get-tuple-element.102), channel_id=1, source_target_pairs={{0,16},{16,32},{32,48},{48,64},{64,80},{80,96},{96,112},{112,128},... | collective-permute-start | bytes 52232 | tf_op jit(solution)/shard_map/ppermute | solution.py:84
  120.3 1.9 collective-permute-start.17
  122.3 3.1 %collective-permute-done.17 = f32[1,34,128]{2,0,1:T(1,128)S(1)} collective-permute-done((f32[1,34,128]{2,0,1:T(1,128)S(1)}, f32[1,34,128]{2,0,1:T(1,128)S(1)}, u32[]{:S(2)}, u32[]{:S(2)}) %collective-permute-start.17) | collective-permute-done | bytes 17440 | tf_op jit(solution)/shard_map/ppermute | solution.py:85
  125.5 3.6 %collective-permute-start.18 = (f32[32,1,128]{2,0,1:T(8,128)S(1)}, f32[32,1,128]{2,0,1:T(8,128)S(1)}, u32[]{:S(2)}, u32[]{:S(2)}) collective-permute-start(f32[32,1,128]{2,0,1:T(8,128)S(1)} %get-tuple-element.107), channel_id=1, source_target_pairs={{0,1},{1,2},{2,3},{3,4},{4,5},{5,6},{6,7},{7,8},{8,9},{9,10},{10,1... | collective-permute-start | bytes 49160 | tf_op jit(solution)/shard_map/ppermute | solution.py:89
  131.3 2.4 collective-permute-done.19
  134.8 3.4 %collective-permute-start.23 = (f32[1,32,128]{2,0,1:T(1,128)S(1)}, f32[1,32,128]{2,0,1:T(1,128)S(1)}, u32[]{:S(2)}, u32[]{:S(2)}) collective-permute-start(f32[1,32,128]{2,0,1:T(1,128)S(1)} %get-tuple-element.115), channel_id=1, source_target_pairs={{0,16},{16,32},{32,48},{48,64},{64,80},{80,96},{96,112},{112,128},... | collective-permute-start | bytes 49160 | tf_op jit(solution)/shard_map/ppermute | solution.py:104
  138.2 1.9 collective-permute-start.22
  140.1 2.8 %collective-permute-start.20 = (f32[32,1,128]{2,0,1:T(8,128)S(1)}, f32[32,1,128]{2,0,1:T(8,128)S(1)}, u32[]{:S(2)}, u32[]{:S(2)}) collective-permute-start(f32[32,1,128]{2,0,1:T(8,128)S(1)} %get-tuple-element.113), channel_id=1, source_target_pairs={{0,1},{1,2},{2,3},{3,4},{4,5},{5,6},{6,7},{7,8},{8,9},{9,10},{10,1... | collective-permute-start | bytes 49160 | tf_op jit(solution)/shard_map/ppermute | solution.py:106
  148.3 1.7 select_maximum_fusion
  150.0 3.9 %multiply_reduce_fusion = (f32[]{:T(128)}, f32[]{:T(128)}, f32[]{:T(128)}, f32[32,32,128]{2,0,1:T(8,128)}) fusion(f32[32,32,128]{2,0,1:T(8,128)S(1)} %copy-done.3, s32[32,32]{0,1:T(8,128)S(1)} %copy.51, f32[34,34,128]{2,0,1:T(8,128)S(1)} %pad.109, f32[34,34,130]{2,0,1:T(8,128)S(1)} %maximum_subtract_fusion, f32[34,34,130]{2,0,1:T(8,128)S(1)} %select_maximum_fusion, ...), kind=kLoop, calls=%fused_computation.135 | loop fusion | flops 7077885 | bytes 8120332 | tf_op jit(solution)/shard_map/reduce_sum | solution.py:192
  153.9 5.2 %concatenate.93 = f32[13]{0:T(128)S(1)} concatenate(f32[1]{0:T(128)} %bitcast.8, f32[1]{0:T(128)} %bitcast.11, f32[1]{0:T(128)} %bitcast.12, f32[1]{0:T(128)} %bitcast.13, f32[1]{0:T(128)} %bitcast.14, f32[1]{0:T(128)} %bitcast.15, f32[1]{0:T(128)} %bitcast.16, f32[1]{0:T(128)} %bitcast.17, f32[1]{0:T(128)} %bitcast.18, f32[1]{0:T(128)} %bitcast.19, f32[1]{0:T(128)} %bitcast.20, ...), dimensions={0} | concatenate | bytes 104 | tf_op jit(solution)/shard_map/concatenate | solution.py:29
  159.1 21.6 %all_to_all.30 = f32[16,1,13]{2,1,0:T(1,128)S(1)} all-to-all(f32[16,1,13]{2,1,0:T(1,128)S(1)} %broadcast_in_dim.22), channel_id=1, replica_groups=mesh['gx'=32,'gy'=16] {'gy'}, dimensions={0} | all-to-all | bytes 1664 | tf_op jit(solution)/shard_map/all_to_all | solution.py:32
  181.6 17.4 %all-to-all-start.3 = ((f32[32,1,118]{2,1,0:T(1,128)}), f32[32,1,118]{2,1,0:T(1,128)S(1)}, u32[]{:S(2)}, u32[]{:S(2)}) async-start(f32[32,1,118]{2,1,0:T(1,128)} %broadcast_in_dim.23), calls=%async_computation.3 | async-start | bytes 32768 | tf_op jit(solution)/shard_map/all_to_all | solution.py:32
  199.6 1.4 reshape.336
  201.0 4.9 %all-to-all-done.3 = f32[32,1,118]{2,1,0:T(1,128)S(1)} async-done(((f32[32,1,118]{2,1,0:T(1,128)}), f32[32,1,118]{2,1,0:T(1,128)S(1)}, u32[]{:S(2)}, u32[]{:S(2)}) %all-to-all-start.3) | async-done | bytes 15136 | tf_op jit(solution)/shard_map/all_to_all | solution.py:32
  206.5 1.7 reshape_reshape.3
  208.2 1.9 slice_reduce_fusion
  210.1 1.8 slice.644
  214.5 1.5 fusion.191
  215.9 1.4 multiply_reduce_fusion.8
  230.0 3.8 %broadcast_multiply_fusion = (f32[32,32,128]{2,0,1:T(8,128)S(1)}, f32[32,32,128]{2,0,1:T(8,128)}) fusion(f32[]{:T(128)} %bitcast.38, s32[32,32]{0,1:T(8,128)} %copy-done.12, f32[]{:T(128)S(6)} %div.81, f32[]{:T(128)} %bitcast.33, f32[32,1,128]{2,0,1:T(8,128)} %copy-done.20, f32[32,1,128]{2,0,1:T(8,128)} %copy-done.19, f32[32,34,128]{2,0,1:T(8,128)S(1)} %copy-done.5, ...), kind=kLoop, calls=%fused_computation.150 | loop fusion | flops 2490368 | bytes 2166808 | tf_op jit(solution)/shard_map/mul | solution.py:237
  233.8 1.3 slice_multiply_fusion.12
  235.1 1.4 slice_multiply_fusion.14
  238.4 3.3 %fusion.45 = f32[32,32,128]{2,0,1:T(8,128)S(1)} fusion(f32[32,32,128]{2,0,1:T(8,128)} %get-tuple-element.91, f32[34,34,128]{2,0,1:T(8,128)S(1)} %scatter.24, f32[32,32,128]{2,0,1:T(8,128)S(1)} %copy-done.9, f32[32,32,128]{2,1,0:T(8,128)} %param.14, f32[34,34,130]{2,0,1:T(8,128)S(1)} %maximum_subtract_fusion, f32[]{:T(128)S(6)} %add.394, f32[]{:T(128)S(6)} %div.82, ...), kind=kLoop, calls=%fused_computation.72 | loop fusion | flops 4456448 | bytes 8052752 | tf_op jit(solution)/shard_map/sub | solution.py:242
  (174 shorter events, 43.3 us)
Async XLA Ops:
  0.6 56.1 %copy-start = (bf16[512,512]{1,0:T(8,128)(2,1)S(1)}, bf16[512,512]{1,0:T(8,128)(2,1)}, u32[]{:S(2)}) copy-start(bf16[512,512]{1,0:T(8,128)(2,1)} %param.17) | copy-start | bytes 1572868
  0.6 26.2 %copy-start.23 = (s32[512]{0:T(512)S(1)}, s32[512]{0:T(512)}, u32[]{:S(2)}) copy-start(s32[512]{0:T(512)} %param.16) | copy-start | bytes 6148
  1.5 148.5 %copy-start.12 = (s32[32,32]{0,1:T(8,128)}, s32[32,32]{0,1:T(8,128)S(1)}, u32[]{:S(2)}) copy-start(s32[32,32]{0,1:T(8,128)S(1)} %copy.51) | copy-start | bytes 12292
  4.8 30.5 %all-to-all-start = ((f32[16,1,1]{2,1,0:T(1,128)}), f32[16,1,1]{2,1,0:T(1,128)S(1)}, u32[]{:S(2)}, u32[]{:S(2)}) async-start(f32[16,1,1]{2,1,0:T(1,128)} %broadcast_in_dim.19), calls=%async_computation | async-start | bytes 16384 | tf_op jit(solution)/shard_map/all_to_all | solution.py:32
  20.8 6.2 %collective-permute-start = (f32[1,32,256]{2,0,1:T(1,128)S(1)}, f32[1,32,256]{2,0,1:T(1,128)S(1)}, u32[]{:S(2)}, u32[]{:S(2)}) collective-permute-start(f32[1,32,256]{2,0,1:T(1,128)S(1)} %get-tuple-element.100), channel_id=1, source_target_pairs={{0,16},{16,32},{32,48},{48,64},{64,80},{80,96},{96,112},{112,128},... | collective-permute-start | bytes 98312 | tf_op jit(solution)/shard_map/ppermute | solution.py:17
  24.8 5.5 %collective-permute-start.1 = (f32[1,32,256]{2,0,1:T(1,128)S(1)}, f32[1,32,256]{2,0,1:T(1,128)S(1)}, u32[]{:S(2)}, u32[]{:S(2)}) collective-permute-start(f32[1,32,256]{2,0,1:T(1,128)S(1)} %get-tuple-element.101), channel_id=1, source_target_pairs={{16,0},{32,16},{48,32},{64,48},{80,64},{96,80},{112,96},{128,112},... | collective-permute-start | bytes 98312 | tf_op jit(solution)/shard_map/ppermute | solution.py:19
  30.4 14.1 %collective-permute-start.2 = (f32[34,1,256]{2,0,1:T(8,128)S(1)}, f32[34,1,256]{2,0,1:T(8,128)S(1)}, u32[]{:S(2)}, u32[]{:S(2)}) collective-permute-start(f32[34,1,256]{2,0,1:T(8,128)S(1)} %get-tuple-element.98), channel_id=1, source_target_pairs={{0,1},{1,2},{2,3},{3,4},{4,5},{5,6},{6,7},{7,8},{8,9},{9,10},{10,1... | collective-permute-start | bytes 104456 | tf_op jit(solution)/shard_map/ppermute | solution.py:17
  34.0 10.6 %collective-permute-start.3 = (f32[34,1,256]{2,0,1:T(8,128)S(1)}, f32[34,1,256]{2,0,1:T(8,128)S(1)}, u32[]{:S(2)}, u32[]{:S(2)}) collective-permute-start(f32[34,1,256]{2,0,1:T(8,128)S(1)} %get-tuple-element.99), channel_id=1, source_target_pairs={{1,0},{2,1},{3,2},{4,3},{5,4},{6,5},{7,6},{8,7},{9,8},{10,9},{11,1... | collective-permute-start | bytes 104456 | tf_op jit(solution)/shard_map/ppermute | solution.py:19
  36.1 24.8 %all-to-all-start.1 = ((f32[32,1,16]{2,1,0:T(1,128)}), f32[32,1,16]{2,1,0:T(1,128)S(1)}, u32[]{:S(2)}, u32[]{:S(2)}) async-start(f32[32,1,16]{2,1,0:T(1,128)} %broadcast_in_dim.21), calls=%async_computation.1 | async-start | bytes 32768 | tf_op jit(solution)/shard_map/all_to_all | solution.py:32
  44.7 1.7 copy-start.1
  51.1 11.1 %collective-permute-start.4 = (f32[1,34,128]{2,0,1:T(1,128)S(1)}, f32[1,34,128]{2,0,1:T(1,128)S(1)}, u32[]{:S(2)}, u32[]{:S(2)}) collective-permute-start(f32[1,34,128]{2,0,1:T(1,128)S(1)} %get-tuple-element.104), channel_id=1, source_target_pairs={{0,16},{16,32},{32,48},{48,64},{64,80},{80,96},{96,112},{112,128},... | collective-permute-start | bytes 52232 | tf_op jit(solution)/shard_map/ppermute | solution.py:84
  54.7 7.6 %collective-permute-start.5 = (f32[1,34,128]{2,0,1:T(1,128)S(1)}, f32[1,34,128]{2,0,1:T(1,128)S(1)}, u32[]{:S(2)}, u32[]{:S(2)}) collective-permute-start(f32[1,34,128]{2,0,1:T(1,128)S(1)} %get-tuple-element.105), channel_id=1, source_target_pairs={{16,0},{32,16},{48,32},{64,48},{80,64},{96,80},{112,96},{128,112},... | collective-permute-start | bytes 52232 | tf_op jit(solution)/shard_map/ppermute | solution.py:85
  60.9 8.9 %copy-start.6 = (bf16[512,512]{1,0:T(8,128)(2,1)}, bf16[512,512]{1,0:T(8,128)(2,1)S(1)}, u32[]{:S(2)}) copy-start(bf16[512,512]{1,0:T(8,128)(2,1)S(1)} %gather_fusion.1) | copy-start | bytes 1572868
  60.9 1.4 copy-start.17
  63.5 6.3 %collective-permute-start.6 = (f32[32,1,128]{2,0,1:T(8,128)S(1)}, f32[32,1,128]{2,0,1:T(8,128)S(1)}, u32[]{:S(2)}, u32[]{:S(2)}) collective-permute-start(f32[32,1,128]{2,0,1:T(8,128)S(1)} %get-tuple-element.111), channel_id=1, source_target_pairs={{0,1},{1,2},{2,3},{3,4},{4,5},{5,6},{6,7},{7,8},{8,9},{9,10},{10,1... | collective-permute-start | bytes 49160 | tf_op jit(solution)/shard_map/ppermute | solution.py:89
  67.5 4.5 %collective-permute-start.7 = (f32[32,1,128]{2,0,1:T(8,128)S(1)}, f32[32,1,128]{2,0,1:T(8,128)S(1)}, u32[]{:S(2)}, u32[]{:S(2)}) collective-permute-start(f32[32,1,128]{2,0,1:T(8,128)S(1)} %get-tuple-element.112), channel_id=1, source_target_pairs={{1,0},{2,1},{3,2},{4,3},{5,4},{6,5},{7,6},{8,7},{9,8},{10,9},{11,1... | collective-permute-start | bytes 49160 | tf_op jit(solution)/shard_map/ppermute | solution.py:90
  69.1 3.8 %copy-start.22 = (f32[1,512]{1,0:T(1,128)}, f32[1,512]{1,0:T(1,128)S(1)}, u32[]{:S(2)}) copy-start(f32[1,512]{1,0:T(1,128)S(1)} %fusion.78) | copy-start | bytes 6148
  69.1 15.5 %slice-start = ((f32[34,34,256]{2,0,1:T(8,128)}), f32[34,34,128]{2,0,1:T(8,128)S(1)}, s32[]{:S(2)}) async-start(f32[34,34,256]{2,0,1:T(8,128)} %copy-done.1), calls=%async_computation.4 | async-start | bytes 1392640 | tf_op jit(solution)/shard_map/slice | solution.py:124
  69.7 63.9 %copy-start.14 = (f32[32,1,128]{2,0,1:T(8,128)}, f32[32,1,128]{2,0,1:T(8,128)S(1)}, u32[]{:S(2)}) copy-start(f32[32,1,128]{2,0,1:T(8,128)S(1)} %collective-permute-done.6) | copy-start | bytes 49156
  71.9 61.7 %copy-start.15 = (f32[32,1,128]{2,0,1:T(8,128)}, f32[32,1,128]{2,0,1:T(8,128)S(1)}, u32[]{:S(2)}) copy-start(f32[32,1,128]{2,0,1:T(8,128)S(1)} %collective-permute-done.7) | copy-start | bytes 49156
  72.8 12.1 %collective-permute-start.11 = (f32[1,32,128]{2,0,1:T(1,128)S(1)}, f32[1,32,128]{2,0,1:T(1,128)S(1)}, u32[]{:S(2)}, u32[]{:S(2)}) collective-permute-start(f32[1,32,128]{2,0,1:T(1,128)S(1)} %get-tuple-element.121), channel_id=1, source_target_pairs={{0,16},{16,32},{32,48},{48,64},{64,80},{80,96},{96,112},{112,128},... | collective-permute-start | bytes 49160 | tf_op jit(solution)/shard_map/ppermute | solution.py:104
  77.9 7.1 %collective-permute-start.10 = (f32[1,32,128]{2,0,1:T(1,128)S(1)}, f32[1,32,128]{2,0,1:T(1,128)S(1)}, u32[]{:S(2)}, u32[]{:S(2)}) collective-permute-start(f32[1,32,128]{2,0,1:T(1,128)S(1)} %get-tuple-element.122), channel_id=1, source_target_pairs={{16,0},{32,16},{48,32},{64,48},{80,64},{96,80},{112,96},{128,112},... | collective-permute-start | bytes 49160 | tf_op jit(solution)/shard_map/ppermute | solution.py:105
  79.9 5.2 %collective-permute-start.8 = (f32[32,1,128]{2,0,1:T(8,128)S(1)}, f32[32,1,128]{2,0,1:T(8,128)S(1)}, u32[]{:S(2)}, u32[]{:S(2)}) collective-permute-start(f32[32,1,128]{2,0,1:T(8,128)S(1)} %get-tuple-element.119), channel_id=1, source_target_pairs={{0,1},{1,2},{2,3},{3,4},{4,5},{5,6},{6,7},{7,8},{8,9},{9,10},{10,1... | collective-permute-start | bytes 49160 | tf_op jit(solution)/shard_map/ppermute | solution.py:106
  83.0 5.7 %collective-permute-start.9 = (f32[32,1,128]{2,0,1:T(8,128)S(1)}, f32[32,1,128]{2,0,1:T(8,128)S(1)}, u32[]{:S(2)}, u32[]{:S(2)}) collective-permute-start(f32[32,1,128]{2,0,1:T(8,128)S(1)} %get-tuple-element.120), channel_id=1, source_target_pairs={{1,0},{2,1},{3,2},{4,3},{5,4},{6,5},{7,6},{8,7},{9,8},{10,9},{11,1... | collective-permute-start | bytes 49160 | tf_op jit(solution)/shard_map/ppermute | solution.py:107
  91.9 20.7 %copy-start.8 = (f32[32,32,128]{2,0,1:T(8,128)}, f32[32,32,128]{2,0,1:T(8,128)S(1)}, u32[]{:S(2)}) copy-start(f32[32,32,128]{2,0,1:T(8,128)S(1)} %get-tuple-element.90) | copy-start | bytes 1572868
  92.2 6.7 %collective-permute-start.12 = (f32[1,32,128]{2,0,1:T(1,128)S(1)}, f32[1,32,128]{2,0,1:T(1,128)S(1)}, u32[]{:S(2)}, u32[]{:S(2)}) collective-permute-start(f32[1,32,128]{2,0,1:T(1,128)S(1)} %get-tuple-element.117), channel_id=1, source_target_pairs={{0,16},{16,32},{32,48},{48,64},{64,80},{80,96},{96,112},{112,128},... | collective-permute-start | bytes 49160 | tf_op jit(solution)/shard_map/ppermute | solution.py:17
  97.0 5.1 %collective-permute-start.13 = (f32[1,32,128]{2,0,1:T(1,128)S(1)}, f32[1,32,128]{2,0,1:T(1,128)S(1)}, u32[]{:S(2)}, u32[]{:S(2)}) collective-permute-start(f32[1,32,128]{2,0,1:T(1,128)S(1)} %get-tuple-element.118), channel_id=1, source_target_pairs={{16,0},{32,16},{48,32},{64,48},{80,64},{96,80},{112,96},{128,112},... | collective-permute-start | bytes 49160 | tf_op jit(solution)/shard_map/ppermute | solution.py:19
  102.0 6.2 %collective-permute-start.14 = (f32[34,1,128]{2,0,1:T(8,128)S(1)}, f32[34,1,128]{2,0,1:T(8,128)S(1)}, u32[]{:S(2)}, u32[]{:S(2)}) collective-permute-start(f32[34,1,128]{2,0,1:T(8,128)S(1)} %get-tuple-element.109), channel_id=1, source_target_pairs={{0,1},{1,2},{2,3},{3,4},{4,5},{5,6},{6,7},{7,8},{8,9},{9,10},{10,1... | collective-permute-start | bytes 52232 | tf_op jit(solution)/shard_map/ppermute | solution.py:17
  106.9 4.8 %collective-permute-start.15 = (f32[34,1,128]{2,0,1:T(8,128)S(1)}, f32[34,1,128]{2,0,1:T(8,128)S(1)}, u32[]{:S(2)}, u32[]{:S(2)}) collective-permute-start(f32[34,1,128]{2,0,1:T(8,128)S(1)} %get-tuple-element.110), channel_id=1, source_target_pairs={{1,0},{2,1},{3,2},{4,3},{5,4},{6,5},{7,6},{8,7},{9,8},{10,9},{11,1... | collective-permute-start | bytes 52232 | tf_op jit(solution)/shard_map/ppermute | solution.py:19
  117.3 5.0 %collective-permute-start.16 = (f32[1,34,128]{2,0,1:T(1,128)S(1)}, f32[1,34,128]{2,0,1:T(1,128)S(1)}, u32[]{:S(2)}, u32[]{:S(2)}) collective-permute-start(f32[1,34,128]{2,0,1:T(1,128)S(1)} %get-tuple-element.102), channel_id=1, source_target_pairs={{0,16},{16,32},{32,48},{48,64},{64,80},{80,96},{96,112},{112,128},... | collective-permute-start | bytes 52232 | tf_op jit(solution)/shard_map/ppermute | solution.py:84
  120.3 5.1 %collective-permute-start.17 = (f32[1,34,128]{2,0,1:T(1,128)S(1)}, f32[1,34,128]{2,0,1:T(1,128)S(1)}, u32[]{:S(2)}, u32[]{:S(2)}) collective-permute-start(f32[1,34,128]{2,0,1:T(1,128)S(1)} %get-tuple-element.103), channel_id=1, source_target_pairs={{16,0},{32,16},{48,32},{64,48},{80,64},{96,80},{112,96},{128,112},... | collective-permute-start | bytes 52232 | tf_op jit(solution)/shard_map/ppermute | solution.py:85
  125.5 9.2 %copy-start.4 = (f32[32,34,128]{2,0,1:T(8,128)}, f32[32,34,128]{2,0,1:T(8,128)S(1)}, u32[]{:S(2)}) copy-start(f32[32,34,128]{2,0,1:T(8,128)S(1)} %fusion.25) | copy-start | bytes 1671172
  125.5 5.8 %collective-permute-start.18 = (f32[32,1,128]{2,0,1:T(8,128)S(1)}, f32[32,1,128]{2,0,1:T(8,128)S(1)}, u32[]{:S(2)}, u32[]{:S(2)}) collective-permute-start(f32[32,1,128]{2,0,1:T(8,128)S(1)} %get-tuple-element.107), channel_id=1, source_target_pairs={{0,1},{1,2},{2,3},{3,4},{4,5},{5,6},{6,7},{7,8},{8,9},{9,10},{10,1... | collective-permute-start | bytes 49160 | tf_op jit(solution)/shard_map/ppermute | solution.py:89
  129.2 4.5 %collective-permute-start.19 = (f32[32,1,128]{2,0,1:T(8,128)S(1)}, f32[32,1,128]{2,0,1:T(8,128)S(1)}, u32[]{:S(2)}, u32[]{:S(2)}) collective-permute-start(f32[32,1,128]{2,0,1:T(8,128)S(1)} %get-tuple-element.108), channel_id=1, source_target_pairs={{1,0},{2,1},{3,2},{4,3},{5,4},{6,5},{7,6},{8,7},{9,8},{10,9},{11,1... | collective-permute-start | bytes 49160 | tf_op jit(solution)/shard_map/ppermute | solution.py:90
  131.3 3.5 %copy-start.19 = (f32[32,1,128]{2,0,1:T(8,128)}, f32[32,1,128]{2,0,1:T(8,128)S(1)}, u32[]{:S(2)}) copy-start(f32[32,1,128]{2,0,1:T(8,128)S(1)} %collective-permute-done.18) | copy-start | bytes 49156
  134.7 9.5 %copy-start.2 = (f32[32,32,128]{2,0,1:T(8,128)}, f32[32,32,128]{2,0,1:T(8,128)S(1)}, u32[]{:S(2)}) copy-start(f32[32,32,128]{2,0,1:T(8,128)S(1)} %get-tuple-element.106) | copy-start | bytes 1572868
  134.8 13.4 %collective-permute-start.23 = (f32[1,32,128]{2,0,1:T(1,128)S(1)}, f32[1,32,128]{2,0,1:T(1,128)S(1)}, u32[]{:S(2)}, u32[]{:S(2)}) collective-permute-start(f32[1,32,128]{2,0,1:T(1,128)S(1)} %get-tuple-element.115), channel_id=1, source_target_pairs={{0,16},{16,32},{32,48},{48,64},{64,80},{80,96},{96,112},{112,128},... | collective-permute-start | bytes 49160 | tf_op jit(solution)/shard_map/ppermute | solution.py:104
  138.2 10.1 %collective-permute-start.22 = (f32[1,32,128]{2,0,1:T(1,128)S(1)}, f32[1,32,128]{2,0,1:T(1,128)S(1)}, u32[]{:S(2)}, u32[]{:S(2)}) collective-permute-start(f32[1,32,128]{2,0,1:T(1,128)S(1)} %get-tuple-element.116), channel_id=1, source_target_pairs={{16,0},{32,16},{48,32},{64,48},{80,64},{96,80},{112,96},{128,112},... | collective-permute-start | bytes 49160 | tf_op jit(solution)/shard_map/ppermute | solution.py:105
  140.1 8.2 %collective-permute-start.20 = (f32[32,1,128]{2,0,1:T(8,128)S(1)}, f32[32,1,128]{2,0,1:T(8,128)S(1)}, u32[]{:S(2)}, u32[]{:S(2)}) collective-permute-start(f32[32,1,128]{2,0,1:T(8,128)S(1)} %get-tuple-element.113), channel_id=1, source_target_pairs={{0,1},{1,2},{2,3},{3,4},{4,5},{5,6},{6,7},{7,8},{8,9},{9,10},{10,1... | collective-permute-start | bytes 49160 | tf_op jit(solution)/shard_map/ppermute | solution.py:106
  142.9 5.3 %collective-permute-start.21 = (f32[32,1,128]{2,0,1:T(8,128)S(1)}, f32[32,1,128]{2,0,1:T(8,128)S(1)}, u32[]{:S(2)}, u32[]{:S(2)}) collective-permute-start(f32[32,1,128]{2,0,1:T(8,128)S(1)} %get-tuple-element.114), channel_id=1, source_target_pairs={{1,0},{2,1},{3,2},{4,3},{5,4},{6,5},{7,6},{8,7},{9,8},{10,9},{11,1... | collective-permute-start | bytes 49160 | tf_op jit(solution)/shard_map/ppermute | solution.py:107
  148.2 1.8 copy-start.3
  153.9 58.0 %copy-start.7 = (bf16[512,512]{1,0:T(8,128)(2,1)S(1)}, bf16[512,512]{1,0:T(8,128)(2,1)}, u32[]{:S(2)}) copy-start(bf16[512,512]{1,0:T(8,128)(2,1)} %copy-done.6) | copy-start | bytes 1572868
  181.6 24.4 %all-to-all-start.3 = ((f32[32,1,118]{2,1,0:T(1,128)}), f32[32,1,118]{2,1,0:T(1,128)S(1)}, u32[]{:S(2)}, u32[]{:S(2)}) async-start(f32[32,1,118]{2,1,0:T(1,128)} %broadcast_in_dim.23), calls=%async_computation.3 | async-start | bytes 32768 | tf_op jit(solution)/shard_map/all_to_all | solution.py:32
  206.5 23.4 %copy-start.5 = (f32[32,34,128]{2,0,1:T(8,128)S(1)}, f32[32,34,128]{2,0,1:T(8,128)}, u32[]{:S(2)}) copy-start(f32[32,34,128]{2,0,1:T(8,128)} %copy-done.4) | copy-start | bytes 1671172
  210.1 2.8 %copy-start.21 = (f32[512]{0:T(512)}, f32[512]{0:T(512)S(1)}, u32[]{:S(2)}) copy-start(f32[512]{0:T(512)S(1)} %get-tuple-element.82) | copy-start | bytes 6148
  230.0 8.4 %copy-start.9 = (f32[32,32,128]{2,0,1:T(8,128)S(1)}, f32[32,32,128]{2,0,1:T(8,128)}, u32[]{:S(2)}) copy-start(f32[32,32,128]{2,0,1:T(8,128)} %copy-done.8) | copy-start | bytes 1572868
  233.7 4.7 %copy-start.13 = (s32[32,32]{0,1:T(8,128)S(1)}, s32[32,32]{0,1:T(8,128)}, u32[]{:S(2)}) copy-start(s32[32,32]{0,1:T(8,128)} %copy-done.12) | copy-start | bytes 12292
  241.7 1.1 copy-start.11
  (4 other events, 3.2 us)

commit v6 on v5

--- a/solution.py
+++ b/solution.py
@@ -1,4 +1,5 @@
 import jax
+import numpy as np
 import jax.numpy as jnp
 from jax import lax
 from jax.sharding import PartitionSpec as P
@@ -94,6 +95,30 @@
     return core
 
 
+def overlap_sum(block, extra):
+    summed = block
+    for axis, dim in (("gx", 0), ("gy", 1)):
+        count = lax.axis_size(axis)
+        up = [(i, i + 1) for i in range(count - 1)]
+        down = [(i + 1, i) for i in range(count - 1)]
+        size = summed.shape[dim]
+        from_low = lax.ppermute(lax.slice_in_dim(summed, size - extra - 1, size, axis=dim), axis, up)
+        from_high = lax.ppermute(lax.slice_in_dim(summed, 0, extra + 1, axis=dim), axis, down)
+        if extra == 0:
+            own = lax.slice_in_dim(summed, 1, size - 1, axis=dim)
+        else:
+            widths = [(0, 0)] * summed.ndim
+            widths[dim] = (extra - 1, extra - 1)
+            own = jnp.pad(summed, widths)
+        rows = own.shape[dim]
+        widths = [(0, 0)] * summed.ndim
+        widths[dim] = (0, rows - extra - 1)
+        low = jnp.pad(from_low, widths)
+        widths[dim] = (rows - extra - 1, 0)
+        summed = own + low + jnp.pad(from_high, widths)
+    return summed
+
+
 def face_halo(cells):
     count_x = lax.axis_size("gx")
     count_y = lax.axis_size("gy")
@@ -120,14 +145,25 @@
     fluid = 1.0 - solid
     residual = fluid * rhs
     masked = residual * fluid
-    both_wide = extend(jnp.concatenate([masked, solid], axis=2))
-    solid_side = both_wide[:, :, depth:]
-    bottom = jnp.ones((rows_x + 2, rows_y + 2, 1), jnp.float32)
-    top = jnp.zeros((rows_x + 2, rows_y + 2, 1), jnp.float32)
-    fluid_wide = 1.0 - jnp.concatenate([bottom, solid_side, top], 2)
-    count = jnp.zeros_like(fluid)
-    for weight in beside_all(fluid_wide):
-        count = count + weight
+    both_wide = with_halo(jnp.concatenate([masked, solid], axis=2), (("gx", 0), ("gy", 1)), 2)
+    solid_two = both_wide[:, :, depth:]
+    masked_wide = both_wide[1:-1, 1:-1, :depth]
+    solid_side = solid_two[1:-1, 1:-1]
+    bottom = jnp.ones((rows_x + 4, rows_y + 4, 1), jnp.float32)
+    top = jnp.zeros((rows_x + 4, rows_y + 4, 1), jnp.float32)
+    fluid_two = 1.0 - jnp.concatenate([bottom, solid_two, top], 2)
+    fluid_wide = fluid_two[1:-1, 1:-1]
+    count_wide = jnp.zeros_like(solid_side)
+    for weight in beside_all(fluid_two):
+        count_wide = count_wide + weight
+    count = count_wide[1:-1, 1:-1]
+    fluid_one = 1.0 - solid_side
+    place_x = lax.axis_index("gx") * rows_x + jnp.arange(rows_x + 4) - 2
+    place_y = lax.axis_index("gy") * rows_y + jnp.arange(rows_y + 4) - 2
+    inside_x = (place_x >= 0) & (place_x < lax.axis_size("gx") * rows_x)
+    inside_y = (place_y >= 0) & (place_y < lax.axis_size("gy") * rows_y)
+    inside_two = (inside_x[:, None] & inside_y[None, :]).astype(jnp.float32)[:, :, None]
+    inside_one = inside_two[1:-1, 1:-1]
     sine_x, value_x = sine_table(rows_x + 2)
     sine_y, value_y = sine_table(rows_y + 2)
     sine_z, value_z = sine_table(depth)
@@ -136,11 +172,9 @@
     count_x = lax.axis_size("gx")
     count_y = lax.axis_size("gy")
 
-    def local_solve(masked, wide=None):
-        if wide is None:
-            wide = extend(masked)
+    def local_solve(wide, extra):
         spectral = modal(wide, sine_x, sine_y, sine_z) * inv_eig
-        return margin_sum(modal(spectral, sine_x, sine_y, sine_z))
+        return overlap_sum(modal(spectral, sine_x, sine_y, sine_z), extra)
 
     permuted = jnp.transpose(jnp.transpose(inverse[index_map])[index_map])
     me = lax.axis_index(("gx", "gy"))
@@ -171,15 +205,30 @@
 
     every = exchange((jnp.sum(masked) / cells).reshape(1), jnp.zeros((0,), jnp.float32))[0]
     vec0, sol0, value0 = coarse(every)
-    local0 = local_solve(masked, both_wide[:, :, :depth])
-    precond = fluid * (local0 + value0)
-    direction = precond
-
-    image = operate(direction)
-    masked_w = image * fluid
-    local_w = local_solve(masked_w)
+    local0_two = local_solve(masked_wide, 2) * inside_two
+    local0 = local0_two[2:-2, 2:-2]
+    near0 = lax.dynamic_slice(
+        jnp.pad(sol0.reshape(count_x, count_y), 1), (lax.axis_index("gx"), lax.axis_index("gy")), (3, 3)
+    )
+    spread0 = jnp.repeat(near0, np.array([2, rows_x, 2]), axis=0, total_repeat_length=rows_x + 4)
+    spread0 = jnp.repeat(spread0, np.array([2, rows_y, 2]), axis=1, total_repeat_length=rows_y + 4)
+    direction_two = (1.0 - solid_two) * (local0_two + spread0[:, :, None])
+    direction = direction_two[2:-2, 2:-2]
+    precond = direction
+
+    padded_two = jnp.pad(direction_two, ((0, 0), (0, 0), (1, 1)))
+    beside = jnp.zeros_like(solid_side)
+    for operate_weight, value in zip(beside_all(fluid_two), beside_all(padded_two)):
+        beside = beside + operate_weight * value
+    centre = direction_two[1:-1, 1:-1]
+    image_wide = fluid_one * (count_wide * centre - beside) + solid_side * centre
+    image = image_wide[1:-1, 1:-1]
+    masked_w_wide = image_wide * fluid_one * inside_one
+    masked_w = masked_w_wide[1:-1, 1:-1]
+    local_w_wide = local_solve(masked_w_wide, 1) * inside_one
+    local_w = local_w_wide[1:-1, 1:-1]
     fluid_local_w = fluid * local_w
-    image_local_w = operate(fluid_local_w)
+    image_local_w = operate(fluid_local_w, fluid_one * local_w_wide)
     every_w, partial = exchange(
         jnp.concatenate([jnp.stack([jnp.sum(masked_w) / cells, jnp.sum(fluid * image_local_w)]), k_row]),
         jnp.stack(

time: 246 us -> 192 us (0.78)
  starting transfers between devices: 107 us -> 65.5 us
  waiting for transfers between devices: 26.4 us -> 14.3 us
  local copies, waits for them, and re-layouts: 33.1 us -> 26 us
  other arithmetic: 31 us -> 36.2 us
    ppermute x16 -> x8, starting transfers between devices: 41.8 us -> 19.8 us  [the longest x4 13 us: overlap_sum(): lax.ppermute(lax.slice_in_dim(summed, size - extra - 1, size, axis=dim),...]
    ppermute x4 -> x2, starting transfers between devices: 17.2 us -> 6.89 us  [with_halo(): lax.ppermute(tail, axis, [(i, (i + 1) % count) for i in range(ends)])]
    ppermute x4 -> x2, waiting for transfers between devices: 10 us -> 0.01 us  [with_halo(): lax.ppermute(head, axis, [((i + 1) % count, i) for i in range(ends)])]
    mul x1 -> x4, other arithmetic: 0.83 us -> 7.8 us  [the longest x2 3.63 us: body(): masked_w_wide = image_wide * fluid_one * inside_one]
    ppermute x16 -> x8, waiting for transfers between devices: 11.4 us -> 5.45 us  [the longest x4 5.44 us: overlap_sum(): lax.ppermute(lax.slice_in_dim(summed, 0, extra + 1, axis=dim), axis, down)]
    all_to_all x3, starting transfers between devices: 41.5 us -> 35.7 us  [exchange(): lax.all_to_all(jnp.broadcast_to(stage[None], (count,) + stage.shape), axi...]
    all_to_all x3, waiting for transfers between devices: 4.92 us -> 8.88 us  [exchange(): lax.all_to_all(jnp.broadcast_to(stage[None], (count,) + stage.shape), axi...]
    ppermute x4 -> x2, starting transfers between devices: 6.43 us -> 3.2 us  [with_halo(): lax.ppermute(head, axis, [((i + 1) % count, i) for i in range(ends)])]
  transfers between devices with their start and end apart: 27 -> 15, of which waited for: 8 -> 4; matrix products, arithmetic and copies ran while one was open for 7% -> 9% of each run, Pallas kernels for 0% -> 0%
where the time goes in v6:
time: 192 us; the launch traced here: 191 us
  starting transfers between devices  65.5 us (34%)
  other arithmetic  36.2 us (19%)
  local copies, waits for them, and re-layouts  26 us (14%)
  blocking collectives  23.4 us (12%)
  waiting for transfers between devices  14.3 us (7%)
  between operations  13.8 us (7%)
  matrix products  11.4 us (6%)
    all_to_all x3, starting transfers between devices, exchange(): lax.all_to_all(jnp.broadcast_to(stage[None], (count,) + stage.shape), axi...  35.7 us
    all_to_all x1, blocking collectives, exchange(): lax.all_to_all(jnp.broadcast_to(stage[None], (count,) + stage.shape), axi...  23.4 us
    ppermute x4, starting transfers between devices, overlap_sum(): lax.ppermute(lax.slice_in_dim(summed, size - extra - 1, size, axis=dim),...  13 us
    all_to_all x3, waiting for transfers between devices, exchange(): lax.all_to_all(jnp.broadcast_to(stage[None], (count,) + stage.shape), axi...  8.88 us
    ppermute x2, starting transfers between devices, with_halo(): lax.ppermute(tail, axis, [(i, (i + 1) % count) for i in range(ends)])  6.89 us
    ppermute x4, starting transfers between devices, overlap_sum(): lax.ppermute(lax.slice_in_dim(summed, 0, extra + 1, axis=dim), axis, down)  6.74 us
    ppermute x4, waiting for transfers between devices, overlap_sum(): lax.ppermute(lax.slice_in_dim(summed, 0, extra + 1, axis=dim), axis, down)  5.44 us
    concatenate x1, local copies, waits for them, and re-layouts, exchange(): stage = jnp.concatenate([gathered, summed])  5.02 us
  transfers between devices with their start and end apart: 15, of which 4 were waited for; matrix products, arithmetic and copies ran while one was open for 9% of the time, Pallas kernels for 0%

profile of v6, /device:TPU:1, one launch (start us, length us, event | category | flops | bytes accessed | tf_op | source)
XLA Modules:
  0.0 190.7 jit_solution(5305697576186416609)
XLA Ops:
  1.5 2.1 %fusion.156 = (f32[]{:T(128)}, f32[32,32,128]{2,0,1:T(8,128)S(1)}, f32[32,32,128]{2,0,1:T(8,128)S(1)}) fusion(f32[32,32,128]{2,1,0:T(8,128)} %param.20, s32[32,32]{0,1:T(8,128)S(1)} %copy.59), kind=kLoop, calls=%fused_computation.258 | loop fusion | flops 786431 | bytes 1576964 | tf_op jit(solution)/shard_map/reduce_sum | solution.py:206
  4.8 15.7 %all-to-all-start = ((f32[16,1,1]{2,1,0:T(1,128)}), f32[16,1,1]{2,1,0:T(1,128)S(1)}, u32[]{:S(2)}, u32[]{:S(2)}) async-start(f32[16,1,1]{2,1,0:T(1,128)} %broadcast_in_dim.41), calls=%async_computation | async-start | bytes 16384 | tf_op jit(solution)/shard_map/all_to_all | solution.py:33
  20.8 4.0 %collective-permute-start = (f32[2,32,256]{2,0,1:T(2,128)S(1)}, f32[2,32,256]{2,0,1:T(2,128)S(1)}, u32[]{:S(2)}, u32[]{:S(2)}) collective-permute-start(f32[2,32,256]{2,0,1:T(2,128)S(1)} %get-tuple-element.129), channel_id=1, source_target_pairs={{0,16},{16,32},{32,48},{48,64},{64,80},{80,96},{96,112},{112,128},... | collective-permute-start | bytes 196616 | tf_op jit(solution)/shard_map/ppermute | solution.py:18
  24.9 1.9 %collective-permute-start.1 = (f32[2,32,256]{2,0,1:T(2,128)S(1)}, f32[2,32,256]{2,0,1:T(2,128)S(1)}, u32[]{:S(2)}, u32[]{:S(2)}) collective-permute-start(f32[2,32,256]{2,0,1:T(2,128)S(1)} %get-tuple-element.130), channel_id=1, source_target_pairs={{16,0},{32,16},{48,32},{64,48},{80,64},{96,80},{112,96},{128,112},... | collective-permute-start | bytes 196616 | tf_op jit(solution)/shard_map/ppermute | solution.py:20
  28.6 3.2 %all-to-all-done = f32[16,1,1]{2,1,0:T(1,128)S(1)} async-done(((f32[16,1,1]{2,1,0:T(1,128)}), f32[16,1,1]{2,1,0:T(1,128)S(1)}, u32[]{:S(2)}, u32[]{:S(2)}) %all-to-all-start) | async-done | bytes 96 | tf_op jit(solution)/shard_map/all_to_all | solution.py:33
  32.6 9.2 %all-to-all-start.1 = ((f32[32,1,16]{2,1,0:T(1,128)}), f32[32,1,16]{2,1,0:T(1,128)S(1)}, u32[]{:S(2)}, u32[]{:S(2)}) async-start(f32[32,1,16]{2,1,0:T(1,128)} %broadcast_in_dim.43), calls=%async_computation.1 | async-start | bytes 32768 | tf_op jit(solution)/shard_map/all_to_all | solution.py:33
  42.5 2.8 %collective-permute-start.2 = (f32[36,2,256]{2,0,1:T(8,128)}, f32[36,2,256]{2,0,1:T(8,128)}, u32[]{:S(2)}, u32[]{:S(2)}) collective-permute-start(f32[36,2,256]{2,0,1:T(8,128)} %get-tuple-element.127), channel_id=1, source_target_pairs={{0,1},{1,2},{2,3},{3,4},{4,5},{5,6},{6,7},{7,8},{8,9},{9,10},{10,1... | collective-permute-start | bytes 221192 | tf_op jit(solution)/shard_map/ppermute | solution.py:18
  45.3 1.3 collective-permute-start.3
  46.7 2.0 %gather_fusion = bf16[512,512]{1,0:T(8,128)(2,1)S(1)} fusion(bf16[512,512]{1,0:T(8,128)(2,1)S(1)} %copy-done, s32[1024]{0:T(1024)S(1)} %pad_clamp_fusion.1), kind=kCustom, calls=%fused_computation | custom fusion | bytes 1050624 | tf_op jit(solution)/shard_map/gather | solution.py:179
  48.9 2.6 %gather_fusion.1 = bf16[512,512]{1,0:T(8,128)(2,1)} fusion(bf16[512,512]{1,0:T(8,128)(2,1)S(1)} %copy.67, s32[1024]{0:T(1024)S(1)} %pad_clamp_fusion.1), kind=kCustom, calls=%fused_computation.1 | custom fusion | bytes 1050624 | tf_op jit(solution)/shard_map/gather | solution.py:179
  53.1 1.3 pad_maximum_fusion
  55.2 0.9 convolution_bitcast_fusion.3
  56.1 1.0 convolution_multiply_fusion.1
  58.0 0.9 convolution_bitcast_fusion.2
  58.9 1.0 fusion.15
  59.9 3.8 %collective-permute-start.4 = (f32[3,34,128]{2,0,1:T(4,128)S(1)}, f32[3,34,128]{2,0,1:T(4,128)S(1)}, u32[]{:S(2)}, u32[]{:S(2)}) collective-permute-start(f32[3,34,128]{2,0,1:T(4,128)S(1)} %get-tuple-element.137), channel_id=1, source_target_pairs={{0,16},{16,32},{32,48},{48,64},{64,80},{80,96},{96,112},{112,128},... | collective-permute-start | bytes 156680 | tf_op jit(solution)/shard_map/ppermute | solution.py:105
  63.8 1.9 %collective-permute-start.5 = (f32[3,34,128]{2,0,1:T(4,128)S(1)}, f32[3,34,128]{2,0,1:T(4,128)S(1)}, u32[]{:S(2)}, u32[]{:S(2)}) collective-permute-start(f32[3,34,128]{2,0,1:T(4,128)S(1)} %get-tuple-element.138), channel_id=1, source_target_pairs={{16,0},{32,16},{48,32},{64,48},{80,64},{96,80},{112,96},{128,112},... | collective-permute-start | bytes 156680 | tf_op jit(solution)/shard_map/ppermute | solution.py:106
  66.1 3.3 %collective-permute-done.5 = f32[3,34,128]{2,0,1:T(4,128)S(1)} collective-permute-done((f32[3,34,128]{2,0,1:T(4,128)S(1)}, f32[3,34,128]{2,0,1:T(4,128)S(1)}, u32[]{:S(2)}, u32[]{:S(2)}) %collective-permute-start.5) | collective-permute-done | bytes 52256 | tf_op jit(solution)/shard_map/ppermute | solution.py:106
  69.5 4.3 %collective-permute-start.6 = (f32[36,3,128]{2,0,1:T(8,128)S(1)}, f32[36,3,128]{2,0,1:T(8,128)S(1)}, u32[]{:S(2)}, u32[]{:S(2)}) collective-permute-start(f32[36,3,128]{2,0,1:T(8,128)S(1)} %get-tuple-element.135), channel_id=1, source_target_pairs={{0,1},{1,2},{2,3},{3,4},{4,5},{5,6},{6,7},{7,8},{8,9},{9,10},{10,1... | collective-permute-start | bytes 165896 | tf_op jit(solution)/shard_map/ppermute | solution.py:105
  73.8 1.5 collective-permute-start.7
  76.6 2.1 %collective-permute-done.7 = f32[36,3,128]{2,0,1:T(8,128)S(1)} collective-permute-done((f32[36,3,128]{2,0,1:T(8,128)S(1)}, f32[36,3,128]{2,0,1:T(8,128)S(1)}, u32[]{:S(2)}, u32[]{:S(2)}) %collective-permute-start.7) | collective-permute-done | bytes 55328 | tf_op jit(solution)/shard_map/ppermute | solution.py:106
  78.7 2.5 %add_multiply_fusion = (f32[36,36,128]{2,0,1:T(8,128)S(1)}, f32[36,36,128]{2,0,1:T(8,128)}, f32[36,36,128]{2,0,1:T(8,128)S(1)}) fusion(f32[36,36]{0,1:T(8,128)S(1)} %bitcast.105, f32[36,36,256]{2,0,1:T(8,128)} %copy-done.3, f32[36,36]{0,1:T(8,128)S(1)} %copy-done.18, f32[36,3,128]{2,0,1:T(8,128)S(1)} %collective-permute-done.7, ...), kind=kLoop, calls=%fused_computation.20 | loop fusion | flops 995328 | bytes 3401856 | tf_op jit(solution)/shard_map/mul | solution.py:215
  81.7 3.6 %multiply_multiply_fusion = (f32[34,34,128]{2,0,1:T(8,128)S(1)}, f32[34,34,128]{2,0,1:T(8,128)}, f32[34,34,128]{2,0,1:T(8,128)S(1)}) fusion(f32[36,36,256]{2,0,1:T(8,128)} %copy-done.3, f32[34,34]{0,1:T(8,128)S(1)} %convert_bitcast_fusion, f32[36,36,130]{2,0,1:T(8,128)S(1)} %maximum_subtract_fusion, f32[36,36,128]{2,0,1:T(8,128)S(1)} %get-tuple-element.118), kind=kLoop, calls=%fused_computation.50 | loop fusion | flops 3551232 | bytes 10784768 | tf_op jit(solution)/shard_map/mul | solution.py:226
  86.8 0.9 convolution_bitcast_fusion.1
  87.7 1.0 convolution_multiply_fusion
  90.4 1.0 fusion.12
  91.5 3.6 %collective-permute-start.8 = (f32[2,34,128]{2,0,1:T(2,128)S(1)}, f32[2,34,128]{2,0,1:T(2,128)S(1)}, u32[]{:S(2)}, u32[]{:S(2)}) collective-permute-start(f32[2,34,128]{2,0,1:T(2,128)S(1)} %get-tuple-element.133), channel_id=1, source_target_pairs={{0,16},{16,32},{32,48},{48,64},{64,80},{80,96},{96,112},{112,128},... | collective-permute-start | bytes 104456 | tf_op jit(solution)/shard_map/ppermute | solution.py:105
  95.1 1.9 %collective-permute-start.9 = (f32[2,34,128]{2,0,1:T(2,128)S(1)}, f32[2,34,128]{2,0,1:T(2,128)S(1)}, u32[]{:S(2)}, u32[]{:S(2)}) collective-permute-start(f32[2,34,128]{2,0,1:T(2,128)S(1)} %get-tuple-element.134), channel_id=1, source_target_pairs={{16,0},{32,16},{48,32},{64,48},{80,64},{96,80},{112,96},{128,112},... | collective-permute-start | bytes 104456 | tf_op jit(solution)/shard_map/ppermute | solution.py:106
  97.0 1.8 fusion.61
  98.8 1.8 fusion.97
  100.6 1.4 collective-permute-start.10
  102.0 1.4 collective-permute-start.11
  103.5 1.4 fusion.94
  108.2 1.7 fusion.22
  110.1 3.1 %multiply_reduce_fusion = (f32[]{:T(128)}, f32[]{:T(128)}, f32[]{:T(128)}, f32[]{:T(128)}, f32[]{:T(128)}, /*index=5*/f32[]{:T(128)}, f32[]{:T(128)}, f32[32,32,128]{2,0,1:T(8,128)}) fusion(f32[34,34,128]{2,0,1:T(8,128)S(1)} %get-tuple-element.114, s32[32,32]{0,1:T(8,128)S(1)} %copy.59, f32[34,34,128]{2,0,1:T(8,128)S(1)} %copy-done.10, ...), kind=kLoop, calls=%fused_computation.104 | loop fusion | flops 4587513 | bytes 9625628 | tf_op jit(solution)/shard_map/reduce_sum | solution.py:241
  113.2 5.0 %concatenate.50 = f32[13]{0:T(128)S(1)} concatenate(f32[1]{0:T(128)} %bitcast.9, f32[1]{0:T(128)} %bitcast.12, f32[1]{0:T(128)} %bitcast.13, f32[1]{0:T(128)} %bitcast.14, f32[1]{0:T(128)} %bitcast.15, f32[1]{0:T(128)} %bitcast.16, f32[1]{0:T(128)} %bitcast.17, f32[1]{0:T(128)} %bitcast.18, f32[1]{0:T(128)} %bitcast.19, f32[1]{0:T(128)} %bitcast.20, f32[1]{0:T(128)} %bitcast.21, ...), dimensions={0} | concatenate | bytes 104 | tf_op jit(solution)/shard_map/concatenate | solution.py:30
  118.2 23.4 %all_to_all.30 = f32[16,1,13]{2,1,0:T(1,128)S(1)} all-to-all(f32[16,1,13]{2,1,0:T(1,128)S(1)} %broadcast_in_dim.46), channel_id=1, replica_groups=mesh['gx'=32,'gy'=16] {'gy'}, dimensions={0} | all-to-all | bytes 1664 | tf_op jit(solution)/shard_map/all_to_all | solution.py:33
  142.5 10.8 %all-to-all-start.3 = ((f32[32,1,118]{2,1,0:T(1,128)}), f32[32,1,118]{2,1,0:T(1,128)S(1)}, u32[]{:S(2)}, u32[]{:S(2)}) async-start(f32[32,1,118]{2,1,0:T(1,128)} %broadcast_in_dim.47), calls=%async_computation.3 | async-start | bytes 32768 | tf_op jit(solution)/shard_map/all_to_all | solution.py:33
  154.6 5.6 %all-to-all-done.3 = f32[32,1,118]{2,1,0:T(1,128)S(1)} async-done(((f32[32,1,118]{2,1,0:T(1,128)}), f32[32,1,118]{2,1,0:T(1,128)S(1)}, u32[]{:S(2)}, u32[]{:S(2)}) %all-to-all-start.3) | async-done | bytes 15136 | tf_op jit(solution)/shard_map/all_to_all | solution.py:33
  164.0 1.3 multiply_reduce_fusion.8
  172.4 1.1 copy.86
  177.0 3.4 %broadcast_multiply_fusion = (f32[32,32,128]{2,0,1:T(8,128)S(1)}, f32[32,32,128]{2,0,1:T(8,128)}) fusion(f32[]{:T(128)} %bitcast.39, s32[32,32]{0,1:T(8,128)S(1)} %copy.59, f32[]{:T(128)S(6)} %div.77, f32[]{:T(128)} %bitcast.34, f32[34,34,128]{2,0,1:T(8,128)} %copy-done.11, f32[]{:T(128)S(6)} %div.78, f32[36,36,128]{2,0,1:T(8,128)S(1)} %get-tuple-element.118, ...), kind=kLoop, calls=%fused_computation.119 | loop fusion | flops 1703936 | bytes 2101268 | tf_op jit(solution)/shard_map/mul | solution.py:286
  180.5 1.3 slice_multiply_fusion.18
  181.8 1.4 slice_multiply_fusion.20
  183.1 1.3 scatter.29
  185.0 3.5 %fusion.48 = f32[32,32,128]{2,0,1:T(8,128)S(1)} fusion(f32[32,32,128]{2,0,1:T(8,128)} %get-tuple-element.112, f32[34,34,128]{2,0,1:T(8,128)S(1)} %scatter.34, f32[32,32,128]{2,1,0:T(8,128)} %param.20, f32[34,34,128]{2,0,1:T(8,128)} %get-tuple-element.116, f32[36,36,130]{2,0,1:T(8,128)S(1)} %maximum_subtract_fusion, f32[34,34,128]{2,0,1:T(8,128)S(1)} %copy-done.7, ...), kind=kLoop, calls=%fused_computation.81 | loop fusion | flops 3801088 | bytes 8577040 | tf_op jit(solution)/shard_map/sub | solution.py:291
  188.5 1.1 copy.77
  189.6 1.1 copy.76
  (157 shorter events, 22.8 us)
Async XLA Ops:
  0.6 46.1 %copy-start = (bf16[512,512]{1,0:T(8,128)(2,1)S(1)}, bf16[512,512]{1,0:T(8,128)(2,1)}, u32[]{:S(2)}) copy-start(bf16[512,512]{1,0:T(8,128)(2,1)} %param.23) | copy-start | bytes 1572868
  1.5 26.3 %copy-start.25 = (s32[512]{0:T(512)S(1)}, s32[512]{0:T(512)}, u32[]{:S(2)}) copy-start(s32[512]{0:T(512)} %param.22) | copy-start | bytes 6148
  1.5 26.3 %copy-start.26 = (s32[36]{0:T(128)S(1)}, s32[36]{0:T(128)}, u32[]{:S(2)}) copy-start(s32[36]{0:T(128)} %constant.394) | copy-start | bytes 436
  3.5 48.0 %copy-start.13 = (f32[32,32,128]{2,0,1:T(8,128)}, f32[32,32,128]{2,0,1:T(8,128)S(1)}, u32[]{:S(2)}) copy-start(f32[32,32,128]{2,0,1:T(8,128)S(1)} %get-tuple-element.148) | copy-start | bytes 1572868
  3.5 49.5 %copy-start.1 = (f32[32,32,128]{2,0,1:T(8,128)}, f32[32,32,128]{2,0,1:T(8,128)S(1)}, u32[]{:S(2)}) copy-start(f32[32,32,128]{2,0,1:T(8,128)S(1)} %get-tuple-element.121) | copy-start | bytes 1572868
  4.8 27.0 %all-to-all-start = ((f32[16,1,1]{2,1,0:T(1,128)}), f32[16,1,1]{2,1,0:T(1,128)S(1)}, u32[]{:S(2)}, u32[]{:S(2)}) async-start(f32[16,1,1]{2,1,0:T(1,128)} %broadcast_in_dim.41), calls=%async_computation | async-start | bytes 16384 | tf_op jit(solution)/shard_map/all_to_all | solution.py:33
  20.8 28.0 %copy-start.4 = (f32[32,32,128]{2,0,1:T(8,128)}, f32[32,32,128]{2,0,1:T(8,128)S(1)}, u32[]{:S(2)}) copy-start(f32[32,32,128]{2,0,1:T(8,128)S(1)} %fusion.60) | copy-start | bytes 1572868
  20.8 21.0 %collective-permute-start = (f32[2,32,256]{2,0,1:T(2,128)S(1)}, f32[2,32,256]{2,0,1:T(2,128)S(1)}, u32[]{:S(2)}, u32[]{:S(2)}) collective-permute-start(f32[2,32,256]{2,0,1:T(2,128)S(1)} %get-tuple-element.129), channel_id=1, source_target_pairs={{0,16},{16,32},{32,48},{48,64},{64,80},{80,96},{96,112},{112,128},... | collective-permute-start | bytes 196616 | tf_op jit(solution)/shard_map/ppermute | solution.py:18
  24.9 16.9 %collective-permute-start.1 = (f32[2,32,256]{2,0,1:T(2,128)S(1)}, f32[2,32,256]{2,0,1:T(2,128)S(1)}, u32[]{:S(2)}, u32[]{:S(2)}) collective-permute-start(f32[2,32,256]{2,0,1:T(2,128)S(1)} %get-tuple-element.130), channel_id=1, source_target_pairs={{16,0},{32,16},{48,32},{64,48},{80,64},{96,80},{112,96},{128,112},... | collective-permute-start | bytes 196616 | tf_op jit(solution)/shard_map/ppermute | solution.py:20
  26.9 29.2 %copy-start.27 = (f32[128]{0:T(128)}, f32[128]{0:T(128)S(1)}, u32[]{:S(2)}) copy-start(f32[128]{0:T(128)S(1)} %get-tuple-element.161) | copy-start | bytes 1540
  32.6 19.0 %all-to-all-start.1 = ((f32[32,1,16]{2,1,0:T(1,128)}), f32[32,1,16]{2,1,0:T(1,128)S(1)}, u32[]{:S(2)}, u32[]{:S(2)}) async-start(f32[32,1,16]{2,1,0:T(1,128)} %broadcast_in_dim.43), calls=%async_computation.1 | async-start | bytes 32768 | tf_op jit(solution)/shard_map/all_to_all | solution.py:33
  42.5 10.6 %collective-permute-start.2 = (f32[36,2,256]{2,0,1:T(8,128)}, f32[36,2,256]{2,0,1:T(8,128)}, u32[]{:S(2)}, u32[]{:S(2)}) collective-permute-start(f32[36,2,256]{2,0,1:T(8,128)} %get-tuple-element.127), channel_id=1, source_target_pairs={{0,1},{1,2},{2,3},{3,4},{4,5},{5,6},{6,7},{7,8},{8,9},{9,10},{10,1... | collective-permute-start | bytes 221192 | tf_op jit(solution)/shard_map/ppermute | solution.py:18
  45.3 7.7 %collective-permute-start.3 = (f32[36,2,256]{2,0,1:T(8,128)}, f32[36,2,256]{2,0,1:T(8,128)}, u32[]{:S(2)}, u32[]{:S(2)}) collective-permute-start(f32[36,2,256]{2,0,1:T(8,128)} %get-tuple-element.128), channel_id=1, source_target_pairs={{1,0},{2,1},{3,2},{4,3},{5,4},{6,5},{7,6},{8,7},{9,8},{10,9},{11,1... | collective-permute-start | bytes 221192 | tf_op jit(solution)/shard_map/ppermute | solution.py:20
  46.6 12.2 %copy-start.23 = (f32[128]{0:T(128)}, f32[128]{0:T(128)S(1)}, u32[]{:S(2)}) copy-start(f32[128]{0:T(128)S(1)} %broadcast_multiply_fusion.1) | copy-start | bytes 1540
  51.6 3.6 %copy-start.16 = (f32[32,1,16]{2,1,0:T(1,128)}, f32[32,1,16]{2,1,0:T(1,128)S(1)}, u32[]{:S(2)}) copy-start(f32[32,1,16]{2,1,0:T(1,128)S(1)} %all-to-all-done.1) | copy-start | bytes 6148
  54.4 2.8 %copy-start.3 = (f32[36,36,256]{2,0,1:T(8,128)}, f32[36,36,256]{2,0,1:T(8,128)S(1)}, u32[]{:S(2)}) copy-start(f32[36,36,256]{2,0,1:T(8,128)S(1)} %pad_maximum_fusion) | copy-start | bytes 3981316
  54.4 1.7 copy-start.20
  58.0 7.7 %copy-start.8 = (bf16[512,512]{1,0:T(8,128)(2,1)S(1)}, bf16[512,512]{1,0:T(8,128)(2,1)}, u32[]{:S(2)}) copy-start(bf16[512,512]{1,0:T(8,128)(2,1)} %gather_fusion.1) | copy-start | bytes 1572868
  59.9 18.9 %copy-start.18 = (f32[36,36]{0,1:T(8,128)S(1)}, f32[36,36]{0,1:T(8,128)}, u32[]{:S(2)}) copy-start(f32[36,36]{0,1:T(8,128)} %and_convert_fusion) | copy-start | bytes 15556
  59.9 6.2 %collective-permute-start.4 = (f32[3,34,128]{2,0,1:T(4,128)S(1)}, f32[3,34,128]{2,0,1:T(4,128)S(1)}, u32[]{:S(2)}, u32[]{:S(2)}) collective-permute-start(f32[3,34,128]{2,0,1:T(4,128)S(1)} %get-tuple-element.137), channel_id=1, source_target_pairs={{0,16},{16,32},{32,48},{48,64},{64,80},{80,96},{96,112},{112,128},... | collective-permute-start | bytes 156680 | tf_op jit(solution)/shard_map/ppermute | solution.py:105
  63.8 5.6 %collective-permute-start.5 = (f32[3,34,128]{2,0,1:T(4,128)S(1)}, f32[3,34,128]{2,0,1:T(4,128)S(1)}, u32[]{:S(2)}, u32[]{:S(2)}) collective-permute-start(f32[3,34,128]{2,0,1:T(4,128)S(1)} %get-tuple-element.138), channel_id=1, source_target_pairs={{16,0},{32,16},{48,32},{64,48},{80,64},{96,80},{112,96},{128,112},... | collective-permute-start | bytes 156680 | tf_op jit(solution)/shard_map/ppermute | solution.py:106
  66.0 9.2 %copy-start.21 = (f32[1,512]{1,0:T(1,128)}, f32[1,512]{1,0:T(1,128)S(1)}, u32[]{:S(2)}) copy-start(f32[1,512]{1,0:T(1,128)S(1)} %fusion.58) | copy-start | bytes 6148
  69.5 7.1 %collective-permute-start.6 = (f32[36,3,128]{2,0,1:T(8,128)S(1)}, f32[36,3,128]{2,0,1:T(8,128)S(1)}, u32[]{:S(2)}, u32[]{:S(2)}) collective-permute-start(f32[36,3,128]{2,0,1:T(8,128)S(1)} %get-tuple-element.135), channel_id=1, source_target_pairs={{0,1},{1,2},{2,3},{3,4},{4,5},{5,6},{6,7},{7,8},{8,9},{9,10},{10,1... | collective-permute-start | bytes 165896 | tf_op jit(solution)/shard_map/ppermute | solution.py:105
  73.8 5.0 %collective-permute-start.7 = (f32[36,3,128]{2,0,1:T(8,128)S(1)}, f32[36,3,128]{2,0,1:T(8,128)S(1)}, u32[]{:S(2)}, u32[]{:S(2)}) collective-permute-start(f32[36,3,128]{2,0,1:T(8,128)S(1)} %get-tuple-element.136), channel_id=1, source_target_pairs={{1,0},{2,1},{3,2},{4,3},{5,4},{6,5},{7,6},{8,7},{9,8},{10,9},{11,1... | collective-permute-start | bytes 165896 | tf_op jit(solution)/shard_map/ppermute | solution.py:106
  85.2 11.8 %copy-start.5 = (f32[34,34,128]{2,0,1:T(8,128)}, f32[34,34,128]{2,0,1:T(8,128)S(1)}, u32[]{:S(2)}) copy-start(f32[34,34,128]{2,0,1:T(8,128)S(1)} %get-tuple-element.117) | copy-start | bytes 1775620
  86.0 1.7 copy-start.24
  86.0 1.7 copy-start.28
  91.5 9.1 %collective-permute-start.8 = (f32[2,34,128]{2,0,1:T(2,128)S(1)}, f32[2,34,128]{2,0,1:T(2,128)S(1)}, u32[]{:S(2)}, u32[]{:S(2)}) collective-permute-start(f32[2,34,128]{2,0,1:T(2,128)S(1)} %get-tuple-element.133), channel_id=1, source_target_pairs={{0,16},{16,32},{32,48},{48,64},{64,80},{80,96},{96,112},{112,128},... | collective-permute-start | bytes 104456 | tf_op jit(solution)/shard_map/ppermute | solution.py:105
  95.1 5.5 %collective-permute-start.9 = (f32[2,34,128]{2,0,1:T(2,128)S(1)}, f32[2,34,128]{2,0,1:T(2,128)S(1)}, u32[]{:S(2)}, u32[]{:S(2)}) collective-permute-start(f32[2,34,128]{2,0,1:T(2,128)S(1)} %get-tuple-element.134), channel_id=1, source_target_pairs={{16,0},{32,16},{48,32},{64,48},{80,64},{96,80},{112,96},{128,112},... | collective-permute-start | bytes 104456 | tf_op jit(solution)/shard_map/ppermute | solution.py:106
  100.6 1.4 copy-start.12
  100.6 7.5 %collective-permute-start.10 = (f32[34,2,128]{2,0,1:T(8,128)S(1)}, f32[34,2,128]{2,0,1:T(8,128)S(1)}, u32[]{:S(2)}, u32[]{:S(2)}) collective-permute-start(f32[34,2,128]{2,0,1:T(8,128)S(1)} %get-tuple-element.131), channel_id=1, source_target_pairs={{0,1},{1,2},{2,3},{3,4},{4,5},{5,6},{6,7},{7,8},{8,9},{9,10},{10,1... | collective-permute-start | bytes 104456 | tf_op jit(solution)/shard_map/ppermute | solution.py:105
  102.0 7.9 %copy-start.2 = (f32[32,32,128]{2,0,1:T(8,128)S(1)}, f32[32,32,128]{2,0,1:T(8,128)}, u32[]{:S(2)}) copy-start(f32[32,32,128]{2,0,1:T(8,128)} %copy-done.1) | copy-start | bytes 1572868
  102.0 6.1 %collective-permute-start.11 = (f32[34,2,128]{2,0,1:T(8,128)S(1)}, f32[34,2,128]{2,0,1:T(8,128)S(1)}, u32[]{:S(2)}, u32[]{:S(2)}) collective-permute-start(f32[34,2,128]{2,0,1:T(8,128)S(1)} %get-tuple-element.132), channel_id=1, source_target_pairs={{1,0},{2,1},{3,2},{4,3},{5,4},{6,5},{7,6},{8,7},{9,8},{10,9},{11,1... | collective-permute-start | bytes 104456 | tf_op jit(solution)/shard_map/ppermute | solution.py:106
  108.1 1.8 copy-start.6
  108.1 1.8 copy-start.10
  108.1 1.9 %copy-start.14 = (f32[36,36,128]{2,0,1:T(8,128)S(1)}, f32[36,36,128]{2,0,1:T(8,128)}, u32[]{:S(2)}) copy-start(f32[36,36,128]{2,0,1:T(8,128)} %get-tuple-element.119) | copy-start | bytes 1990660
  109.9 3.3 %copy-start.11 = (f32[34,34,128]{2,0,1:T(8,128)}, f32[34,34,128]{2,0,1:T(8,128)S(1)}, u32[]{:S(2)}) copy-start(f32[34,34,128]{2,0,1:T(8,128)S(1)} %get-tuple-element.114) | copy-start | bytes 1775620
  110.1 43.9 %copy-start.17 = (f32[32,1,16]{2,1,0:T(1,128)S(1)}, f32[32,1,16]{2,1,0:T(1,128)}, u32[]{:S(2)}) copy-start(f32[32,1,16]{2,1,0:T(1,128)} %copy-done.16) | copy-start | bytes 6148
  113.2 49.0 %copy-start.9 = (bf16[512,512]{1,0:T(8,128)(2,1)S(1)}, bf16[512,512]{1,0:T(8,128)(2,1)}, u32[]{:S(2)}) copy-start(bf16[512,512]{1,0:T(8,128)(2,1)} %gather_fusion.1) | copy-start | bytes 1572868
  142.5 17.7 %all-to-all-start.3 = ((f32[32,1,118]{2,1,0:T(1,128)}), f32[32,1,118]{2,1,0:T(1,128)S(1)}, u32[]{:S(2)}, u32[]{:S(2)}) async-start(f32[32,1,118]{2,1,0:T(1,128)} %broadcast_in_dim.47), calls=%async_computation.3 | async-start | bytes 32768 | tf_op jit(solution)/shard_map/all_to_all | solution.py:33
  161.0 1.7 copy-start.19
  161.0 3.0 %copy-start.22 = (f32[1,512]{1,0:T(1,128)S(1)}, f32[1,512]{1,0:T(1,128)}, u32[]{:S(2)}) copy-start(f32[1,512]{1,0:T(1,128)} %copy-done.21) | copy-start | bytes 6148
  177.0 8.0 %copy-start.7 = (f32[34,34,128]{2,0,1:T(8,128)S(1)}, f32[34,34,128]{2,0,1:T(8,128)}, u32[]{:S(2)}) copy-start(f32[34,34,128]{2,0,1:T(8,128)} %copy-done.5) | copy-start | bytes 1775620
  185.0 4.6 %copy-start.15 = (f32[32,32,128]{2,0,1:T(8,128)S(1)}, f32[32,32,128]{2,0,1:T(8,128)}, u32[]{:S(2)}) copy-start(f32[32,32,128]{2,0,1:T(8,128)} %get-tuple-element.145) | copy-start | bytes 1572868

commit v7 on v6

--- a/solution.py
+++ b/solution.py
@@ -193,9 +193,16 @@
         return fluid * (count * direction - beside) + solid * direction
 
     inner = fluid_wide[:, :, 1:-1]
+    basis = [
+        operate(fluid, jnp.pad(fluid, ((1, 1), (1, 1), (0, 0)))),
+        jnp.pad(-(fluid[:1] * inner[:1, 1:-1]), ((0, rows_x - 1), (0, 0), (0, 0))),
+        jnp.pad(-(fluid[-1:] * inner[-1:, 1:-1]), ((rows_x - 1, 0), (0, 0), (0, 0))),
+        jnp.pad(-(fluid[:, :1] * inner[1:-1, :1]), ((0, 0), (0, rows_y - 1), (0, 0))),
+        jnp.pad(-(fluid[:, -1:] * inner[1:-1, -1:]), ((0, 0), (rows_y - 1, 0), (0, 0))),
+    ]
     k_row = jnp.stack(
         [
-            jnp.sum(fluid * operate(fluid, jnp.pad(fluid, ((1, 1), (1, 1), (0, 0))))),
+            jnp.sum(fluid * basis[0]),
             -jnp.sum(fluid[0] * inner[0, 1:-1]),
             -jnp.sum(fluid[-1] * inner[-1, 1:-1]),
             -jnp.sum(fluid[:, 0] * inner[1:-1, 0]),
@@ -249,15 +256,11 @@
     vec_w, sol_w, value_w = coarse(every_w[:, 0])
     delta_now = partial[0]
     step_size = energy_now / delta_now
-    solution = step_size * direction
-    residual = residual - step_size * image
     cross_r = partial[1] + cells * jnp.sum(vec0 * sol_w)
     cross_w = partial[2] + cells * jnp.sum(vec_w * sol0)
     square_w = partial[3] + cells * jnp.sum(vec_w * sol_w)
     energy_next = energy_now - step_size * (cross_r + cross_w) + step_size * step_size * square_w
     ratio = energy_next / energy_now
-    precond = precond - step_size * (fluid * (local_w + value_w))
-    direction = precond + ratio * direction
 
     coarse_w = sol_w
     grid_w = coarse_w.reshape(count_x, count_y)
@@ -275,20 +278,16 @@
     square_m = partial[4] + 2.0 * jnp.sum(coarse_w * every_w[:, 1]) + coarse_energy
     grow = 1.0 + ratio
     delta_next = grow * grow * delta_now - 2.0 * step_size * grow * square_w + step_size * step_size * square_m
+    last_step = energy_next / delta_next
 
     mine = near_w[lax.axis_index("gx"), lax.axis_index("gy")]
-    coarse_wide = jnp.zeros((rows_x + 2, rows_y + 2, depth), jnp.float32)
-    coarse_wide = coarse_wide.at[1:-1, 1:-1].set(fluid * mine[0])
-    coarse_wide = coarse_wide.at[0, 1:-1].set(inner[0, 1:-1] * mine[1])
-    coarse_wide = coarse_wide.at[-1, 1:-1].set(inner[-1, 1:-1] * mine[2])
-    coarse_wide = coarse_wide.at[1:-1, 0].set(inner[1:-1, 0] * mine[3])
-    coarse_wide = coarse_wide.at[1:-1, -1].set(inner[1:-1, -1] * mine[4])
-    image_m = image_local_w + operate(fluid * mine[0], coarse_wide)
-    image = grow * image - step_size * image_m
-
-    step_size = energy_next / delta_next
-    solution = solution + step_size * direction
-    residual = residual - step_size * image
+    lead = step_size + last_step * grow
+    both = last_step * step_size
+    coarse_image = (
+        mine[0] * basis[0] + mine[1] * basis[1] + mine[2] * basis[2] + mine[3] * basis[3] + mine[4] * basis[4]
+    )
+    solution = lead * direction - both * (fluid_local_w + fluid * value_w)
+    residual = residual - lead * image + both * (image_local_w + coarse_image)
     return (solution, residual)
 
 

time: 192 us -> 191 us (level)
  waiting for transfers between devices: 14.3 us -> 18.7 us
  other arithmetic: 36.2 us -> 33.6 us
    mul x3 -> x0, other arithmetic: 6.1 us -> none  [the longest x1 3.42 us: body(): image_m = image_local_w + operate(fluid * mine[0], coarse_wide)]
    add x0 -> x1, other arithmetic: none -> 5.88 us  [body(): residual = residual - lead * image + both * (image_local_w + coarse_image)]
    sub x1 -> x0, other arithmetic: 3.5 us -> none  [body(): residual = residual - step_size * image]
    ppermute x4, waiting for transfers between devices: 5.44 us -> 7.96 us  [overlap_sum(): lax.ppermute(lax.slice_in_dim(summed, 0, extra + 1, axis=dim), axis, down)]
    slice x4, local copies, waits for them, and re-layouts: 0.07 us -> 2.14 us  [overlap_sum(): lax.slice_in_dim(summed, size - extra - 1, size, axis=dim)]
    unnamed x66 -> x62, local copies, waits for them, and re-layouts: 4.48 us -> 4.63 us
  transfers between devices with their start and end apart: 15 -> 15, of which waited for: 4 -> 5; matrix products, arithmetic and copies ran while one was open for 9% -> 8% of each run, Pallas kernels for 0% -> 0%
where the time goes in v7:
time: 191 us; the launch traced here: 190 us
  starting transfers between devices  65.7 us (34%)
  other arithmetic  33.6 us (18%)
  local copies, waits for them, and re-layouts  25.3 us (13%)
  blocking collectives  22 us (12%)
  waiting for transfers between devices  18.7 us (10%)
  between operations  13.2 us (7%)
  matrix products  11.4 us (6%)
    all_to_all x3, starting transfers between devices, exchange(): lax.all_to_all(jnp.broadcast_to(stage[None], (count,) + stage.shape), axi...  35.2 us
    all_to_all x1, blocking collectives, exchange(): lax.all_to_all(jnp.broadcast_to(stage[None], (count,) + stage.shape), axi...  22 us
    ppermute x4, starting transfers between devices, overlap_sum(): lax.ppermute(lax.slice_in_dim(summed, size - extra - 1, size, axis=dim),...  14.4 us
    all_to_all x3, waiting for transfers between devices, exchange(): lax.all_to_all(jnp.broadcast_to(stage[None], (count,) + stage.shape), axi...  10.8 us
    ppermute x4, waiting for transfers between devices, overlap_sum(): lax.ppermute(lax.slice_in_dim(summed, 0, extra + 1, axis=dim), axis, down)  7.96 us
    ppermute x4, starting transfers between devices, overlap_sum(): lax.ppermute(lax.slice_in_dim(summed, 0, extra + 1, axis=dim), axis, down)  6.58 us
    ppermute x2, starting transfers between devices, with_halo(): lax.ppermute(tail, axis, [(i, (i + 1) % count) for i in range(ends)])  6.28 us
    add x1, other arithmetic, body(): residual = residual - lead * image + both * (image_local_w + coarse_image)  5.88 us
  transfers between devices with their start and end apart: 15, of which 5 were waited for; matrix products, arithmetic and copies ran while one was open for 8% of the time, Pallas kernels for 0%

profile of v7, /device:TPU:1, one launch (start us, length us, event | category | flops | bytes accessed | tf_op | source)
XLA Modules:
  0.0 190.0 jit_solution(2118859138461584656)
XLA Ops:
  1.5 2.0 %fusion.142 = (f32[]{:T(128)}, f32[32,32,128]{2,0,1:T(8,128)S(1)}, f32[32,32,128]{2,0,1:T(8,128)S(1)}) fusion(f32[32,32,128]{2,1,0:T(8,128)} %param.10, s32[32,32]{0,1:T(8,128)S(1)} %copy.59), kind=kLoop, calls=%fused_computation.234 | loop fusion | flops 786431 | bytes 1576964 | tf_op jit(solution)/shard_map/reduce_sum | solution.py:213
  4.8 15.7 %all-to-all-start = ((f32[16,1,1]{2,1,0:T(1,128)}), f32[16,1,1]{2,1,0:T(1,128)S(1)}, u32[]{:S(2)}, u32[]{:S(2)}) async-start(f32[16,1,1]{2,1,0:T(1,128)} %broadcast_in_dim.41), calls=%async_computation | async-start | bytes 16384 | tf_op jit(solution)/shard_map/all_to_all | solution.py:33
  20.8 4.0 %collective-permute-start = (f32[2,32,256]{2,0,1:T(2,128)S(1)}, f32[2,32,256]{2,0,1:T(2,128)S(1)}, u32[]{:S(2)}, u32[]{:S(2)}) collective-permute-start(f32[2,32,256]{2,0,1:T(2,128)S(1)} %get-tuple-element.73), channel_id=1, source_target_pairs={{0,16},{16,32},{32,48},{48,64},{64,80},{80,96},{96,112},{112,128},... | collective-permute-start | bytes 196616 | tf_op jit(solution)/shard_map/ppermute | solution.py:18
  24.9 1.9 %collective-permute-start.1 = (f32[2,32,256]{2,0,1:T(2,128)S(1)}, f32[2,32,256]{2,0,1:T(2,128)S(1)}, u32[]{:S(2)}, u32[]{:S(2)}) collective-permute-start(f32[2,32,256]{2,0,1:T(2,128)S(1)} %get-tuple-element.74), channel_id=1, source_target_pairs={{16,0},{32,16},{48,32},{64,48},{80,64},{96,80},{112,96},{128,112},... | collective-permute-start | bytes 196616 | tf_op jit(solution)/shard_map/ppermute | solution.py:20
  27.9 3.9 %all-to-all-done = f32[16,1,1]{2,1,0:T(1,128)S(1)} async-done(((f32[16,1,1]{2,1,0:T(1,128)}), f32[16,1,1]{2,1,0:T(1,128)S(1)}, u32[]{:S(2)}, u32[]{:S(2)}) %all-to-all-start) | async-done | bytes 96 | tf_op jit(solution)/shard_map/all_to_all | solution.py:33
  32.6 9.2 %all-to-all-start.1 = ((f32[32,1,16]{2,1,0:T(1,128)}), f32[32,1,16]{2,1,0:T(1,128)S(1)}, u32[]{:S(2)}, u32[]{:S(2)}) async-start(f32[32,1,16]{2,1,0:T(1,128)} %broadcast_in_dim.43), calls=%async_computation.1 | async-start | bytes 32768 | tf_op jit(solution)/shard_map/all_to_all | solution.py:33
  41.9 2.2 %collective-permute-start.2 = (f32[36,2,256]{2,0,1:T(8,128)S(1)}, f32[36,2,256]{2,0,1:T(8,128)S(1)}, u32[]{:S(2)}, u32[]{:S(2)}) collective-permute-start(f32[36,2,256]{2,0,1:T(8,128)S(1)} %get-tuple-element.71), channel_id=1, source_target_pairs={{0,1},{1,2},{2,3},{3,4},{4,5},{5,6},{6,7},{7,8},{8,9},{9,10},{10,1... | collective-permute-start | bytes 221192 | tf_op jit(solution)/shard_map/ppermute | solution.py:18
  44.1 1.3 collective-permute-start.3
  46.1 2.0 %gather_fusion = bf16[512,512]{1,0:T(8,128)(2,1)S(1)} fusion(bf16[512,512]{1,0:T(8,128)(2,1)S(1)} %copy-done, s32[1024]{0:T(1024)S(1)} %pad_clamp_fusion.1), kind=kCustom, calls=%fused_computation | custom fusion | bytes 1050624 | tf_op jit(solution)/shard_map/gather | solution.py:179
  48.3 2.6 %gather_fusion.1 = bf16[512,512]{1,0:T(8,128)(2,1)} fusion(bf16[512,512]{1,0:T(8,128)(2,1)S(1)} %copy.67, s32[1024]{0:T(1024)S(1)} %pad_clamp_fusion.1), kind=kCustom, calls=%fused_computation.1 | custom fusion | bytes 1050624 | tf_op jit(solution)/shard_map/gather | solution.py:179
  52.4 1.3 pad_maximum_fusion
  54.5 0.9 convolution_bitcast_fusion.3
  55.4 1.0 convolution_multiply_fusion.1
  57.3 0.9 convolution_bitcast_fusion.2
  58.2 1.0 fusion.15
  59.9 3.8 %collective-permute-start.4 = (f32[3,34,128]{2,0,1:T(4,128)}, f32[3,34,128]{2,0,1:T(4,128)}, u32[]{:S(2)}, u32[]{:S(2)}) collective-permute-start(f32[3,34,128]{2,0,1:T(4,128)} %get-tuple-element.81), channel_id=1, source_target_pairs={{0,16},{16,32},{32,48},{48,64},{64,80},{80,96},{96,112},{112,128},... | collective-permute-start | bytes 156680 | tf_op jit(solution)/shard_map/ppermute | solution.py:105
  63.8 1.9 %collective-permute-start.5 = (f32[3,34,128]{2,0,1:T(4,128)}, f32[3,34,128]{2,0,1:T(4,128)}, u32[]{:S(2)}, u32[]{:S(2)}) collective-permute-start(f32[3,34,128]{2,0,1:T(4,128)} %get-tuple-element.82), channel_id=1, source_target_pairs={{16,0},{32,16},{48,32},{64,48},{80,64},{96,80},{112,96},{128,112},... | collective-permute-start | bytes 156680 | tf_op jit(solution)/shard_map/ppermute | solution.py:106
  66.1 3.6 %collective-permute-done.5 = f32[3,34,128]{2,0,1:T(4,128)} collective-permute-done((f32[3,34,128]{2,0,1:T(4,128)}, f32[3,34,128]{2,0,1:T(4,128)}, u32[]{:S(2)}, u32[]{:S(2)}) %collective-permute-start.5) | collective-permute-done | bytes 52256 | tf_op jit(solution)/shard_map/ppermute | solution.py:106
  69.7 1.3 pad_add_fusion.1
  71.7 4.9 %collective-permute-start.6 = (f32[36,3,128]{2,0,1:T(8,128)}, f32[36,3,128]{2,0,1:T(8,128)}, u32[]{:S(2)}, u32[]{:S(2)}) collective-permute-start(f32[36,3,128]{2,0,1:T(8,128)} %get-tuple-element.79), channel_id=1, source_target_pairs={{0,1},{1,2},{2,3},{3,4},{4,5},{5,6},{6,7},{7,8},{8,9},{9,10},{10,1... | collective-permute-start | bytes 165896 | tf_op jit(solution)/shard_map/ppermute | solution.py:105
  76.6 1.5 collective-permute-start.7
  79.4 2.5 %collective-permute-done.7 = f32[36,3,128]{2,0,1:T(8,128)} collective-permute-done((f32[36,3,128]{2,0,1:T(8,128)}, f32[36,3,128]{2,0,1:T(8,128)}, u32[]{:S(2)}, u32[]{:S(2)}) %collective-permute-start.7) | collective-permute-done | bytes 55328 | tf_op jit(solution)/shard_map/ppermute | solution.py:106
  81.9 2.5 %add_multiply_fusion = (f32[36,36,128]{2,0,1:T(8,128)S(1)}, f32[36,36,128]{2,0,1:T(8,128)}, f32[36,36,128]{2,0,1:T(8,128)S(1)}) fusion(f32[36,36]{0,1:T(8,128)S(1)} %bitcast.103, f32[36,36,256]{2,0,1:T(8,128)S(1)} %pad_maximum_fusion, f32[36,36]{0,1:T(8,128)S(1)} %and_convert_fusion, f32[36,3,128]{2,0,1:T(8,128)} %collective-permute-done.7, ...), kind=kLoop, calls=%fused_computation.18 | loop fusion | flops 995328 | bytes 3401856 | tf_op jit(solution)/shard_map/mul | solution.py:222
  84.8 1.7 fusion.138
  86.5 3.8 %multiply_multiply_fusion = (f32[34,34,128]{2,0,1:T(8,128)S(1)}, f32[34,34,128]{2,0,1:T(8,128)}, f32[34,34,128]{2,0,1:T(8,128)}) fusion(f32[36,36,256]{2,0,1:T(8,128)} %copy-done.3, f32[34,34]{0,1:T(8,128)S(1)} %convert_bitcast_fusion, f32[36,36,130]{2,0,1:T(8,128)S(1)} %maximum_subtract_fusion, f32[36,36,128]{2,0,1:T(8,128)S(1)} %get-tuple-element.62), kind=kLoop, calls=%fused_computation.48 | loop fusion | flops 3551232 | bytes 10784768 | tf_op jit(solution)/shard_map/mul | solution.py:233
  91.2 0.9 convolution_bitcast_fusion.1
  92.1 1.0 convolution_multiply_fusion
  94.0 0.9 convolution_bitcast_fusion
  94.8 1.0 fusion.12
  95.9 3.6 %collective-permute-start.8 = (f32[2,34,128]{2,0,1:T(2,128)S(1)}, f32[2,34,128]{2,0,1:T(2,128)S(1)}, u32[]{:S(2)}, u32[]{:S(2)}) collective-permute-start(f32[2,34,128]{2,0,1:T(2,128)S(1)} %get-tuple-element.77), channel_id=1, source_target_pairs={{0,16},{16,32},{32,48},{48,64},{64,80},{80,96},{96,112},{112,128},... | collective-permute-start | bytes 104456 | tf_op jit(solution)/shard_map/ppermute | solution.py:105
  99.4 1.9 %collective-permute-start.9 = (f32[2,34,128]{2,0,1:T(2,128)S(1)}, f32[2,34,128]{2,0,1:T(2,128)S(1)}, u32[]{:S(2)}, u32[]{:S(2)}) collective-permute-start(f32[2,34,128]{2,0,1:T(2,128)S(1)} %get-tuple-element.78), channel_id=1, source_target_pairs={{16,0},{32,16},{48,32},{64,48},{80,64},{96,80},{112,96},{128,112},... | collective-permute-start | bytes 104456 | tf_op jit(solution)/shard_map/ppermute | solution.py:106
  101.4 1.4 fusion.112
  102.8 1.9 collective-permute-done.9
  105.5 2.1 %collective-permute-start.10 = (f32[34,2,128]{2,0,1:T(8,128)}, f32[34,2,128]{2,0,1:T(8,128)}, u32[]{:S(2)}, u32[]{:S(2)}) collective-permute-start(f32[34,2,128]{2,0,1:T(8,128)} %get-tuple-element.75), channel_id=1, source_target_pairs={{0,1},{1,2},{2,3},{3,4},{4,5},{5,6},{6,7},{7,8},{8,9},{9,10},{10,1... | collective-permute-start | bytes 104456 | tf_op jit(solution)/shard_map/ppermute | solution.py:105
  107.6 1.3 collective-permute-start.11
  110.9 1.4 reduce_sum.202
  112.9 1.4 reduce_sum.203
  115.6 1.7 fusion.22
  117.7 3.8 %multiply_reduce_fusion = (f32[]{:T(128)}, f32[]{:T(128)}, f32[]{:T(128)}, f32[]{:T(128)}, f32[]{:T(128)}, /*index=5*/f32[]{:T(128)}, f32[]{:T(128)}, f32[]{:T(128)}, f32[32,32,128]{2,0,1:T(8,128)}, f32[32,32,128]{2,0,1:T(8,128)}) fusion(f32[34,34,128]{2,0,1:T(8,128)S(1)} %get-tuple-element.58, s32[32,32]{0,1:T(8,128)S(1)} %copy.59, ...), kind=kLoop, calls=%fused_computation.83 | loop fusion | flops 6946808 | bytes 12943392 | tf_op jit(solution)/shard_map/reduce_sum | solution.py:248
  121.4 5.0 %concatenate.36 = f32[13]{0:T(128)S(1)} concatenate(f32[1]{0:T(128)} %bitcast.9, f32[1]{0:T(128)} %bitcast.12, f32[1]{0:T(128)} %bitcast.13, f32[1]{0:T(128)} %bitcast.14, f32[1]{0:T(128)} %bitcast.15, f32[1]{0:T(128)} %bitcast.16, f32[1]{0:T(128)} %bitcast.17, f32[1]{0:T(128)} %bitcast.18, f32[1]{0:T(128)} %bitcast.19, f32[1]{0:T(128)} %bitcast.20, f32[1]{0:T(128)} %bitcast.21, ...), dimensions={0} | concatenate | bytes 104 | tf_op jit(solution)/shard_map/concatenate | solution.py:30
  126.5 22.0 %all_to_all.30 = f32[16,1,13]{2,1,0:T(1,128)S(1)} all-to-all(f32[16,1,13]{2,1,0:T(1,128)S(1)} %broadcast_in_dim.46), channel_id=1, replica_groups=mesh['gx'=32,'gy'=16] {'gy'}, dimensions={0} | all-to-all | bytes 1664 | tf_op jit(solution)/shard_map/all_to_all | solution.py:33
  149.4 10.3 %all-to-all-start.3 = ((f32[32,1,118]{2,1,0:T(1,128)}), f32[32,1,118]{2,1,0:T(1,128)S(1)}, u32[]{:S(2)}, u32[]{:S(2)}) async-start(f32[32,1,118]{2,1,0:T(1,128)} %broadcast_in_dim.82), calls=%async_computation.3 | async-start | bytes 32768 | tf_op jit(solution)/shard_map/all_to_all | solution.py:33
  159.8 6.8 %all-to-all-done.3 = f32[32,1,118]{2,1,0:T(1,128)S(1)} async-done(((f32[32,1,118]{2,1,0:T(1,128)}), f32[32,1,118]{2,1,0:T(1,128)S(1)}, u32[]{:S(2)}, u32[]{:S(2)}) %all-to-all-start.3) | async-done | bytes 15136 | tf_op jit(solution)/shard_map/all_to_all | solution.py:33
  167.2 0.8 slice.514
  176.7 1.1 copy.86
  181.9 5.9 %multiply_add_fusion = (f32[32,32,128]{2,0,1:T(8,128)S(1)}, f32[32,32,128]{2,0,1:T(8,128)S(1)}) fusion(f32[32,32,128]{2,0,1:T(8,128)} %get-tuple-element.56, f32[32,1,128]{2,0,1:T(8,128)S(1)} %get-tuple-element.67, f32[32,1,128]{2,0,1:T(8,128)S(1)} %get-tuple-element.66, f32[1,32,128]{2,0,1:T(1,128)S(1)} %get-tuple-element.53, ...), kind=kLoop, calls=%fused_computation.81 | loop fusion | flops 3145728 | bytes 4263968 | tf_op jit(solution)/shard_map/add | solution.py:290
  187.8 1.1 copy.77
  188.9 1.1 copy.76
  (144 shorter events, 21.0 us)
Async XLA Ops:
  0.6 45.4 %copy-start = (bf16[512,512]{1,0:T(8,128)(2,1)S(1)}, bf16[512,512]{1,0:T(8,128)(2,1)}, u32[]{:S(2)}) copy-start(bf16[512,512]{1,0:T(8,128)(2,1)} %param.13) | copy-start | bytes 1572868
  1.5 26.2 %copy-start.23 = (s32[512]{0:T(512)S(1)}, s32[512]{0:T(512)}, u32[]{:S(2)}) copy-start(s32[512]{0:T(512)} %param.12) | copy-start | bytes 6148
  1.5 26.2 %copy-start.24 = (s32[36]{0:T(128)S(1)}, s32[36]{0:T(128)}, u32[]{:S(2)}) copy-start(s32[36]{0:T(128)} %constant.247) | copy-start | bytes 436
  3.5 47.4 %copy-start.14 = (f32[32,32,128]{2,0,1:T(8,128)}, f32[32,32,128]{2,0,1:T(8,128)S(1)}, u32[]{:S(2)}) copy-start(f32[32,32,128]{2,0,1:T(8,128)S(1)} %get-tuple-element.92) | copy-start | bytes 1572868
  3.5 48.8 %copy-start.1 = (f32[32,32,128]{2,0,1:T(8,128)}, f32[32,32,128]{2,0,1:T(8,128)S(1)}, u32[]{:S(2)}) copy-start(f32[32,32,128]{2,0,1:T(8,128)S(1)} %get-tuple-element.65) | copy-start | bytes 1572868
  4.8 27.0 %all-to-all-start = ((f32[16,1,1]{2,1,0:T(1,128)}), f32[16,1,1]{2,1,0:T(1,128)S(1)}, u32[]{:S(2)}, u32[]{:S(2)}) async-start(f32[16,1,1]{2,1,0:T(1,128)} %broadcast_in_dim.41), calls=%async_computation | async-start | bytes 16384 | tf_op jit(solution)/shard_map/all_to_all | solution.py:33
  20.8 27.3 %copy-start.4 = (f32[32,32,128]{2,0,1:T(8,128)}, f32[32,32,128]{2,0,1:T(8,128)S(1)}, u32[]{:S(2)}) copy-start(f32[32,32,128]{2,0,1:T(8,128)S(1)} %fusion.44) | copy-start | bytes 1572868
  20.8 21.0 %collective-permute-start = (f32[2,32,256]{2,0,1:T(2,128)S(1)}, f32[2,32,256]{2,0,1:T(2,128)S(1)}, u32[]{:S(2)}, u32[]{:S(2)}) collective-permute-start(f32[2,32,256]{2,0,1:T(2,128)S(1)} %get-tuple-element.73), channel_id=1, source_target_pairs={{0,16},{16,32},{32,48},{48,64},{64,80},{80,96},{96,112},{112,128},... | collective-permute-start | bytes 196616 | tf_op jit(solution)/shard_map/ppermute | solution.py:18
  24.9 17.0 %collective-permute-start.1 = (f32[2,32,256]{2,0,1:T(2,128)S(1)}, f32[2,32,256]{2,0,1:T(2,128)S(1)}, u32[]{:S(2)}, u32[]{:S(2)}) collective-permute-start(f32[2,32,256]{2,0,1:T(2,128)S(1)} %get-tuple-element.74), channel_id=1, source_target_pairs={{16,0},{32,16},{48,32},{64,48},{80,64},{96,80},{112,96},{128,112},... | collective-permute-start | bytes 196616 | tf_op jit(solution)/shard_map/ppermute | solution.py:20
  27.4 30.8 %copy-start.19 = (f32[128]{0:T(128)}, f32[128]{0:T(128)S(1)}, u32[]{:S(2)}) copy-start(f32[128]{0:T(128)S(1)} %get-tuple-element.104) | copy-start | bytes 1540
  27.8 27.6 %copy-start.17 = (f32[34,34]{0,1:T(8,128)}, f32[34,34]{0,1:T(8,128)S(1)}, u32[]{:S(2)}) copy-start(f32[34,34]{0,1:T(8,128)S(1)} %broadcast_add_fusion) | copy-start | bytes 13876
  32.6 18.3 %all-to-all-start.1 = ((f32[32,1,16]{2,1,0:T(1,128)}), f32[32,1,16]{2,1,0:T(1,128)S(1)}, u32[]{:S(2)}, u32[]{:S(2)}) async-start(f32[32,1,16]{2,1,0:T(1,128)} %broadcast_in_dim.43), calls=%async_computation.1 | async-start | bytes 32768 | tf_op jit(solution)/shard_map/all_to_all | solution.py:33
  41.9 10.5 %collective-permute-start.2 = (f32[36,2,256]{2,0,1:T(8,128)S(1)}, f32[36,2,256]{2,0,1:T(8,128)S(1)}, u32[]{:S(2)}, u32[]{:S(2)}) collective-permute-start(f32[36,2,256]{2,0,1:T(8,128)S(1)} %get-tuple-element.71), channel_id=1, source_target_pairs={{0,1},{1,2},{2,3},{3,4},{4,5},{5,6},{6,7},{7,8},{8,9},{9,10},{10,1... | collective-permute-start | bytes 221192 | tf_op jit(solution)/shard_map/ppermute | solution.py:18
  44.1 8.3 %collective-permute-start.3 = (f32[36,2,256]{2,0,1:T(8,128)S(1)}, f32[36,2,256]{2,0,1:T(8,128)}, u32[]{:S(2)}, u32[]{:S(2)}) collective-permute-start(f32[36,2,256]{2,0,1:T(8,128)S(1)} %get-tuple-element.72), channel_id=1, source_target_pairs={{1,0},{2,1},{3,2},{4,3},{5,4},{6,5},{7,6},{8,7},{9,8},{10,9},{11,1... | collective-permute-start | bytes 221192 | tf_op jit(solution)/shard_map/ppermute | solution.py:20
  53.7 28.2 %copy-start.3 = (f32[36,36,256]{2,0,1:T(8,128)}, f32[36,36,256]{2,0,1:T(8,128)S(1)}, u32[]{:S(2)}) copy-start(f32[36,36,256]{2,0,1:T(8,128)S(1)} %pad_maximum_fusion) | copy-start | bytes 3981316
  53.7 1.7 copy-start.21
  53.7 1.7 copy-start.25
  57.3 8.4 %copy-start.5 = (bf16[512,512]{1,0:T(8,128)(2,1)S(1)}, bf16[512,512]{1,0:T(8,128)(2,1)}, u32[]{:S(2)}) copy-start(bf16[512,512]{1,0:T(8,128)(2,1)} %gather_fusion.1) | copy-start | bytes 1572868
  59.2 6.8 %copy-start.11 = (f32[34,34,128]{2,0,1:T(8,128)}, f32[34,34,128]{2,0,1:T(8,128)S(1)}, u32[]{:S(2)}) copy-start(f32[34,34,128]{2,0,1:T(8,128)S(1)} %fusion.15) | copy-start | bytes 1775620
  59.9 6.2 %collective-permute-start.4 = (f32[3,34,128]{2,0,1:T(4,128)}, f32[3,34,128]{2,0,1:T(4,128)}, u32[]{:S(2)}, u32[]{:S(2)}) collective-permute-start(f32[3,34,128]{2,0,1:T(4,128)} %get-tuple-element.81), channel_id=1, source_target_pairs={{0,16},{16,32},{32,48},{48,64},{64,80},{80,96},{96,112},{112,128},... | collective-permute-start | bytes 156680 | tf_op jit(solution)/shard_map/ppermute | solution.py:105
  63.8 5.9 %collective-permute-start.5 = (f32[3,34,128]{2,0,1:T(4,128)}, f32[3,34,128]{2,0,1:T(4,128)}, u32[]{:S(2)}, u32[]{:S(2)}) collective-permute-start(f32[3,34,128]{2,0,1:T(4,128)} %get-tuple-element.82), channel_id=1, source_target_pairs={{16,0},{32,16},{48,32},{64,48},{80,64},{96,80},{112,96},{128,112},... | collective-permute-start | bytes 156680 | tf_op jit(solution)/shard_map/ppermute | solution.py:106
  71.0 5.6 %copy-start.12 = (f32[36,34,128]{2,0,1:T(8,128)}, f32[36,34,128]{2,0,1:T(8,128)S(1)}, u32[]{:S(2)}) copy-start(f32[36,34,128]{2,0,1:T(8,128)S(1)} %pad_add_fusion.1) | copy-start | bytes 1880068
  71.7 7.7 %collective-permute-start.6 = (f32[36,3,128]{2,0,1:T(8,128)}, f32[36,3,128]{2,0,1:T(8,128)}, u32[]{:S(2)}, u32[]{:S(2)}) collective-permute-start(f32[36,3,128]{2,0,1:T(8,128)} %get-tuple-element.79), channel_id=1, source_target_pairs={{0,1},{1,2},{2,3},{3,4},{4,5},{5,6},{6,7},{7,8},{8,9},{9,10},{10,1... | collective-permute-start | bytes 165896 | tf_op jit(solution)/shard_map/ppermute | solution.py:105
  76.6 5.3 %collective-permute-start.7 = (f32[36,3,128]{2,0,1:T(8,128)}, f32[36,3,128]{2,0,1:T(8,128)}, u32[]{:S(2)}, u32[]{:S(2)}) collective-permute-start(f32[36,3,128]{2,0,1:T(8,128)} %get-tuple-element.80), channel_id=1, source_target_pairs={{1,0},{2,1},{3,2},{4,3},{5,4},{6,5},{7,6},{8,7},{9,8},{10,9},{11,1... | collective-permute-start | bytes 165896 | tf_op jit(solution)/shard_map/ppermute | solution.py:106
  90.3 1.7 copy-start.18
  90.3 1.7 copy-start.20
  90.3 1.8 copy-start.22
  90.3 1.8 copy-start.26
  95.9 6.9 %collective-permute-start.8 = (f32[2,34,128]{2,0,1:T(2,128)S(1)}, f32[2,34,128]{2,0,1:T(2,128)S(1)}, u32[]{:S(2)}, u32[]{:S(2)}) collective-permute-start(f32[2,34,128]{2,0,1:T(2,128)S(1)} %get-tuple-element.77), channel_id=1, source_target_pairs={{0,16},{16,32},{32,48},{48,64},{64,80},{80,96},{96,112},{112,128},... | collective-permute-start | bytes 104456 | tf_op jit(solution)/shard_map/ppermute | solution.py:105
  99.4 5.3 %collective-permute-start.9 = (f32[2,34,128]{2,0,1:T(2,128)S(1)}, f32[2,34,128]{2,0,1:T(2,128)S(1)}, u32[]{:S(2)}, u32[]{:S(2)}) collective-permute-start(f32[2,34,128]{2,0,1:T(2,128)S(1)} %get-tuple-element.78), channel_id=1, source_target_pairs={{16,0},{32,16},{48,32},{64,48},{80,64},{96,80},{112,96},{128,112},... | collective-permute-start | bytes 104456 | tf_op jit(solution)/shard_map/ppermute | solution.py:106
  104.8 4.9 %copy-start.13 = (f32[34,34,128]{2,0,1:T(8,128)}, f32[34,34,128]{2,0,1:T(8,128)S(1)}, u32[]{:S(2)}) copy-start(f32[34,34,128]{2,0,1:T(8,128)S(1)} %pad_add_fusion) | copy-start | bytes 1775620
  105.5 10.1 %collective-permute-start.10 = (f32[34,2,128]{2,0,1:T(8,128)}, f32[34,2,128]{2,0,1:T(8,128)}, u32[]{:S(2)}, u32[]{:S(2)}) collective-permute-start(f32[34,2,128]{2,0,1:T(8,128)} %get-tuple-element.75), channel_id=1, source_target_pairs={{0,1},{1,2},{2,3},{3,4},{4,5},{5,6},{6,7},{7,8},{8,9},{9,10},{10,1... | collective-permute-start | bytes 104456 | tf_op jit(solution)/shard_map/ppermute | solution.py:105
  107.6 8.0 %collective-permute-start.11 = (f32[34,2,128]{2,0,1:T(8,128)}, f32[34,2,128]{2,0,1:T(8,128)}, u32[]{:S(2)}, u32[]{:S(2)}) collective-permute-start(f32[34,2,128]{2,0,1:T(8,128)} %get-tuple-element.76), channel_id=1, source_target_pairs={{1,0},{2,1},{3,2},{4,3},{5,4},{6,5},{7,6},{8,7},{9,8},{10,9},{11,1... | collective-permute-start | bytes 104456 | tf_op jit(solution)/shard_map/ppermute | solution.py:106
  115.5 1.8 copy-start.2
  115.5 1.8 copy-start.9
  115.6 1.9 %copy-start.15 = (f32[36,36,128]{2,0,1:T(8,128)S(1)}, f32[36,36,128]{2,0,1:T(8,128)}, u32[]{:S(2)}) copy-start(f32[36,36,128]{2,0,1:T(8,128)} %get-tuple-element.63) | copy-start | bytes 1990660
  115.6 2.1 %copy-start.16 = (f32[34,34,128]{2,0,1:T(8,128)S(1)}, f32[34,34,128]{2,0,1:T(8,128)}, u32[]{:S(2)}) copy-start(f32[34,34,128]{2,0,1:T(8,128)} %get-tuple-element.61) | copy-start | bytes 1775620
  117.3 4.1 %copy-start.7 = (f32[34,34,128]{2,0,1:T(8,128)}, f32[34,34,128]{2,0,1:T(8,128)S(1)}, u32[]{:S(2)}) copy-start(f32[34,34,128]{2,0,1:T(8,128)S(1)} %get-tuple-element.58) | copy-start | bytes 1775620
  121.4 46.6 %copy-start.6 = (bf16[512,512]{1,0:T(8,128)(2,1)S(1)}, bf16[512,512]{1,0:T(8,128)(2,1)}, u32[]{:S(2)}) copy-start(bf16[512,512]{1,0:T(8,128)(2,1)} %gather_fusion.1) | copy-start | bytes 1572868
  149.4 17.3 %all-to-all-start.3 = ((f32[32,1,118]{2,1,0:T(1,128)}), f32[32,1,118]{2,1,0:T(1,128)S(1)}, u32[]{:S(2)}, u32[]{:S(2)}) async-start(f32[32,1,118]{2,1,0:T(1,128)} %broadcast_in_dim.82), calls=%async_computation.3 | async-start | bytes 32768 | tf_op jit(solution)/shard_map/all_to_all | solution.py:33
  159.7 22.2 %copy-start.8 = (f32[34,34,128]{2,0,1:T(8,128)S(1)}, f32[34,34,128]{2,0,1:T(8,128)}, u32[]{:S(2)}) copy-start(f32[34,34,128]{2,0,1:T(8,128)} %copy-done.7) | copy-start | bytes 1775620
  159.7 22.2 %copy-start.10 = (f32[34,34,128]{2,0,1:T(8,128)S(1)}, f32[34,34,128]{2,0,1:T(8,128)}, u32[]{:S(2)}) copy-start(f32[34,34,128]{2,0,1:T(8,128)} %get-tuple-element.60) | copy-start | bytes 1775620
